TPU v7x, 32 devices: a whole 2x2x4 slice. The times are simulated.
32 devices in a mesh: body: 8 (over z, y), across: 4 (over x, core).
Axes of the slice: x: 2, y: 2, z: 4, core: 2. Of those that a mesh axis runs over, the one named last changes fastest.
Arguments:
- cotangent: float32 [3, 64, 128, 256], P(None, 'body', 'across'), may hold values from -6 to 6
- shear_modulus: float32 [64, 128, 256], P('body', 'across'), may hold values from 0.3 to 3
- lame_first: float32 [64, 128, 256], P('body', 'across'), may hold values from 0.3 to 3
- inertia: float32 [64, 128, 256], P('body', 'across'), may hold values from 0.02 to 0.2
- surface_points: float32 [8, 4, 16, 3, 128], P('body', 'across'), may hold values from -0.3 to 1, as said below
- point_counts: int32 [8, 4, 16], P('body', 'across'), may hold values from 64 to 128, as said below
- surface_maps: int32 [8, 4, 16, 128], P('body', 'across'), may hold values from 0 to 65535, as said below
- contact_pairs: int32 [8, 4, 3, 32], P('body', 'across'), may hold values from 0 to 15, as said below
Outputs:
- displacement: float32 [3, 64, 128, 256], P(None, 'body', 'across')
- residual: float32 [3, 64, 128, 256], P(None, 'body', 'across')
Inputs may be any that keep to these rules, and one draw needn't show every extreme that they name: `surface_points`: coordinates 0 and 1 lie in [0, 1]; coordinate 2 lies in [0.3, 0.6] for even-numbered blocks and in [-0.3, 0] for odd-numbered blocks. `point_counts`: every device has a block with all 128 points active. `surface_maps`: the cells of one device's points are distinct. `contact_pairs`: row 0 holds even block numbers and row 2 odd block numbers below 16; row 1 is a first-split index, and the partner shares the device's second-split index. Every device names every first-split index, its own included, exactly 4 times.
All inputs are finite; a program needn't handle non-finite values.
Results may differ from a plain program's by a relative error of at most 0.0003.
Values sent between devices are 32-bit elements; how exact they have to be, the bound alone decides.
No kernel may reach another device: no remote copies, remote signals or barrier semaphores. Data moves between devices by JAX's collectives and lax.ppermute only.
A program may use at most 192 MiB of HBM per device.

v0:
```python
import jax
import jax.numpy as jnp
from jax import lax
from jax.sharding import PartitionSpec as P

CAP = 4
ITERS = 2


barrier_reach = 1.0
barrier_scale = 0.005


def padded_2(cells, sides, width):
    for axis, dim in sides:
        count = lax.axis_size(axis)
        ends = count - 1
        head = lax.slice_in_dim(cells, 0, width, axis=dim)
        tail = lax.slice_in_dim(cells, cells.shape[dim] - width, cells.shape[dim], axis=dim)
        cells = jnp.concatenate(
            [
                lax.ppermute(tail, axis, [(i, (i + 1) % count) for i in range(ends)]),
                cells,
                lax.ppermute(head, axis, [((i + 1) % count, i) for i in range(ends)]),
            ],
            axis=dim,
        )
    return cells


def shifted(padded, direction, offset):
    leading = padded.ndim - 3
    selection = [slice(None)] * leading + [slice(1, -1)] * 3
    length = padded.shape[leading + direction]
    selection[leading + direction] = slice(1 + offset, length - 1 + offset)
    return padded[tuple(selection)]


def stencil_apply(
    vector, padded_vector, shear, lame, padded_shear, padded_lame, inertia, global_rows, cut_row
):
    result = inertia[None] * vector
    for direction in range(3):
        selector = (jnp.arange(3) == direction).astype(jnp.float32)[:, None, None, None]
        stiffness = shear[None] + (lame + shear)[None] * selector
        for offset in (1, -1):
            near_vector = shifted(padded_vector, direction, offset)
            near_shear = shifted(padded_shear, direction, offset)
            near_lame = shifted(padded_lame, direction, offset)
            near_stiffness = near_shear[None] + (near_lame + near_shear)[None] * selector
            face_weight = 0.5 * (stiffness + near_stiffness)
            if direction == 0:
                blocked_row = cut_row - 1 if offset == 1 else cut_row
                keep_rows = jnp.where(global_rows == blocked_row, 0.0, 1.0).astype(jnp.float32)
                face_weight = face_weight * keep_rows[None, :, None, None]
            result = result + face_weight * (vector - near_vector)
    return result


def barrier_weights(first_points, second_points, first_count, second_count, live_flag):
    offsets = first_points[:, :, None] - second_points[:, None, :]
    squared = jnp.sum(offsets * offsets, axis=0)
    point_width = first_points.shape[1]
    point_ranks = jnp.arange(point_width, dtype=jnp.int32)
    active = (point_ranks[:, None] < first_count) & (point_ranks[None, :] < second_count)
    active = active & (squared < barrier_reach) & (live_flag > 0)
    safe = jnp.where(active, squared, barrier_reach)
    excess = safe - barrier_reach
    return barrier_scale * (
        -2.0 * jnp.log(safe / barrier_reach) - 4.0 * excess / safe + excess * excess / (safe * safe)
    )


def pair_forces(weights, first_moves, second_moves):
    first_side = first_moves * jnp.sum(weights, axis=1)[None, :] - jnp.einsum(
        "ij,cj->ci", weights, second_moves, precision=lax.Precision.HIGHEST
    )
    second_side = second_moves * jnp.sum(weights, axis=0)[None, :] - jnp.einsum(
        "ij,ci->cj", weights, first_moves, precision=lax.Precision.HIGHEST
    )
    return (first_side, second_side)


def pair_task(packed):
    first_points, second_points, first_moves, second_moves, first_count, second_count, live_flag = (
        packed
    )
    weights = barrier_weights(first_points, second_points, first_count, second_count, live_flag)
    return pair_forces(weights, first_moves, second_moves)


def on_device(
    cotangent,
    shear_modulus,
    lame_first,
    inertia,
    surface_points,
    point_counts,
    surface_maps,
    contact_pairs,
):
    row_count, col_count, depth = shear_modulus.shape
    cell_count = row_count * col_count * depth
    slab_total = lax.axis_size("body")
    global_rows = lax.axis_index("body") * row_count + jnp.arange(row_count, dtype=jnp.int32)
    cut_row = slab_total // 4 * row_count
    material = padded_2(jnp.stack([shear_modulus, lame_first]), (("body", 1), ("across", 2)), 1)
    material = jnp.pad(material, ((0, 0), (0, 0), (0, 0), (1, 1)))
    points = surface_points[0, 0]
    counts = point_counts[0, 0]
    cell_maps = surface_maps[0, 0]
    pair_table = contact_pairs[0, 0]
    block_total = points.shape[0]
    point_width = points.shape[2]
    own_blocks = pair_table[0]
    partner_rows = pair_table[1]
    partner_blocks = pair_table[2]
    pair_order = jnp.arange(pair_table.shape[1], dtype=jnp.int32)
    same_partner = partner_rows[:, None] == partner_rows[None, :]
    earlier = pair_order[None, :] < pair_order[:, None]
    pair_ranks = jnp.sum((same_partner & earlier).astype(jnp.int32), axis=1)
    slot_index = partner_rows * CAP + pair_ranks
    slot_total = slab_total * CAP
    block_ids = jnp.arange(block_total, dtype=jnp.int32)
    pair_onehot = (own_blocks[:, None] == block_ids[None, :]).astype(jnp.float32)

    def to_slots(values):
        empty = jnp.zeros((slot_total,) + values.shape[1:], values.dtype)
        return empty.at[slot_index].set(values).reshape((slab_total, CAP) + values.shape[1:])

    sent_points = to_slots(points[own_blocks])
    slot_header = to_slots(
        jnp.stack([partner_blocks, counts[own_blocks], jnp.ones_like(own_blocks)], axis=1)
    )

    def pick_moves(vector):
        return vector.reshape(3, cell_count)[:, cell_maps].transpose(1, 0, 2)

    def collect(owner_forces, targets, returned):
        target_onehot = (targets.reshape(-1)[:, None] == block_ids[None, :]).astype(jnp.float32)
        owner_blocks = jnp.einsum(
            "nk,ncp->kcp",
            target_onehot,
            owner_forces.reshape(-1, 3, point_width),
            precision=lax.Precision.HIGHEST,
        )
        pair_back = returned.reshape(slot_total, 3, point_width)[slot_index]
        requester_blocks = jnp.einsum(
            "nk,ncp->kcp", pair_onehot, pair_back, precision=lax.Precision.HIGHEST
        )
        total_forces = owner_blocks + requester_blocks
        spread = (
            jnp.zeros((3, cell_count), jnp.float32)
            .at[:, cell_maps]
            .add(total_forces.transpose(1, 0, 2))
        )
        return spread.reshape(3, row_count, col_count, depth)

    def contact(vector):
        block_moves = pick_moves(vector)
        got_points = lax.all_to_all(sent_points, "body", split_axis=0, concat_axis=0, tiled=True)
        got_moves = lax.all_to_all(
            to_slots(block_moves[own_blocks]), "body", split_axis=0, concat_axis=0, tiled=True
        )
        got_header = lax.all_to_all(slot_header, "body", split_axis=0, concat_axis=0, tiled=True)
        slot_shape = (got_points.shape[0], got_points.shape[1], 3, point_width)
        flat_header = got_header.reshape(-1, 3)
        targets = flat_header[:, 0]
        first_side, second_side = lax.map(
            pair_task,
            (
                got_points.reshape(-1, 3, point_width),
                points[targets],
                got_moves.reshape(-1, 3, point_width),
                block_moves[targets],
                flat_header[:, 1],
                counts[targets],
                flat_header[:, 2],
            ),
            batch_size=16,
        )
        returned = lax.all_to_all(
            first_side.reshape(slot_shape), "body", split_axis=0, concat_axis=0, tiled=True
        )
        returned, owner_forces, targets = (
            returned,
            second_side.reshape(slot_shape),
            got_header[:, :, 0],
        )
        return collect(owner_forces, targets, returned)

    def apply_system(vector):
        padded_vector = padded_2(vector, (("body", 1), ("across", 2)), 1)
        padded_vector = jnp.pad(padded_vector, ((0, 0), (0, 0), (0, 0), (1, 1)))
        elastic = stencil_apply(
            vector,
            padded_vector,
            shear_modulus,
            lame_first,
            material[0],
            material[1],
            inertia,
            global_rows,
            cut_row,
        )
        return elastic + contact(vector)

    def two_products(residual, applied):
        return lax.psum(
            (jnp.sum(residual * residual), jnp.sum(residual * applied)), ("body", "across")
        )

    displacement = jnp.zeros_like(cotangent)
    residual = cotangent
    applied = apply_system(residual)
    norm_now, product = two_products(residual, applied)
    step_length = norm_now / product
    direction = residual
    along = applied
    for iteration in range(ITERS):
        displacement = displacement + step_length * direction
        residual = residual - step_length * along
        if iteration + 1 < ITERS:
            applied = apply_system(residual)
            norm_next, product = two_products(residual, applied)
            ratio = norm_next / norm_now
            step_length = norm_next / (product - ratio * norm_next / step_length)
            direction = residual + ratio * direction
            along = applied + ratio * along
            norm_now = norm_next
    return (displacement, residual)


def solution(mesh):
    placed = (
        P(None, "body", "across", None),
        P("body", "across", None),
        P("body", "across", None),
        P("body", "across", None),
        P("body", "across", None, None, None),
        P("body", "across", None),
        P("body", "across", None, None),
        P("body", "across", None, None),
    )
    return jax.shard_map(
        on_device,
        mesh=mesh,
        in_specs=placed,
        out_specs=(P(None, "body", "across", None), P(None, "body", "across", None)),
        check_vma=False,
    )
```

profile of v0, /device:TPU:0, one launch (start us, length us, event | category | flops | bytes accessed | tf_op | source)
XLA Modules:
  0.0 391.5 jit_solution(3844756696125490881)
XLA Ops:
  4.7 7.3 %all-to-all-start = ((s32[8,4,3]{1,2,0:T(4,128)}), s32[8,4,3]{1,2,0:T(4,128)S(1)}, u32[]{:S(2)}, u32[]{:S(2)}) async-start(s32[8,4,3]{1,2,0:T(4,128)} %copy.108), calls=%async_computation | async-start | bytes 32768 | tf_op jit(solution)/shard_map/all_to_all | solution.py:165
  12.9 3.9 %collective-permute-start.5 = (f32[3,1,32,256]{3,2,1,0:T(8,128)S(1)}, f32[3,1,32,256]{3,2,1,0:T(8,128)S(1)}, u32[]{:S(2)}, u32[]{:S(2)}) collective-permute-start(f32[3,1,32,256]{3,2,1,0:T(8,128)S(1)} %get-tuple-element.381), channel_id=1, source_target_pairs={{0,4},{4,8},{8,12},{12,16},{16,20},{20,24},{24,28},{1,5},{5,9},{9,... | collective-permute-start | bytes 294920 | tf_op jit(solution)/shard_map/ppermute | solution.py:22
  20.3 5.2 %collective-permute-start = (f32[2,1,32,256]{3,2,1,0:T(8,128)S(1)}, f32[2,1,32,256]{3,2,1,0:T(8,128)S(1)}, u32[]{:S(2)}, u32[]{:S(2)}) collective-permute-start(f32[2,1,32,256]{3,2,1,0:T(8,128)S(1)} %get-tuple-element.390), channel_id=1, source_target_pairs={{0,4},{4,8},{8,12},{12,16},{16,20},{20,24},{24,28},{1,5},{5,9},{9,... | collective-permute-start | bytes 196616 | tf_op jit(solution)/shard_map/ppermute | solution.py:22
  25.5 16.6 %copy.109 = f32[3,8,32,256]{0,3,2,1:T(8,128)} copy(f32[3,8,32,256]{3,2,1,0:T(8,128)S(1)} %copy-done.2) | data formatting | bytes 1572864 | tf_op args[0]
  43.4 18.2 %gather_fusion.1 = f32[2048,3]{1,0:T(8,128)} fusion(f32[3,65536]{0,1:T(8,128)} %bitcast.194, s32[2048]{0:T(1024)S(1)} %broadcast_clamp_fusion), kind=kCustom, calls=%fused_computation.1 | custom fusion | bytes 57344 | tf_op jit(solution)/shard_map/gather | solution.py:137
  69.3 6.0 %all-to-all-start.2 = ((f32[8,4,3,128]{3,1,2,0:T(4,128)}), f32[8,4,3,128]{3,1,2,0:T(4,128)S(1)}, u32[]{:S(2)}, u32[]{:S(2)}) async-start(f32[8,4,3,128]{3,1,2,0:T(4,128)} %copy.115), calls=%async_computation.2 | async-start | bytes 98304 | tf_op jit(solution)/shard_map/all_to_all | solution.py:161
  77.7 4.4 %all-to-all-done.2 = f32[8,4,3,128]{3,1,2,0:T(4,128)S(1)} async-done(((f32[8,4,3,128]{3,1,2,0:T(4,128)}), f32[8,4,3,128]{3,1,2,0:T(4,128)S(1)}, u32[]{:S(2)}, u32[]{:S(2)}) %all-to-all-start.2) | async-done | bytes 49184 | tf_op jit(solution)/shard_map/all_to_all | solution.py:161
  92.2 10.4 %while.28 = (s32[]{:T(128)}, f32[2,16,3,128]{3,2,1,0:T(4,128)S(1)}, f32[2,16,3,128]{3,2,1,0:T(4,128)S(1)}, f32[2,16,3,128]{3,1,0,2:T(8,128)S(1)}, s32[2,16]{1,0:...) while((s32[]{:T(128)}, f32[2,16,3,128]{3,2,1,0:T(4,128)S(1)}, ...), condition=%wide.region_10.11_spmd, body=%wide.region_6.10_spmd.sunk | while | flops 25452560 | bytes 5662313 | solution.py:169
  103.3 3.7 all-to-all-start.3
  119.9 25.0 %scatter_custom_fusion.3 = f32[3,65536]{0,1:T(8,128)} fusion(s32[2048]{0:T(1024)S(1)} %fusion.69, f32[2048,3]{1,0:T(8,128)} %bitcast.208, f32[]{:T(128)} %constant.135.clone.1), kind=kCustom, calls=%fused_computation.70 | custom fusion | flops 6144 | bytes 786944 | tf_op jit(solution)/shard_map/scatter-add | solution.py:155
  144.9 19.5 %copy.125 = f32[3,8,32,256]{3,2,1,0:T(8,128)S(1)} copy(f32[3,8,32,256]{0,3,2,1:T(8,128)} %bitcast.193) | data formatting | bytes 1572864 | tf_op jit(solution)/shard_map/reshape | solution.py:157
  164.4 5.1 %multiply_reduce_fusion.4 = (f32[]{:T(128)}, f32[]{:T(128)}, f32[3,8,32,256]{3,2,1,0:T(8,128)S(1)}) fusion(f32[3,8,32,256]{3,2,1,0:T(8,128)S(1)} %copy-done.2, f32[3,8,32,256]{3,2,1,0:T(8,128)S(1)} %copy.125, f32[3,10,34,258]{3,2,1,0:T(8,128)} %select_maximum_fusion.4, f32[8,32,256]{2,1,0:T(8,128)S(1)} %get-tuple-element.365, ...), kind=kLoop, calls=%fused_computation.148 | loop fusion | flops 11403262 | bytes 9105516 | tf_op jit(solution)/shard_map/reduce_sum | solution.py:210
  169.5 43.2 %all-reduce.4 = (f32[]{:T(128)}, f32[]{:T(128)}) all-reduce(f32[]{:T(128)} %get-tuple-element.305, f32[]{:T(128)} %get-tuple-element.304), channel_id=1, replica_groups=mesh['body'=8,'across'=4] {'body','across'}, use_global_device_ids=true, to_apply=%region_1.2 | all-reduce | flops 2 | bytes 16 | tf_op jit(solution)/shard_map/psum | solution.py:209
  214.1 16.6 %copy.126 = f32[3,8,32,256]{0,3,2,1:T(8,128)} copy(f32[3,8,32,256]{3,2,1,0:T(8,128)S(1)} %multiply_subtract_fusion.1) | data formatting | bytes 1572864 | tf_op jit(solution)/shard_map/sub | solution.py:222
  230.8 18.1 %gather_fusion.8 = f32[2048,3]{1,0:T(8,128)} fusion(f32[3,65536]{0,1:T(8,128)} %bitcast.195, s32[2048]{0:T(1024)S(1)} %broadcast_clamp_fusion), kind=kCustom, calls=%fused_computation.8 | custom fusion | bytes 57344 | tf_op jit(solution)/shard_map/gather | solution.py:137
  253.3 5.6 %all-to-all-start.4 = ((f32[8,4,3,128]{3,1,2,0:T(4,128)}), f32[8,4,3,128]{3,1,2,0:T(4,128)S(1)}, u32[]{:S(2)}, u32[]{:S(2)}) async-start(f32[8,4,3,128]{3,1,2,0:T(4,128)} %copy.128), calls=%async_computation.4 | async-start | bytes 98304 | tf_op jit(solution)/shard_map/all_to_all | solution.py:162
  261.0 4.8 %collective-permute-start.9 = (f32[3,1,32,256]{3,2,1,0:T(8,128)S(1)}, f32[3,1,32,256]{3,2,1,0:T(8,128)S(1)}, u32[]{:S(2)}, u32[]{:S(2)}) collective-permute-start(f32[3,1,32,256]{3,2,1,0:T(8,128)S(1)} %get-tuple-element.378), channel_id=1, source_target_pairs={{0,4},{4,8},{8,12},{12,16},{16,20},{20,24},{24,28},{1,5},{5,9},{9,... | collective-permute-start | bytes 294920 | tf_op jit(solution)/shard_map/ppermute | solution.py:22
  265.9 10.4 %while.29 = (s32[]{:T(128)}, f32[2,16,3,128]{3,2,1,0:T(4,128)S(1)}, f32[2,16,3,128]{3,2,1,0:T(4,128)S(1)}, f32[2,16,3,128]{3,1,0,2:T(8,128)S(1)}, s32[2,16]{1,0:...) while((s32[]{:T(128)}, f32[2,16,3,128]{3,2,1,0:T(4,128)S(1)}, ...), condition=%wide.region_21.22_spmd, body=%wide.region_17.21_spmd.sunk | while | flops 25452560 | bytes 5662313 | solution.py:169
  281.6 5.9 %all-to-all-start.5 = ((f32[8,4,3,128]{3,1,2,0:T(4,128)}), f32[8,4,3,128]{3,1,2,0:T(4,128)S(1)}, u32[]{:S(2)}, u32[]{:S(2)}) async-start(f32[8,4,3,128]{3,1,2,0:T(4,128)} %copy.134), calls=%async_computation.5 | async-start | bytes 98304 | tf_op jit(solution)/shard_map/all_to_all | solution.py:182
  289.7 4.7 %all-to-all-done.5 = f32[8,4,3,128]{3,1,2,0:T(4,128)S(1)} async-done(((f32[8,4,3,128]{3,1,2,0:T(4,128)}), f32[8,4,3,128]{3,1,2,0:T(4,128)S(1)}, u32[]{:S(2)}, u32[]{:S(2)}) %all-to-all-start.5) | async-done | bytes 49184 | tf_op jit(solution)/shard_map/all_to_all | solution.py:182
  296.6 25.0 %scatter_custom_fusion.5 = f32[3,65536]{0,1:T(8,128)} fusion(s32[2048]{0:T(1024)} %copy-done.25, f32[2048,3]{1,0:T(8,128)} %bitcast.207, f32[]{:T(128)} %constant.135.clone.1), kind=kCustom, calls=%fused_computation.68 | custom fusion | flops 6144 | bytes 786944 | tf_op jit(solution)/shard_map/scatter-add | solution.py:155
  321.6 20.2 %copy.138 = f32[3,8,32,256]{3,2,1,0:T(8,128)} copy(f32[3,8,32,256]{0,3,2,1:T(8,128)} %bitcast.192) | data formatting | bytes 1572864 | tf_op jit(solution)/shard_map/reshape | solution.py:157
  341.9 5.4 %multiply_reduce_fusion.2 = (f32[]{:T(128)}, f32[]{:T(128)}, f32[3,8,32,256]{3,2,1,0:T(8,128)S(1)}) fusion(f32[3,8,32,256]{3,2,1,0:T(8,128)S(1)} %multiply_subtract_fusion.1, f32[3,8,32,256]{3,2,1,0:T(8,128)} %copy.138, f32[3,10,34,258]{3,2,1,0:T(8,128)} %select_maximum_fusion, f32[8,32,256]{2,1,0:T(8,128)} %copy-done.8, ...), kind=kLoop, calls=%fused_computation.145 | loop fusion | flops 12189694 | bytes 8122476 | tf_op jit(solution)/shard_map/reduce_sum | solution.py:210
  347.3 38.2 %all-reduce.3 = (f32[]{:T(128)}, f32[]{:T(128)}) all-reduce(f32[]{:T(128)} %get-tuple-element.303, f32[]{:T(128)} %get-tuple-element.302), channel_id=1, replica_groups=mesh['body'=8,'across'=4] {'body','across'}, use_global_device_ids=true, to_apply=%region_15.16 | all-reduce | flops 2 | bytes 16 | tf_op jit(solution)/shard_map/psum | solution.py:209
  (223 shorter events, 81.3 us)
Async XLA Ops:
  1.4 116.9 %copy-start.29 = (s32[32]{0:T(128)}, s32[32]{0:T(128)S(1)}, u32[]{:S(2)}) copy-start(s32[32]{0:T(128)S(1)} %get-tuple-element.393) | copy-start | bytes 388
  2.3 64.9 %copy-start.21 = (s32[32]{0:T(128)}, s32[32]{0:T(128)S(1)}, u32[]{:S(2)}) copy-start(s32[32]{0:T(128)S(1)} %get-tuple-element.397) | copy-start | bytes 388
  2.3 64.2 %copy-start.23 = (s32[1024]{0:T(1024)}, s32[1024]{0:T(1024)S(1)}, u32[]{:S(2)}) copy-start(s32[1024]{0:T(1024)S(1)} %pad_clamp_fusion.2) | copy-start | bytes 12292
  4.7 64.6 %all-to-all-start = ((s32[8,4,3]{1,2,0:T(4,128)}), s32[8,4,3]{1,2,0:T(4,128)S(1)}, u32[]{:S(2)}, u32[]{:S(2)}) async-start(s32[8,4,3]{1,2,0:T(4,128)} %copy.108), calls=%async_computation | async-start | bytes 32768 | tf_op jit(solution)/shard_map/all_to_all | solution.py:165
  12.9 97.0 %collective-permute-start.5 = (f32[3,1,32,256]{3,2,1,0:T(8,128)S(1)}, f32[3,1,32,256]{3,2,1,0:T(8,128)S(1)}, u32[]{:S(2)}, u32[]{:S(2)}) collective-permute-start(f32[3,1,32,256]{3,2,1,0:T(8,128)S(1)} %get-tuple-element.381), channel_id=1, source_target_pairs={{0,4},{4,8},{8,12},{12,16},{16,20},{20,24},{24,28},{1,5},{5,9},{9,... | collective-permute-start | bytes 294920 | tf_op jit(solution)/shard_map/ppermute | solution.py:22
  16.9 93.1 %collective-permute-start.4 = (f32[3,1,32,256]{3,2,1,0:T(8,128)S(1)}, f32[3,1,32,256]{3,2,1,0:T(8,128)S(1)}, u32[]{:S(2)}, u32[]{:S(2)}) collective-permute-start(f32[3,1,32,256]{3,2,1,0:T(8,128)S(1)} %get-tuple-element.380), channel_id=1, source_target_pairs={{4,0},{8,4},{12,8},{16,12},{20,16},{24,20},{28,24},{5,1},{9,5},{13... | collective-permute-start | bytes 294920 | tf_op jit(solution)/shard_map/ppermute | solution.py:24
  19.0 66.4 %collective-permute-start.1 = (f32[2,1,32,256]{3,2,1,0:T(8,128)S(1)}, f32[2,1,32,256]{3,2,1,0:T(8,128)S(1)}, u32[]{:S(2)}, u32[]{:S(2)}) collective-permute-start(f32[2,1,32,256]{3,2,1,0:T(8,128)S(1)} %get-tuple-element.391), channel_id=1, source_target_pairs={{4,0},{8,4},{12,8},{16,12},{20,16},{24,20},{28,24},{5,1},{9,5},{13... | collective-permute-start | bytes 196616 | tf_op jit(solution)/shard_map/ppermute | solution.py:24
  20.3 65.2 %collective-permute-start = (f32[2,1,32,256]{3,2,1,0:T(8,128)S(1)}, f32[2,1,32,256]{3,2,1,0:T(8,128)S(1)}, u32[]{:S(2)}, u32[]{:S(2)}) collective-permute-start(f32[2,1,32,256]{3,2,1,0:T(8,128)S(1)} %get-tuple-element.390), channel_id=1, source_target_pairs={{0,4},{4,8},{8,12},{12,16},{16,20},{20,24},{24,28},{1,5},{5,9},{9,... | collective-permute-start | bytes 196616 | tf_op jit(solution)/shard_map/ppermute | solution.py:22
  42.1 77.7 %copy-start.25 = (s32[2048]{0:T(1024)}, s32[2048]{0:T(1024)S(1)}, u32[]{:S(2)}) copy-start(s32[2048]{0:T(1024)S(1)} %fusion.69) | copy-start | bytes 24580
  42.2 75.5 %copy-start.26 = (s32[1024]{0:T(1024)}, s32[1024]{0:T(1024)S(1)}, u32[]{:S(2)}) copy-start(s32[1024]{0:T(1024)S(1)} %pad_clamp_fusion) | copy-start | bytes 12292
  43.4 120.9 %copy-start.6 = (f32[8,32,256]{2,1,0:T(8,128)}, f32[8,32,256]{2,1,0:T(8,128)S(1)}, u32[]{:S(2)}) copy-start(f32[8,32,256]{2,1,0:T(8,128)S(1)} %add.349) | copy-start | bytes 786436
  69.3 12.8 %all-to-all-start.2 = ((f32[8,4,3,128]{3,1,2,0:T(4,128)}), f32[8,4,3,128]{3,1,2,0:T(4,128)S(1)}, u32[]{:S(2)}, u32[]{:S(2)}) async-start(f32[8,4,3,128]{3,1,2,0:T(4,128)} %copy.115), calls=%async_computation.2 | async-start | bytes 98304 | tf_op jit(solution)/shard_map/all_to_all | solution.py:161
  82.1 10.1 %all-to-all-start.1 = ((f32[8,4,3,128]{3,1,2,0:T(4,128)}), f32[8,4,3,128]{3,1,2,0:T(4,128)S(1)}, u32[]{:S(2)}, u32[]{:S(2)}) async-start(f32[8,4,3,128]{3,1,2,0:T(4,128)} %copy.111), calls=%async_computation.1 | async-start | bytes 98304 | tf_op jit(solution)/shard_map/all_to_all | solution.py:162
  85.5 21.5 %collective-permute-start.3 = (f32[2,10,1,256]{3,2,1,0:T(1,128)S(1)}, f32[2,10,1,256]{3,2,1,0:T(1,128)S(1)}, u32[]{:S(2)}, u32[]{:S(2)}) collective-permute-start(f32[2,10,1,256]{3,2,1,0:T(1,128)S(1)} %get-tuple-element.383), channel_id=1, source_target_pairs={{1,0},{2,1},{3,2},{5,4},{6,5},{7,6},{9,8},{10,9},{11,10},{13,12},{... | collective-permute-start | bytes 61448 | tf_op jit(solution)/shard_map/ppermute | solution.py:24
  86.8 20.2 %collective-permute-start.2 = (f32[2,10,1,256]{3,2,1,0:T(1,128)S(1)}, f32[2,10,1,256]{3,2,1,0:T(1,128)S(1)}, u32[]{:S(2)}, u32[]{:S(2)}) collective-permute-start(f32[2,10,1,256]{3,2,1,0:T(1,128)S(1)} %get-tuple-element.382), channel_id=1, source_target_pairs={{0,1},{1,2},{2,3},{4,5},{5,6},{6,7},{8,9},{9,10},{10,11},{12,13},{... | collective-permute-start | bytes 61448 | tf_op jit(solution)/shard_map/ppermute | solution.py:22
  103.3 14.4 %all-to-all-start.3 = ((f32[8,4,3,128]{3,1,2,0:T(4,128)}), f32[8,4,3,128]{3,1,2,0:T(4,128)S(1)}, u32[]{:S(2)}, u32[]{:S(2)}) async-start(f32[8,4,3,128]{3,1,2,0:T(4,128)} %copy.121), calls=%async_computation.3 | async-start | bytes 98304 | tf_op jit(solution)/shard_map/all_to_all | solution.py:182
  110.1 5.0 %collective-permute-start.6 = (f32[3,10,1,256]{3,2,1,0:T(1,128)S(1)}, f32[3,10,1,256]{3,2,1,0:T(1,128)S(1)}, u32[]{:S(2)}, u32[]{:S(2)}) collective-permute-start(f32[3,10,1,256]{3,2,1,0:T(1,128)S(1)} %get-tuple-element.375), channel_id=1, source_target_pairs={{1,0},{2,1},{3,2},{5,4},{6,5},{7,6},{9,8},{10,9},{11,10},{13,12},{... | collective-permute-start | bytes 92168 | tf_op jit(solution)/shard_map/ppermute | solution.py:24
  111.4 4.2 %collective-permute-start.7 = (f32[3,10,1,256]{3,2,1,0:T(1,128)S(1)}, f32[3,10,1,256]{3,2,1,0:T(1,128)S(1)}, u32[]{:S(2)}, u32[]{:S(2)}) collective-permute-start(f32[3,10,1,256]{3,2,1,0:T(1,128)S(1)} %get-tuple-element.374), channel_id=1, source_target_pairs={{0,1},{1,2},{2,3},{4,5},{5,6},{6,7},{8,9},{9,10},{10,11},{12,13},{... | collective-permute-start | bytes 92168 | tf_op jit(solution)/shard_map/ppermute | solution.py:22
  253.3 12.5 %all-to-all-start.4 = ((f32[8,4,3,128]{3,1,2,0:T(4,128)}), f32[8,4,3,128]{3,1,2,0:T(4,128)S(1)}, u32[]{:S(2)}, u32[]{:S(2)}) async-start(f32[8,4,3,128]{3,1,2,0:T(4,128)} %copy.128), calls=%async_computation.4 | async-start | bytes 98304 | tf_op jit(solution)/shard_map/all_to_all | solution.py:162
  259.7 16.6 %collective-permute-start.8 = (f32[3,1,32,256]{3,2,1,0:T(8,128)S(1)}, f32[3,1,32,256]{3,2,1,0:T(8,128)S(1)}, u32[]{:S(2)}, u32[]{:S(2)}) collective-permute-start(f32[3,1,32,256]{3,2,1,0:T(8,128)S(1)} %get-tuple-element.379), channel_id=1, source_target_pairs={{4,0},{8,4},{12,8},{16,12},{20,16},{24,20},{28,24},{5,1},{9,5},{13... | collective-permute-start | bytes 294920 | tf_op jit(solution)/shard_map/ppermute | solution.py:24
  261.0 15.4 %collective-permute-start.9 = (f32[3,1,32,256]{3,2,1,0:T(8,128)S(1)}, f32[3,1,32,256]{3,2,1,0:T(8,128)S(1)}, u32[]{:S(2)}, u32[]{:S(2)}) collective-permute-start(f32[3,1,32,256]{3,2,1,0:T(8,128)S(1)} %get-tuple-element.378), channel_id=1, source_target_pairs={{0,4},{4,8},{8,12},{12,16},{16,20},{20,24},{24,28},{1,5},{5,9},{9,... | collective-permute-start | bytes 294920 | tf_op jit(solution)/shard_map/ppermute | solution.py:22
  276.5 11.1 %collective-permute-start.10 = (f32[3,10,1,256]{3,2,1,0:T(1,128)S(1)}, f32[3,10,1,256]{3,2,1,0:T(1,128)S(1)}, u32[]{:S(2)}, u32[]{:S(2)}) collective-permute-start(f32[3,10,1,256]{3,2,1,0:T(1,128)S(1)} %get-tuple-element.373), channel_id=1, source_target_pairs={{1,0},{2,1},{3,2},{5,4},{6,5},{7,6},{9,8},{10,9},{11,10},{13,12},{... | collective-permute-start | bytes 92168 | tf_op jit(solution)/shard_map/ppermute | solution.py:24
  277.8 9.8 %collective-permute-start.11 = (f32[3,10,1,256]{3,2,1,0:T(1,128)S(1)}, f32[3,10,1,256]{3,2,1,0:T(1,128)S(1)}, u32[]{:S(2)}, u32[]{:S(2)}) collective-permute-start(f32[3,10,1,256]{3,2,1,0:T(1,128)S(1)} %get-tuple-element.372), channel_id=1, source_target_pairs={{0,1},{1,2},{2,3},{4,5},{5,6},{6,7},{8,9},{9,10},{10,11},{12,13},{... | collective-permute-start | bytes 92168 | tf_op jit(solution)/shard_map/ppermute | solution.py:22
  281.6 12.7 %all-to-all-start.5 = ((f32[8,4,3,128]{3,1,2,0:T(4,128)}), f32[8,4,3,128]{3,1,2,0:T(4,128)S(1)}, u32[]{:S(2)}, u32[]{:S(2)}) async-start(f32[8,4,3,128]{3,1,2,0:T(4,128)} %copy.134), calls=%async_computation.5 | async-start | bytes 98304 | tf_op jit(solution)/shard_map/all_to_all | solution.py:182
  (32 other events, 600.3 us)
where the time goes:
time: 393 us; the launch traced here: 392 us
  local copies, waits for them, and re-layouts  134 us (34%)
  other arithmetic  82.1 us (21%)
  blocking collectives  81.4 us (21%)
  starting transfers between devices  63.1 us (16%)
  waiting for transfers between devices  11.9 us (3%)
  matrix products  11.6 us (3%)
  between operations  7.32 us (2%)
    psum x2, blocking collectives, two_products(): lax.psum((jnp.sum(residual * residual), jnp.sum(residual * applied)), ('b...  81.4 us
    scatter-add x2, other arithmetic, collect(): spread = jnp.zeros((3, cell_count), jnp.float32).at[:, cell_maps].add(tot...  50 us
    reshape x2, local copies, waits for them, and re-layouts, collect(): return spread.reshape(3, row_count, col_count, depth)  39.7 us
    gather x4, local copies, waits for them, and re-layouts, pick_moves(): return vector.reshape(3, cell_count)[:, cell_maps].transpose(1, 0, 2)  39.5 us
    ppermute x6, starting transfers between devices, padded_2(): lax.ppermute(tail, axis, [(i, (i + 1) % count) for i in range(ends)])  23.5 us
    unnamed x80, local copies, waits for them, and re-layouts  16.9 us
    sub x1, local copies, waits for them, and re-layouts, on_device(): residual = residual - step_length * along  16.6 us
    reduce_sum x2, other arithmetic, two_products(): jnp.sum(residual * applied)  10.5 us
  transfers between devices with their start and end apart: 18, of which 5 were waited for; matrix products, arithmetic and copies ran while one was open for 20% of the time, Pallas kernels for 0%

commit v1 on v0

v1 whole, which is shorter than its diff:
```python
import jax
import jax.numpy as jnp
from jax import lax
from jax.experimental import pallas as pl
from jax.experimental.pallas import tpu as pltpu
from jax.sharding import PartitionSpec as P

F32 = jnp.float32
BF16 = jnp.bfloat16
I32 = jnp.int32

barrier_reach = 1.0
barrier_scale = 0.005
FAR = 1000.0

VMEM = pl.BlockSpec(memory_space=pltpu.VMEM)
SMEM = pl.BlockSpec(memory_space=pltpu.SMEM)


def sds(shape, dtype=F32):
    return jax.ShapeDtypeStruct(shape, dtype)


def call(body, name, in_specs, out_specs, out_shape, scratch=(), cost=2.0):
    estimate = pl.CostEstimate(flops=int(cost * 1e8), transcendentals=0, bytes_accessed=int(cost * 3e6))
    return pl.pallas_call(
        body,
        name=name,
        in_specs=in_specs,
        out_specs=out_specs,
        out_shape=out_shape,
        scratch_shapes=list(scratch),
        cost_estimate=estimate,
        compiler_params=pltpu.CompilerParams(vmem_limit_bytes=56 << 20),
    )


def split(values):
    high = values.astype(BF16)
    low = (values - high.astype(F32)).astype(BF16)
    return high, low


def even_faces(block, axis_parity, last):
    first = jnp.where(axis_parity == 0, last, 0)
    return first, last - first


def write_faces(sources, xe_ref, xo_ref, ye_ref, yo_ref):
    bpar = lax.rem(lax.axis_index("body"), 2)
    apar = lax.rem(lax.axis_index("across"), 2)
    for k, (ref, lead) in enumerate(sources):
        at = (lambda x: ref[lead, x]) if lead is not None else (lambda x: ref[x])
        rows = ref.shape[-3]
        cols = ref.shape[-2]
        xi = jnp.where(bpar == 0, rows - 1, 0)
        xe_ref[k] = at(xi)
        xo_ref[k] = at(rows - 1 - xi)
        for x in range(rows):
            slab = at(x)
            low = slab[0:1]
            high = slab[cols - 1 : cols]
            ye_ref[k, x : x + 1] = jnp.where(apar == 0, high, low)
            yo_ref[k, x : x + 1] = jnp.where(apar == 0, low, high)


def prepare_kernel(
    r_ref, sh_ref, la_ref, pt_ref, cnt_ref, pair_ref,
    xe_ref, xo_ref, ye_ref, yo_ref, msg_ref, own_ref, table_ref, fill_ref,
):
    bodies, width = msg_ref.shape[0], msg_ref.shape[1]
    blocks = pt_ref.shape[0]
    odd_total = blocks // 2
    cap = width - odd_total
    pairs = pair_ref.shape[1]
    lane = lax.broadcasted_iota(I32, (1, pt_ref.shape[2]), 1)
    for d in range(bodies):
        fill_ref[d] = 0

    def masked(k, far):
        return jnp.where(lane < cnt_ref[k], pt_ref[k], far)

    for k in range(blocks):
        own_ref[k, 0:3, :] = masked(k, -FAR)
        own_ref[k, 3:4, :] = jnp.ones_like(lane, F32)

    def odd_blocks(d, carry):
        for j in range(odd_total):
            msg_ref[d, cap + j, 0:3, :] = masked(2 * j + 1, FAR)
            msg_ref[d, cap + j, 3:4, :] = jnp.zeros_like(lane, F32)
        return carry

    lax.fori_loop(0, bodies, odd_blocks, 0)

    def place(n, carry):
        first = pair_ref[0, n]
        dest = pair_ref[1, n]
        second = pair_ref[2, n]
        rank = fill_ref[dest]
        fill_ref[dest] = rank + 1
        msg_ref[dest, rank, 0:3, :] = masked(first, FAR)
        msg_ref[dest, rank, 3:4, :] = jnp.full((1, lane.shape[1]), second.astype(F32))
        table_ref[0, dest * cap + rank] = first
        table_ref[1, dest * cap + rank] = second
        return carry

    lax.fori_loop(0, pairs, place, 0)
    sources = [(r_ref, 0), (r_ref, 1), (r_ref, 2), (sh_ref, None), (la_ref, None)]
    write_faces(sources, xe_ref, xo_ref, ye_ref, yo_ref)


def cell_parts(cells, depth):
    if depth & (depth - 1) == 0:
        shift = depth.bit_length() - 1
        return lax.shift_right_logical(cells, shift), jnp.bitwise_and(cells, depth - 1)
    row = cells // depth
    return row, cells - row * depth


def gather_into(load, rows, depth, map_ref, hi_ref, lo_ref, out_ref):
    for c in range(3):
        value = load(c)
        high, low = split(value)
        hi_ref[c * rows : (c + 1) * rows, :] = high
        lo_ref[c * rows : (c + 1) * rows, :] = low
    span = map_ref.shape[2]
    blocks = out_ref.shape[0]
    per = blocks // map_ref.shape[0]
    points = span // per
    depth_iota = lax.broadcasted_iota(I32, (depth, span), 0)
    row_iota = lax.broadcasted_iota(I32, (rows, span), 0)

    def chunk(j, carry):
        row, deep = cell_parts(map_ref[j], depth)
        onehot = jnp.where(depth_iota == deep, 1.0, 0.0).astype(BF16)
        picked = jnp.dot(hi_ref[...], onehot, preferred_element_type=F32)
        picked = picked + jnp.dot(lo_ref[...], onehot, preferred_element_type=F32)
        here = row_iota == row
        for c in range(3):
            part = jnp.where(here, picked[c * rows : (c + 1) * rows], 0.0)
            line = jnp.sum(part, axis=0, keepdims=True)
            for b in range(per):
                out_ref[j * per + b, c : c + 1, :] = line[:, b * points : (b + 1) * points]
        for b in range(per):
            out_ref[j * per + b, 3:4, :] = jnp.ones((1, points), F32)
        return carry

    lax.fori_loop(0, map_ref.shape[0], chunk, 0)


def gather_kernel(r_ref, map_ref, table_ref, move_ref, msg_ref, hi_ref, lo_ref):
    rows = r_ref.shape[1] * r_ref.shape[2]
    depth = r_ref.shape[3]
    gather_into(
        lambda c: r_ref[c].reshape(rows, depth), rows, depth, map_ref, hi_ref, lo_ref, move_ref
    )
    bodies, width = msg_ref.shape[0], msg_ref.shape[1]
    odd_total = move_ref.shape[0] // 2
    cap = width - odd_total

    def pack(d, carry):
        for s in range(cap):
            msg_ref[d, s] = move_ref[table_ref[0, d * cap + s]]
        for j in range(odd_total):
            msg_ref[d, cap + j] = move_ref[2 * j + 1]
        return carry

    lax.fori_loop(0, bodies, pack, 0)


def weights_kernel(got_ref, own_ref, table_ref, w_ref, target_ref):
    bodies, width = got_ref.shape[0], got_ref.shape[1]
    odd_total = own_ref.shape[0] // 2
    cap = width - odd_total
    pairs = bodies * cap
    points = own_ref.shape[2]

    def find(d, carry):
        for s in range(cap):
            target_ref[d * cap + s] = jnp.max(got_ref[d, s, 3:4, :]).astype(I32)
            target_ref[pairs + d * cap + s] = table_ref[0, d * cap + s]
        return carry

    lax.fori_loop(0, bodies, find, 0)

    def weigh(n, source, target):
        columns = jnp.transpose(jnp.concatenate([source, source], axis=0))
        squared = None
        for c in range(3):
            gap = columns[:, c : c + 1] - target[c : c + 1, :]
            squared = gap * gap if squared is None else squared + gap * gap
        inverse = 1.0 / squared
        q = 1.0 - inverse
        weight = barrier_scale * (-2.0 * jnp.log(squared) - 4.0 * q + q * q)
        weight = jnp.where(squared < barrier_reach, weight, 0.0)
        high, low = split(weight)
        w_ref[n, :, 0:points] = high
        w_ref[n, :, points:] = low

    def device(d, carry):
        for s in range(cap):
            n = d * cap + s
            weigh(n, got_ref[d, s], own_ref[target_ref[n]])
            odd = lax.shift_right_logical(table_ref[1, n], 1)
            weigh(pairs + n, got_ref[d, cap + odd], own_ref[table_ref[0, n]])
        return carry

    lax.fori_loop(0, bodies, device, 0)


def pair_forces(got_ref, slot_of, w_ref, target_ref, acc_ref):
    bodies = got_ref.shape[0]
    pairs = target_ref.shape[0] // 2
    cap = pairs // bodies
    points = got_ref.shape[3]
    acc_ref[...] = jnp.zeros_like(acc_ref)

    def one(n, moves):
        high = moves.astype(BF16).astype(F32)
        lhs = jnp.concatenate([high, moves - high], axis=0).astype(BF16)
        out = jnp.dot(lhs, w_ref[n], preferred_element_type=F32)
        part = (out[0:4, :points] + out[4:8, :points]) + (out[0:4, points:] + out[4:8, points:])
        return target_ref[n], part

    def device(d, carry):
        results = []
        for s in range(cap):
            n = d * cap + s
            results.append(one(n, got_ref[d, s]))
            results.append(one(pairs + n, got_ref[d, slot_of(d, s, n)]))
        for at, part in results:
            acc_ref[at] = acc_ref[at] + part
        return carry

    lax.fori_loop(0, bodies, device, 0)


def forces_one_kernel(
    got_ref, w_ref, target_ref, table_ref, move_ref, next_ref, force_ref, sum_ref, msg_ref, acc_ref
):
    bodies, width = got_ref.shape[0], got_ref.shape[1]
    blocks = move_ref.shape[0]
    cap = width - blocks // 2
    pairs = bodies * cap
    pair_forces(
        got_ref,
        lambda d, s, n: cap + lax.shift_right_logical(table_ref[1, n], 1),
        w_ref, target_ref, acc_ref,
    )
    for k in range(blocks):
        acc = acc_ref[k]
        force = move_ref[k] * acc[3:4] - acc
        force_ref[k] = force
        moved = next_ref[k]
        row = lax.broadcasted_iota(I32, moved.shape, 0)
        sum_ref[k] = jnp.where(row < 3, moved + force, 1.0)

    def pack(d, carry):
        for s in range(cap):
            n = d * cap + s
            msg_ref[d, s] = sum_ref[table_ref[0, n]]
            msg_ref[d, cap + s] = sum_ref[target_ref[n]]
        return carry

    lax.fori_loop(0, bodies, pack, 0)


def forces_two_kernel(got_ref, w_ref, target_ref, move_ref, dots_ref, force_ref, red_ref, acc_ref):
    cap = got_ref.shape[1] // 2
    pair_forces(got_ref, lambda d, s, n: cap + s, w_ref, target_ref, acc_ref)
    total = jnp.zeros((1, move_ref.shape[2]), F32)
    for k in range(move_ref.shape[0]):
        acc = acc_ref[k]
        moved = move_ref[k]
        force = moved * acc[3:4] - acc
        force_ref[k] = force
        total = total + jnp.sum((moved * force)[0:3], axis=0, keepdims=True)
    line = dots_ref[...]
    row = lax.broadcasted_iota(I32, line.shape, 0)
    line = line + jnp.where(row == 3, total, 0.0)
    for d in range(red_ref.shape[0]):
        red_ref[d] = line


def scatter_sum(base, rows, depth, map_ref, force_ref, left_ref, right_ref):
    span = map_ref.shape[2]
    per = force_ref.shape[0] // map_ref.shape[0]
    depth_iota = lax.broadcasted_iota(I32, (depth, span), 0)
    row_iota = lax.broadcasted_iota(I32, (rows, span), 0)
    chunks = map_ref.shape[0]
    for j in range(chunks):
        row, deep = cell_parts(map_ref[j], depth)
        onehot = jnp.where(depth_iota == deep, 1.0, 0.0).astype(BF16)
        right_ref[:, j * span : (j + 1) * span] = onehot
        right_ref[:, (chunks + j) * span : (chunks + j + 1) * span] = onehot
        here = row_iota == row
        for c in range(3):
            line = jnp.concatenate(
                [force_ref[j * per + b, c : c + 1, :] for b in range(per)], axis=1
            )
            high = line.astype(BF16).astype(F32)
            at = slice(c * rows, (c + 1) * rows)
            left_ref[at, j * span : (j + 1) * span] = jnp.where(here, high, 0.0).astype(BF16)
            left_ref[at, (chunks + j) * span : (chunks + j + 1) * span] = jnp.where(
                here, line - high, 0.0
            ).astype(BF16)
    spread = lax.dot_general(
        left_ref[...], right_ref[...], (((1,), (1,)), ((), ())), preferred_element_type=F32
    )
    return [base(c) + spread[c * rows : (c + 1) * rows] for c in range(3)]


def scatter_one_kernel(
    e_ref, force_ref, map_ref, w1_ref, xe_ref, xo_ref, ye_ref, yo_ref, left_ref, right_ref
):
    shape = e_ref.shape[1:]
    rows, depth = shape[0] * shape[1], shape[2]
    sums = scatter_sum(
        lambda c: e_ref[c].reshape(rows, depth), rows, depth, map_ref, force_ref, left_ref, right_ref
    )
    for c in range(3):
        w1_ref[c] = sums[c].reshape(shape)
    write_faces([(w1_ref, 0), (w1_ref, 1), (w1_ref, 2)], xe_ref, xo_ref, ye_ref, yo_ref)


def scatter_two_kernel(e_ref, force_ref, map_ref, w2_ref, left_ref, right_ref):
    shape = e_ref.shape[1:]
    rows, depth = shape[0] * shape[1], shape[2]
    sums = scatter_sum(
        lambda c: e_ref[c].reshape(rows, depth), rows, depth, map_ref, force_ref, left_ref, right_ref
    )
    for c in range(3):
        w2_ref[c] = sums[c].reshape(shape)


def elastic(v_ref, sh_ref, la_ref, in_ref, vector_halo, stiff_halo, emit):
    rows, cols, depth = sh_ref.shape
    b, a = lax.axis_index("body"), lax.axis_index("across")
    bodies, acrosses = lax.axis_size("body"), lax.axis_size("across")
    bpar, apar = lax.rem(b, 2), lax.rem(a, 2)
    cut = bodies // 4
    x_low = jnp.where(b != 0, 1.0, 0.0).astype(F32)
    x_high = jnp.where(b != bodies - 1, 1.0, 0.0).astype(F32)
    keep_low = jnp.where(b != cut, 1.0, 0.0).astype(F32)
    keep_high = jnp.where(b + 1 != cut, 1.0, 0.0).astype(F32)
    y_low = jnp.where(a != 0, 1.0, 0.0).astype(F32)
    y_high = jnp.where(a != acrosses - 1, 1.0, 0.0).astype(F32)
    vxe, vxo, vye, vyo = vector_halo
    sxe, sxo, sye, syo = stiff_halo
    row = lax.broadcasted_iota(I32, (cols, depth), 0)
    lane = lax.broadcasted_iota(I32, (cols, depth), 1)
    z_mask = jnp.where(lane == depth - 1, 0.0, 1.0)
    start = lane == 0
    top = row == cols - 1
    bottom = row == 0

    def stiffness(shear, lame):
        return 0.5 * shear, shear + 0.5 * lame

    def pick(parity, even, odd):
        return jnp.where(parity == 0, even, odd)

    def x_halo(high):
        e, o = (sxe, sxo) if high else (sxo, sxe)
        there = x_high if high else x_low
        shear, lame = pick(bpar, e[3], o[3]), pick(bpar, e[4], o[4])
        e, o = (vxe, vxo) if high else (vxo, vxe)
        values = [there * pick(bpar, e[c], o[c]) for c in range(3)]
        return stiffness(there * shear, there * lame), values

    def y_halo(high, x):
        e, o = (sye, syo) if high else (syo, sye)
        there = y_high if high else y_low
        at = slice(x, x + 1)
        shear, lame = pick(apar, e[3, at], o[3, at]), pick(apar, e[4, at], o[4, at])
        e, o = (vye, vyo) if high else (vyo, vye)
        values = [there * pick(apar, e[c, at], o[c, at]) for c in range(3)]
        return stiffness(there * shear, there * lame), values

    def slab(x):
        return stiffness(sh_ref[x], la_ref[x]), [v_ref[c, x] for c in range(3)]

    def flux(near, far, along, mask):
        (off, diag), values = near
        (far_off, far_diag), far_values = far
        side, front = off + far_off, diag + far_diag
        if mask is not None:
            side, front = side * mask, front * mask
        return [
            (front if c == along else side) * (values[c] - far_values[c]) for c in range(3)
        ]

    before = flux(x_halo(False), slab(0), 0, keep_low)
    here = slab(0)
    for x in range(rows):
        after = slab(x + 1) if x + 1 < rows else x_halo(True)
        out = flux(here, after, 0, None if x + 1 < rows else keep_high)
        (off, diag), values = here
        inertia = in_ref[x]
        total = [inertia * values[c] + (out[c] - before[c]) for c in range(3)]
        before = out

        def up(value, edge):
            return jnp.where(top, edge, pltpu.roll(value, cols - 1, 0))

        (h_off, h_diag), h_values = y_halo(True, x)
        shifted = (up(off, h_off), up(diag, h_diag)), [up(values[c], h_values[c]) for c in range(3)]
        out = flux(here, shifted, 1, None)
        first = (off[0:1], diag[0:1]), [values[c][0:1] for c in range(3)]
        edge = flux(y_halo(False, x), first, 1, None)
        total = [
            total[c] + (out[c] - jnp.where(bottom, edge[c], pltpu.roll(out[c], 1, 0)))
            for c in range(3)
        ]

        def right(value):
            return z_mask * pltpu.roll(value, depth - 1, 1)

        shifted = (right(off), right(diag)), [right(values[c]) for c in range(3)]
        out = flux(here, shifted, 2, None)
        edge = [-(diag if c == 2 else off) * values[c] for c in range(3)]
        total = [
            total[c] + (out[c] - jnp.where(start, edge[c], pltpu.roll(out[c], 1, 1)))
            for c in range(3)
        ]
        emit(x, total)
        here = after


def stencil_one_kernel(
    r_ref, sh_ref, la_ref, in_ref, xe, xo, ye, yo, map_ref, e_ref, next_ref, hi_ref, lo_ref
):
    def emit(x, total):
        for c in range(3):
            e_ref[c, x] = total[c]

    elastic(r_ref, sh_ref, la_ref, in_ref, (xe, xo, ye, yo), (xe, xo, ye, yo), emit)
    rows, depth = e_ref.shape[1] * e_ref.shape[2], e_ref.shape[3]
    gather_into(
        lambda c: e_ref[c].reshape(rows, depth), rows, depth, map_ref, hi_ref, lo_ref, next_ref
    )


def fold(value):
    cols, depth = value.shape
    total = None
    for k in range(depth // 128):
        part = value[:, k * 128 : (k + 1) * 128]
        part = jnp.sum(part.reshape(cols // 8, 8, 128), axis=0)
        total = part if total is None else total + part
    return total


def stencil_two_kernel(
    w_ref, sh_ref, la_ref, in_ref, xe, xo, ye, yo, cxe, cxo, cye, cyo, r_ref, e_ref, dots_ref
):
    sums = [jnp.zeros((8, 128), F32) for _ in range(4)]

    def emit(x, total):
        for c in range(3):
            e_ref[c, x] = total[c]
            r, w = r_ref[c, x], w_ref[c, x]
            sums[0] = sums[0] + fold(r * r)
            sums[1] = sums[1] + fold(r * w)
            sums[2] = sums[2] + fold(w * w)
            sums[3] = sums[3] + fold(w * total[c])

    elastic(w_ref, sh_ref, la_ref, in_ref, (xe, xo, ye, yo), (cxe, cxo, cye, cyo), emit)
    for k in range(4):
        dots_ref[k : k + 1, :] = jnp.sum(sums[k], axis=0, keepdims=True)


def final_kernel(r_ref, w1_ref, w2_ref, red_ref, x_ref, res_ref):
    line = jnp.sum(red_ref[...], axis=0)
    moment = [
        jnp.broadcast_to(jnp.sum(line[k : k + 1], axis=1, keepdims=True), (8, 128)) for k in range(4)
    ]
    m0, m1, m2, m3 = moment
    step = m0 / m1
    norm = (m0 - step * m1) + step * (step * m2 - m1)
    ratio = norm / m0
    grown = 1.0 + ratio
    curve = grown * (grown * m1 - 2.0 * step * m2) + step * step * m3
    next_step = norm / curve
    alpha = step + next_step * grown
    gamma = next_step * step
    cols, depth = r_ref.shape[2], r_ref.shape[3]
    alpha = jnp.broadcast_to(alpha[0:1, 0:1], (cols, depth))
    gamma = jnp.broadcast_to(gamma[0:1, 0:1], (cols, depth))
    for c in range(3):
        for x in range(r_ref.shape[1]):
            r, w1 = r_ref[c, x], w1_ref[c, x]
            x_ref[c, x] = alpha * r - gamma * w1
            res_ref[c, x] = r - alpha * w1 + gamma * w2_ref[c, x]


def exchange(xe, xo, ye, yo):
    def pairs(axis, start):
        count = lax.axis_size(axis)
        chosen = []
        for i in range(count):
            partner = i + 1 if (i - start) % 2 == 0 else i - 1
            chosen.append((i, partner if 0 <= partner < count else i))
        return chosen

    return (
        lax.ppermute(xe, "body", pairs("body", 0)),
        lax.ppermute(xo, "body", pairs("body", 1)),
        lax.ppermute(ye, "across", pairs("across", 0)),
        lax.ppermute(yo, "across", pairs("across", 1)),
    )


def on_device(
    cotangent, shear, lame, inertia, surface_points, point_counts, surface_maps, contact_pairs
):
    rows, cols, depth = shear.shape
    points = surface_points[0, 0]
    counts = point_counts[0, 0]
    cell_maps = surface_maps[0, 0]
    pair_table = contact_pairs[0, 0]
    blocks, _, width = points.shape
    pairs = pair_table.shape[1]
    bodies, acrosses = lax.axis_size("body"), lax.axis_size("across")
    devices = bodies * acrosses
    cap = pairs // bodies
    slots = cap + blocks // 2
    chunks = blocks // 2
    cell_maps = cell_maps.reshape(chunks, 1, 2 * width)
    flat = rows * cols
    vector = sds((3, rows, cols, depth))

    def faces(count):
        return (
            sds((count, cols, depth)), sds((count, cols, depth)),
            sds((count, rows, depth)), sds((count, rows, depth)),
        )

    moves = sds((blocks, 4, width))
    halves = (pltpu.VMEM((3 * flat, depth), BF16), pltpu.VMEM((3 * flat, depth), BF16))
    wide = 2 * blocks * width
    sides = (pltpu.VMEM((3 * flat, wide), BF16), pltpu.VMEM((depth, wide), BF16))

    xe, xo, ye, yo, static_message, own_points, table = call(
        prepare_kernel, "prepare",
        [VMEM] * 4 + [SMEM] * 2,
        [VMEM] * 6 + [SMEM],
        faces(5) + (sds((bodies, slots, 4, width)), moves, sds((2, pairs), I32)),
        scratch=(pltpu.SMEM((bodies,), I32),), cost=1.0,
    )(cotangent, shear, lame, points, counts, pair_table)
    got_static = lax.all_to_all(static_message, "body", 0, 0, tiled=True)
    first_moves, message = call(
        gather_kernel, "gather", [VMEM] * 2 + [SMEM], [VMEM] * 2,
        (moves, sds((bodies, slots, 4, width))), scratch=halves, cost=3.0,
    )(cotangent, cell_maps, table)
    got_moves = lax.all_to_all(message, "body", 0, 0, tiled=True)
    halo = exchange(xe, xo, ye, yo)
    weights, targets = call(
        weights_kernel, "weights", [VMEM] * 2 + [SMEM], [VMEM, SMEM],
        (sds((2 * pairs, width, 2 * width), BF16), sds((2 * pairs,), I32)), cost=6.0,
    )(got_static, own_points, table)
    elastic_one, next_moves = call(
        stencil_one_kernel, "stencil_one", [VMEM] * 9, [VMEM] * 2, (vector, moves),
        scratch=halves, cost=5.0,
    )(cotangent, shear, lame, inertia, *halo, cell_maps)
    force_one, second_moves, message = call(
        forces_one_kernel, "forces_one", [VMEM] * 2 + [SMEM] * 2 + [VMEM] * 2, [VMEM] * 3,
        (moves, moves, sds((bodies, 2 * cap, 4, width))),
        scratch=(pltpu.VMEM((blocks, 4, width), F32),), cost=2.0,
    )(got_moves, weights, targets, table, first_moves, next_moves)
    got_moves = lax.all_to_all(message, "body", 0, 0, tiled=True)
    w1, xe, xo, ye, yo = call(
        scatter_one_kernel, "scatter_one", [VMEM] * 3, [VMEM] * 5, (vector,) + faces(3),
        scratch=sides, cost=3.0,
    )(elastic_one, force_one, cell_maps)
    halo_two = exchange(xe, xo, ye, yo)
    elastic_two, dots = call(
        stencil_two_kernel, "stencil_two", [VMEM] * 13, [VMEM] * 2, (vector, sds((4, 128))), cost=3.0,
    )(w1, shear, lame, inertia, *halo_two, *halo, cotangent)
    force_two, partial = call(
        forces_two_kernel, "forces_two", [VMEM] * 2 + [SMEM] + [VMEM] * 2, [VMEM] * 2,
        (moves, sds((devices, 4, 128))),
        scratch=(pltpu.VMEM((blocks, 4, width), F32),), cost=2.0,
    )(got_moves, weights, targets, second_moves, dots)
    sums = lax.all_to_all(partial, ("body", "across"), 0, 0, tiled=True)
    w2 = call(
        scatter_two_kernel, "scatter_two", [VMEM] * 3, VMEM, vector, scratch=sides, cost=3.0,
    )(elastic_two, force_two, cell_maps)
    return call(
        final_kernel, "final", [VMEM] * 4, [VMEM] * 2, (vector, vector), cost=1.0,
    )(cotangent, w1, w2, sums)


def solution(mesh):
    placed = (
        P(None, "body", "across", None),
        P("body", "across", None),
        P("body", "across", None),
        P("body", "across", None),
        P("body", "across", None, None, None),
        P("body", "across", None),
        P("body", "across", None, None),
        P("body", "across", None, None),
    )
    return jax.shard_map(
        on_device,
        mesh=mesh,
        in_specs=placed,
        out_specs=(P(None, "body", "across", None), P(None, "body", "across", None)),
        check_vma=False,
    )
```

time: 393 us -> 105 us (0.27)
  local copies, waits for them, and re-layouts: 134 us -> 6.57 us
  other arithmetic: 82.1 us -> 0 us
  blocking collectives: 81.4 us -> 0 us
  Pallas kernels: 0 us -> 48.3 us
  starting transfers between devices: 63.1 us -> 36.4 us
  matrix products: 11.6 us -> 0 us
  between operations: 7.32 us -> 0.73 us
    psum x2 -> x0, blocking collectives: 81.4 us -> none  [two_products(): lax.psum((jnp.sum(residual * residual), jnp.sum(residual * applied)), ('b...]
    scatter-add x2 -> x0, other arithmetic: 50 us -> none  [collect(): spread = jnp.zeros((3, cell_count), jnp.float32).at[:, cell_maps].add(tot...]
    pallas_call x0 -> x10, Pallas kernels: none -> 48.3 us  [the longest x1 10.6 us: on_device(): call(weights_kernel, 'weights', [VMEM] * 2 + [SMEM], [VMEM, SMEM], (sds((...]
    gather x14 -> x0, local copies, waits for them, and re-layouts: 46.1 us -> none  [the longest x4 39.5 us: pick_moves(): return vector.reshape(3, cell_count)[:, cell_maps].transpose(1, 0, 2)]
    reshape x8 -> x0, local copies, waits for them, and re-layouts: 42.5 us -> none  [the longest x2 39.7 us: collect(): return spread.reshape(3, row_count, col_count, depth)]
    ppermute x12 -> x8, starting transfers between devices: 31.3 us -> 9.85 us  [the longest x2 3.94 us: exchange(): lax.ppermute(xe, 'body', pairs('body', 0))]
    reduce_sum x11 -> x0, other arithmetic: 19.4 us -> none  [the longest x2 10.5 us: two_products(): jnp.sum(residual * applied)]
    sub x5 -> x0, local copies, waits for them, and re-layouts: 16.7 us -> none  [the longest x1 16.6 us: on_device(): residual = residual - step_length * along]
  transfers between devices with their start and end apart: 18 -> 12, of which waited for: 5 -> 4; matrix products, arithmetic and copies ran while one was open for 20% -> 0% of each run, Pallas kernels for 0% -> 32%
where the time goes in v1:
time: 105 us; the launch traced here: 104 us
  Pallas kernels  48.3 us (46%)
  starting transfers between devices  36.4 us (35%)
  waiting for transfers between devices  11.6 us (11%)
  local copies, waits for them, and re-layouts  6.57 us (6%)
    pallas_call x1, Pallas kernels, on_device(): call(weights_kernel, 'weights', [VMEM] * 2 + [SMEM], [VMEM, SMEM], (sds((...  10.6 us
    all_to_all x1, starting transfers between devices, on_device(): sums = lax.all_to_all(partial, ('body', 'across'), 0, 0, tiled=True)  10.1 us
    all_to_all x2, starting transfers between devices, on_device(): got_moves = lax.all_to_all(message, 'body', 0, 0, tiled=True)  9.08 us
    all_to_all x1, starting transfers between devices, on_device(): got_static = lax.all_to_all(static_message, 'body', 0, 0, tiled=True)  7.32 us
    unnamed x26, local copies, waits for them, and re-layouts  6.57 us
    pallas_call x1, Pallas kernels, on_device(): call(stencil_one_kernel, 'stencil_one', [VMEM] * 9, [VMEM] * 2, (vector,...  6.21 us
    ppermute x2, waiting for transfers between devices, exchange(): lax.ppermute(xe, 'body', pairs('body', 0))  5.19 us
    pallas_call x1, Pallas kernels, on_device(): call(gather_kernel, 'gather', [VMEM] * 2 + [SMEM], [VMEM] * 2, (moves, sd...  5.07 us
  transfers between devices with their start and end apart: 12, of which 4 were waited for; matrix products, arithmetic and copies ran while one was open for 0% of the time, Pallas kernels for 32%

profile of v1, /device:TPU:0, one launch (start us, length us, event | category | flops | bytes accessed | tf_op | source)
XLA Modules:
  0.0 103.6 jit_solution(16374400991329129850)
XLA Ops:
  1.9 1.4 %copy.14 = f32[1,1,16,3,128]{4,3,2,1,0:T(4,128)} copy(f32[1,1,16,3,128]{4,2,3,1,0:T(8,128)} %param.12) | data formatting | bytes 49152 | tf_op args[4]
  3.3 2.7 %prepare.1 = (f32[5,32,256]{2,1,0:T(8,128)}, f32[5,32,256]{2,1,0:T(8,128)}, f32[5,8,256]{2,1,0:T(8,128)}, f32[5,8,256]{2,1,0:T(8,128)}, f32[8,12,4,128]{3,2,1,0:...) custom-call(f32[3,8,32,256]{3,2,1,0:T(8,128)} %r_ref.9, f32[8,32,256]{2,1,0:T(8,128)} %sh_ref.5, f32[8,32,256]{2,1,0:T(8,128)} %la_ref.5, ...), custom_call_target="tpu_custom_call" | custom-call | flops 100000000 | bytes 3000000 | tf_op jit(solution)/shard_map/prepare/pallas_call | solution.py:544
  6.0 7.3 %all-to-all-start.1 = ((f32[8,12,4,128]{3,2,1,0:T(4,128)}), f32[8,12,4,128]{3,2,1,0:T(4,128)S(1)}, u32[]{:S(2)}, u32[]{:S(2)}) async-start(f32[8,12,4,128]{3,2,1,0:T(4,128)} %get-tuple-element.34), calls=%async_computation.1 | async-start | bytes 393216 | tf_op jit(solution)/shard_map/all_to_all | solution.py:551
  13.3 5.1 %gather.1 = (f32[16,4,128]{2,1,0:T(4,128)}, f32[8,12,4,128]{3,2,1,0:T(4,128)}) custom-call(f32[3,8,32,256]{3,2,1,0:T(8,128)} %r_ref.9, s32[8,1,256]{2,1,0:T(1,128)} %bitcast.9, s32[2,32]{1,0:T(2,128)} %get-tuple-element.32.table_ref), custom_call_target="tpu_custom_call" | custom-call | flops 300000000 | bytes 9000000 | tf_op jit(solution)/shard_map/gather/pallas_call | solution.py:552
  18.3 2.9 %all-to-all-done.1.got_ref = f32[8,12,4,128]{3,2,1,0:T(4,128)S(1)} async-done(((f32[8,12,4,128]{3,2,1,0:T(4,128)}), f32[8,12,4,128]{3,2,1,0:T(4,128)S(1)}, u32[]{:S(2)}, u32[]{:S(2)}) %all-to-all-start.1) | async-done | bytes 196640 | tf_op jit(solution)/shard_map/all_to_all | solution.py:551
  21.2 3.4 %all-to-all-start = ((f32[8,12,4,128]{3,2,1,0:T(4,128)}), f32[8,12,4,128]{3,2,1,0:T(4,128)S(1)}, u32[]{:S(2)}, u32[]{:S(2)}) async-start(f32[8,12,4,128]{3,2,1,0:T(4,128)} %get-tuple-element.33), calls=%async_computation | async-start | bytes 393216 | tf_op jit(solution)/shard_map/all_to_all | solution.py:556
  24.6 1.9 %collective-permute-start = (f32[5,32,256]{2,1,0:T(8,128)}, f32[5,32,256]{2,1,0:T(8,128)S(1)}, u32[]{:S(2)}, u32[]{:S(2)}) collective-permute-start(f32[5,32,256]{2,1,0:T(8,128)} %get-tuple-element.27), channel_id=1, source_target_pairs={{0,4},{4,0},{8,12},{12,8},{16,20},{20,16},{24,28},{28,24},{1,5},{5... | collective-permute-start | bytes 491528 | tf_op jit(solution)/shard_map/ppermute | solution.py:507
  26.6 1.6 %collective-permute-start.1 = (f32[5,32,256]{2,1,0:T(8,128)}, f32[5,32,256]{2,1,0:T(8,128)S(1)}, u32[]{:S(2)}, u32[]{:S(2)}) collective-permute-start(f32[5,32,256]{2,1,0:T(8,128)} %get-tuple-element.28), channel_id=1, source_target_pairs={{0,0},{4,8},{8,4},{12,16},{16,12},{20,24},{24,20},{28,28},{1,1},{5... | collective-permute-start | bytes 491528 | tf_op jit(solution)/shard_map/ppermute | solution.py:508
  28.1 1.4 %collective-permute-start.3 = (f32[5,8,256]{2,1,0:T(8,128)}, f32[5,8,256]{2,1,0:T(8,128)S(1)}, u32[]{:S(2)}, u32[]{:S(2)}) collective-permute-start(f32[5,8,256]{2,1,0:T(8,128)} %get-tuple-element.30), channel_id=1, source_target_pairs={{0,0},{1,2},{2,1},{3,3},{4,4},{5,6},{6,5},{7,7},{8,8},{9,10},{10,9... | collective-permute-start | bytes 122888 | tf_op jit(solution)/shard_map/ppermute | solution.py:510
  29.6 4.9 %collective-permute-done.xe.cxe = f32[5,32,256]{2,1,0:T(8,128)S(1)} collective-permute-done((f32[5,32,256]{2,1,0:T(8,128)}, f32[5,32,256]{2,1,0:T(8,128)S(1)}, u32[]{:S(2)}, u32[]{:S(2)}) %collective-permute-start) | collective-permute-done | bytes 163872 | tf_op jit(solution)/shard_map/ppermute | solution.py:507
  35.8 6.2 %stencil_one.1 = (f32[3,8,32,256]{3,2,1,0:T(8,128)}, f32[16,4,128]{2,1,0:T(4,128)}) custom-call(f32[3,8,32,256]{3,2,1,0:T(8,128)} %r_ref.9, f32[8,32,256]{2,1,0:T(8,128)} %sh_ref.5, f32[8,32,256]{2,1,0:T(8,128)} %la_ref.5, f32[8,32,256]{2,1,0:T(8,128)} %in_ref.3, f32[5,32,256]{2,1,0:T(8,128)} %copy-done.1, f32[5,32,256]{2,1,0:T(8,128)} %copy-done.2, ...), custom_call_target="tpu_custom_call" | custom-call | flops 500000000 | bytes 15000000 | tf_op jit(solution)/shard_map/stencil_one/pallas_call | solution.py:562
  42.0 10.6 %weights.1 = (bf16[64,128,256]{2,1,0:T(8,128)(2,1)}, s32[64]{0:T(128)}) custom-call(f32[8,12,4,128]{3,2,1,0:T(4,128)} %copy-done.5, f32[16,4,128]{2,1,0:T(4,128)} %get-tuple-element.35.own_ref, s32[2,32]{1,0:T(2,128)} %get-tuple-element.32.table_ref), custom_call_target="tpu_custom_call" | custom-call | flops 600000000 | bytes 18000000 | tf_op jit(solution)/shard_map/weights/pallas_call | solution.py:558
  53.3 4.5 %forces_one.1 = (f32[16,4,128]{2,1,0:T(4,128)}, f32[16,4,128]{2,1,0:T(4,128)}, f32[8,8,4,128]{3,2,1,0:T(4,128)}) custom-call(f32[8,12,4,128]{3,2,1,0:T(4,128)} %copy-done, bf16[64,128,256]{2,1,0:T(8,128)(2,1)} %get-tuple-element.36.w_ref, s32[64]{0:T(128)} %get-tuple-element.37.target_ref, s32[2,32]{1,0:T(2,128)} %get-tuple-element.32.table_ref, ...), custom_call_target="tpu_custom_call" | custom-call | flops 200000000 | bytes 6000000 | tf_op jit(solution)/shard_map/forces_one/pallas_call | solution.py:566
  57.8 5.7 %all-to-all-start.2 = ((f32[8,8,4,128]{3,2,1,0:T(4,128)}), f32[8,8,4,128]{3,2,1,0:T(4,128)S(1)}, u32[]{:S(2)}, u32[]{:S(2)}) async-start(f32[8,8,4,128]{3,2,1,0:T(4,128)} %get-tuple-element.47), calls=%async_computation.2 | async-start | bytes 262144 | tf_op jit(solution)/shard_map/all_to_all | solution.py:571
  63.5 3.9 %scatter_one.1 = (f32[3,8,32,256]{3,2,1,0:T(8,128)}, f32[3,32,256]{2,1,0:T(8,128)}, f32[3,32,256]{2,1,0:T(8,128)}, f32[3,8,256]{2,1,0:T(8,128)}, f32[3,8,256]{2,1,0:T(8,128)}) custom-call(f32[3,8,32,256]{3,2,1,0:T(8,128)} %get-tuple-element.31.e_ref, f32[16,4,128]{2,1,0:T(4,128)} %get-tuple-element.40.force_ref, s32[8,1,256]{2,1,0:T(1,128)} %bitcast.11), custom_call_target="tpu_custom_call" | custom-call | flops 300000000 | bytes 9000000 | tf_op jit(solution)/shard_map/scatter_one/pallas_call | solution.py:572
  67.5 2.0 %collective-permute-start.4 = (f32[3,32,256]{2,1,0:T(8,128)}, f32[3,32,256]{2,1,0:T(8,128)S(1)}, u32[]{:S(2)}, u32[]{:S(2)}) collective-permute-start(f32[3,32,256]{2,1,0:T(8,128)} %get-tuple-element.42), channel_id=1, source_target_pairs={{0,4},{4,0},{8,12},{12,8},{16,20},{20,16},{24,28},{28,24},{1,5},{5... | collective-permute-start | bytes 294920 | tf_op jit(solution)/shard_map/ppermute | solution.py:507
  69.5 1.5 %collective-permute-start.5 = (f32[3,32,256]{2,1,0:T(8,128)}, f32[3,32,256]{2,1,0:T(8,128)S(1)}, u32[]{:S(2)}, u32[]{:S(2)}) collective-permute-start(f32[3,32,256]{2,1,0:T(8,128)} %get-tuple-element.43), channel_id=1, source_target_pairs={{0,0},{4,8},{8,4},{12,16},{16,12},{20,24},{24,20},{28,28},{1,1},{5... | collective-permute-start | bytes 294920 | tf_op jit(solution)/shard_map/ppermute | solution.py:508
  71.0 1.4 %collective-permute-start.7 = (f32[3,8,256]{2,1,0:T(8,128)}, f32[3,8,256]{2,1,0:T(8,128)S(1)}, u32[]{:S(2)}, u32[]{:S(2)}) collective-permute-start(f32[3,8,256]{2,1,0:T(8,128)} %get-tuple-element.45), channel_id=1, source_target_pairs={{0,0},{1,2},{2,1},{3,3},{4,4},{5,6},{6,5},{7,7},{8,8},{9,10},{10,9... | collective-permute-start | bytes 73736 | tf_op jit(solution)/shard_map/ppermute | solution.py:510
  73.4 3.9 %stencil_two.1 = (f32[3,8,32,256]{3,2,1,0:T(8,128)}, f32[4,128]{1,0:T(4,128)}) custom-call(f32[3,8,32,256]{3,2,1,0:T(8,128)} %get-tuple-element.41.w_ref.w1_ref, f32[8,32,256]{2,1,0:T(8,128)} %sh_ref.5, f32[8,32,256]{2,1,0:T(8,128)} %la_ref.5, f32[8,32,256]{2,1,0:T(8,128)} %in_ref.3, f32[3,32,256]{2,1,0:T(8,128)} %copy-done.8, f32[3,32,256]{2,1,0:T(8,128)} %copy-done.9, ...), custom_call_target="tpu_custom_call" | custom-call | flops 300000000 | bytes 9000000 | tf_op jit(solution)/shard_map/stencil_two/pallas_call | solution.py:577
  78.0 4.4 %forces_two.1 = (f32[16,4,128]{2,1,0:T(4,128)}, f32[32,4,128]{2,1,0:T(4,128)}) custom-call(f32[8,8,4,128]{3,2,1,0:T(4,128)} %copy-done.3, bf16[64,128,256]{2,1,0:T(8,128)(2,1)} %get-tuple-element.36.w_ref, s32[64]{0:T(128)} %get-tuple-element.37.target_ref, f32[16,4,128]{2,1,0:T(4,128)} %get-tuple-element.48.move_ref, f32[4,128]{1,0:T(4,128)} %get-tuple-element.49.dots_ref), custom_call_target="tpu_custom_call" | custom-call | flops 200000000 | bytes 6000000 | tf_op jit(solution)/shard_map/forces_two/pallas_call | solution.py:580
  82.4 10.1 %all-to-all-start.3 = ((f32[32,4,128]{2,1,0:T(4,128)}), f32[32,4,128]{2,1,0:T(4,128)S(1)}, u32[]{:S(2)}, u32[]{:S(2)}) async-start(f32[32,4,128]{2,1,0:T(4,128)} %get-tuple-element.51), calls=%async_computation.3 | async-start | bytes 131072 | tf_op jit(solution)/shard_map/all_to_all | solution.py:585
  92.5 3.9 %scatter_two.1.w2_ref = f32[3,8,32,256]{3,2,1,0:T(8,128)} custom-call(f32[3,8,32,256]{3,2,1,0:T(8,128)} %get-tuple-element.46.e_ref, f32[16,4,128]{2,1,0:T(4,128)} %get-tuple-element.50.force_ref, s32[8,1,256]{2,1,0:T(1,128)} %bitcast.12), custom_call_target="tpu_custom_call" | custom-call | flops 300000000 | bytes 9000000 | tf_op jit(solution)/shard_map/scatter_two/pallas_call | solution.py:586
  96.4 3.5 %all-to-all-done.3.red_ref = f32[32,4,128]{2,1,0:T(4,128)S(1)} async-done(((f32[32,4,128]{2,1,0:T(4,128)}), f32[32,4,128]{2,1,0:T(4,128)S(1)}, u32[]{:S(2)}, u32[]{:S(2)}) %all-to-all-start.3) | async-done | bytes 65568 | tf_op jit(solution)/shard_map/all_to_all | solution.py:585
  100.5 3.1 %final.1 = (f32[3,8,32,256]{3,2,1,0:T(8,128)}, f32[3,8,32,256]{3,2,1,0:T(8,128)}) custom-call(f32[3,8,32,256]{3,2,1,0:T(8,128)} %r_ref.9, f32[3,8,32,256]{3,2,1,0:T(8,128)} %get-tuple-element.41.w_ref.w1_ref, f32[3,8,32,256]{3,2,1,0:T(8,128)} %scatter_two.1.w2_ref, f32[32,4,128]{2,1,0:T(4,128)} %copy-done.4), custom_call_target="tpu_custom_call" | custom-call | flops 100000000 | bytes 3000000 | tf_op jit(solution)/shard_map/final/pallas_call | solution.py:589
  (36 shorter events, 5.5 us)
Async XLA Ops:
  6.0 15.3 %all-to-all-start.1 = ((f32[8,12,4,128]{3,2,1,0:T(4,128)}), f32[8,12,4,128]{3,2,1,0:T(4,128)S(1)}, u32[]{:S(2)}, u32[]{:S(2)}) async-start(f32[8,12,4,128]{3,2,1,0:T(4,128)} %get-tuple-element.34), calls=%async_computation.1 | async-start | bytes 393216 | tf_op jit(solution)/shard_map/all_to_all | solution.py:551
  21.2 20.8 %copy-start.5 = (f32[8,12,4,128]{3,2,1,0:T(4,128)}, f32[8,12,4,128]{3,2,1,0:T(4,128)S(1)}, u32[]{:S(2)}) copy-start(f32[8,12,4,128]{3,2,1,0:T(4,128)S(1)} %all-to-all-done.1.got_ref) | copy-start | bytes 589828
  21.2 31.4 %all-to-all-start = ((f32[8,12,4,128]{3,2,1,0:T(4,128)}), f32[8,12,4,128]{3,2,1,0:T(4,128)S(1)}, u32[]{:S(2)}, u32[]{:S(2)}) async-start(f32[8,12,4,128]{3,2,1,0:T(4,128)} %get-tuple-element.33), calls=%async_computation | async-start | bytes 393216 | tf_op jit(solution)/shard_map/all_to_all | solution.py:556
  24.6 9.8 %collective-permute-start = (f32[5,32,256]{2,1,0:T(8,128)}, f32[5,32,256]{2,1,0:T(8,128)S(1)}, u32[]{:S(2)}, u32[]{:S(2)}) collective-permute-start(f32[5,32,256]{2,1,0:T(8,128)} %get-tuple-element.27), channel_id=1, source_target_pairs={{0,4},{4,0},{8,12},{12,8},{16,20},{20,16},{24,28},{28,24},{1,5},{5... | collective-permute-start | bytes 491528 | tf_op jit(solution)/shard_map/ppermute | solution.py:507
  26.6 7.9 %collective-permute-start.1 = (f32[5,32,256]{2,1,0:T(8,128)}, f32[5,32,256]{2,1,0:T(8,128)S(1)}, u32[]{:S(2)}, u32[]{:S(2)}) collective-permute-start(f32[5,32,256]{2,1,0:T(8,128)} %get-tuple-element.28), channel_id=1, source_target_pairs={{0,0},{4,8},{8,4},{12,16},{16,12},{20,24},{24,20},{28,28},{1,1},{5... | collective-permute-start | bytes 491528 | tf_op jit(solution)/shard_map/ppermute | solution.py:508
  28.1 1.4 %collective-permute-start.2 = (f32[5,8,256]{2,1,0:T(8,128)}, f32[5,8,256]{2,1,0:T(8,128)S(1)}, u32[]{:S(2)}, u32[]{:S(2)}) collective-permute-start(f32[5,8,256]{2,1,0:T(8,128)} %get-tuple-element.29), channel_id=1, source_target_pairs={{0,1},{1,0},{2,3},{3,2},{4,5},{5,4},{6,7},{7,6},{8,9},{9,8},{10,11... | collective-permute-start | bytes 122888 | tf_op jit(solution)/shard_map/ppermute | solution.py:509
  28.1 1.4 %collective-permute-start.3 = (f32[5,8,256]{2,1,0:T(8,128)}, f32[5,8,256]{2,1,0:T(8,128)S(1)}, u32[]{:S(2)}, u32[]{:S(2)}) collective-permute-start(f32[5,8,256]{2,1,0:T(8,128)} %get-tuple-element.30), channel_id=1, source_target_pairs={{0,0},{1,2},{2,1},{3,3},{4,4},{5,6},{6,5},{7,7},{8,8},{9,10},{10,9... | collective-permute-start | bytes 122888 | tf_op jit(solution)/shard_map/ppermute | solution.py:510
  29.5 4.9 %copy-start.6 = (f32[5,8,256]{2,1,0:T(8,128)}, f32[5,8,256]{2,1,0:T(8,128)S(1)}, u32[]{:S(2)}) copy-start(f32[5,8,256]{2,1,0:T(8,128)S(1)} %collective-permute-done.2.ye.cye) | copy-start | bytes 122884
  29.6 4.9 %copy-start.7 = (f32[5,8,256]{2,1,0:T(8,128)}, f32[5,8,256]{2,1,0:T(8,128)S(1)}, u32[]{:S(2)}) copy-start(f32[5,8,256]{2,1,0:T(8,128)S(1)} %collective-permute-done.3.yo.cyo) | copy-start | bytes 122884
  34.5 0.7 copy-start.1
  35.1 0.7 copy-start.2
  52.6 0.7 copy-start
  57.8 19.5 %all-to-all-start.2 = ((f32[8,8,4,128]{3,2,1,0:T(4,128)}), f32[8,8,4,128]{3,2,1,0:T(4,128)S(1)}, u32[]{:S(2)}, u32[]{:S(2)}) async-start(f32[8,8,4,128]{3,2,1,0:T(4,128)} %get-tuple-element.47), calls=%async_computation.2 | async-start | bytes 262144 | tf_op jit(solution)/shard_map/all_to_all | solution.py:571
  67.5 5.3 %collective-permute-start.4 = (f32[3,32,256]{2,1,0:T(8,128)}, f32[3,32,256]{2,1,0:T(8,128)S(1)}, u32[]{:S(2)}, u32[]{:S(2)}) collective-permute-start(f32[3,32,256]{2,1,0:T(8,128)} %get-tuple-element.42), channel_id=1, source_target_pairs={{0,4},{4,0},{8,12},{12,8},{16,20},{20,16},{24,28},{28,24},{1,5},{5... | collective-permute-start | bytes 294920 | tf_op jit(solution)/shard_map/ppermute | solution.py:507
  69.5 3.3 %collective-permute-start.5 = (f32[3,32,256]{2,1,0:T(8,128)}, f32[3,32,256]{2,1,0:T(8,128)S(1)}, u32[]{:S(2)}, u32[]{:S(2)}) collective-permute-start(f32[3,32,256]{2,1,0:T(8,128)} %get-tuple-element.43), channel_id=1, source_target_pairs={{0,0},{4,8},{8,4},{12,16},{16,12},{20,24},{24,20},{28,28},{1,1},{5... | collective-permute-start | bytes 294920 | tf_op jit(solution)/shard_map/ppermute | solution.py:508
  71.0 1.4 %collective-permute-start.6 = (f32[3,8,256]{2,1,0:T(8,128)}, f32[3,8,256]{2,1,0:T(8,128)S(1)}, u32[]{:S(2)}, u32[]{:S(2)}) collective-permute-start(f32[3,8,256]{2,1,0:T(8,128)} %get-tuple-element.44), channel_id=1, source_target_pairs={{0,1},{1,0},{2,3},{3,2},{4,5},{5,4},{6,7},{7,6},{8,9},{9,8},{10,11... | collective-permute-start | bytes 73736 | tf_op jit(solution)/shard_map/ppermute | solution.py:509
  71.0 1.4 %collective-permute-start.7 = (f32[3,8,256]{2,1,0:T(8,128)}, f32[3,8,256]{2,1,0:T(8,128)S(1)}, u32[]{:S(2)}, u32[]{:S(2)}) collective-permute-start(f32[3,8,256]{2,1,0:T(8,128)} %get-tuple-element.45), channel_id=1, source_target_pairs={{0,0},{1,2},{2,1},{3,3},{4,4},{5,6},{6,5},{7,7},{8,8},{9,10},{10,9... | collective-permute-start | bytes 73736 | tf_op jit(solution)/shard_map/ppermute | solution.py:510
  72.4 0.6 copy-start.10
  72.4 0.6 copy-start.11
  72.7 0.6 copy-start.8
  72.7 0.7 copy-start.9
  77.3 0.7 copy-start.3
  82.4 17.6 %all-to-all-start.3 = ((f32[32,4,128]{2,1,0:T(4,128)}), f32[32,4,128]{2,1,0:T(4,128)S(1)}, u32[]{:S(2)}, u32[]{:S(2)}) async-start(f32[32,4,128]{2,1,0:T(4,128)} %get-tuple-element.51), calls=%async_computation.3 | async-start | bytes 131072 | tf_op jit(solution)/shard_map/all_to_all | solution.py:585
  99.9 0.6 copy-start.4

commit v2 on v1

v2 whole, which is shorter than its diff:
```python
import jax
import jax.numpy as jnp
from jax import lax
from jax.experimental import pallas as pl
from jax.experimental.pallas import tpu as pltpu
from jax.sharding import PartitionSpec as P

F32 = jnp.float32
BF16 = jnp.bfloat16
I32 = jnp.int32

barrier_reach = 1.0
barrier_scale = 0.005
FAR = 1000.0

VMEM = pl.BlockSpec(memory_space=pltpu.VMEM)
SMEM = pl.BlockSpec(memory_space=pltpu.SMEM)
HBM = pl.BlockSpec(memory_space=pltpu.HBM)


def sds(shape, dtype=F32):
    return jax.ShapeDtypeStruct(shape, dtype)


def call(body, name, in_specs, out_specs, out_shape, scratch=(), cost=2.0, mib=8):
    estimate = pl.CostEstimate(flops=int(cost * 1e8), transcendentals=0, bytes_accessed=int(cost * 3e6))
    return pl.pallas_call(
        body,
        name=name,
        in_specs=in_specs,
        out_specs=out_specs,
        out_shape=out_shape,
        scratch_shapes=list(scratch),
        cost_estimate=estimate,
        compiler_params=pltpu.CompilerParams(vmem_limit_bytes=mib << 20),
    )


def in_hbm(*arrays):
    return tuple(pltpu.with_memory_space_constraint(array, pltpu.HBM) for array in arrays)


def split(values):
    high = values.astype(BF16)
    low = (values - high.astype(F32)).astype(BF16)
    return high, low


def even_faces(block, axis_parity, last):
    first = jnp.where(axis_parity == 0, last, 0)
    return first, last - first


def write_faces(sources, xe_ref, xo_ref, ye_ref, yo_ref):
    bpar = lax.rem(lax.axis_index("body"), 2)
    apar = lax.rem(lax.axis_index("across"), 2)
    for k, (ref, lead) in enumerate(sources):
        at = (lambda x: ref[lead, x]) if lead is not None else (lambda x: ref[x])
        rows = ref.shape[-3]
        cols = ref.shape[-2]
        xi = jnp.where(bpar == 0, rows - 1, 0)
        xe_ref[k] = at(xi)
        xo_ref[k] = at(rows - 1 - xi)
        for x in range(rows):
            slab = at(x)
            low = slab[0:1]
            high = slab[cols - 1 : cols]
            ye_ref[k, x : x + 1] = jnp.where(apar == 0, high, low)
            yo_ref[k, x : x + 1] = jnp.where(apar == 0, low, high)


def cell_parts(cells, depth):
    if depth & (depth - 1) == 0:
        shift = depth.bit_length() - 1
        return lax.shift_right_logical(cells, shift), jnp.bitwise_and(cells, depth - 1)
    row = cells // depth
    return row, cells - row * depth


def gather_into(load, rows, depth, map_ref, both_ref, write):
    for c in range(3):
        high, low = split(load(c))
        both_ref[c * rows : (c + 1) * rows, 0:depth] = high
        both_ref[c * rows : (c + 1) * rows, depth:] = low
    chunks, _, span = map_ref.shape
    depth_iota = lax.broadcasted_iota(I32, (depth, span), 0)
    row_iota = lax.broadcasted_iota(I32, (rows, span), 0)

    def chunk(j, carry):
        row, deep = cell_parts(map_ref[j], depth)
        onehot = jnp.where(depth_iota == deep, 1.0, 0.0).astype(BF16)
        onehot = jnp.concatenate([onehot, onehot], axis=0)
        picked = jnp.dot(both_ref[...], onehot, preferred_element_type=F32)
        here = row_iota == row
        for c in range(3):
            part = jnp.where(here, picked[c * rows : (c + 1) * rows], 0.0)
            write(j, c, jnp.sum(part, axis=0, keepdims=True))
        return carry

    lax.fori_loop(0, chunks, chunk, 0)


def open_kernel(
    r_hbm, sh_hbm, la_hbm, in_hbm, pt_hbm, cnt_hbm, pair_hbm, map_hbm,
    r_ref, sh_ref, la_ref, in_ref, map_ref,
    xe_ref, xo_ref, ye_ref, yo_ref, own_ref, move_ref, msg_ref, table_ref,
    pt_ref, cnt_ref, pair_ref, fill_ref, sent_ref, both_ref, sem,
):
    copies = [
        pltpu.make_async_copy(source, target, sem.at[k])
        for k, (source, target) in enumerate([
            (cnt_hbm, cnt_ref), (pair_hbm, pair_ref), (pt_hbm, pt_ref), (map_hbm, map_ref),
            (r_hbm.at[0], r_ref.at[0]), (r_hbm.at[1], r_ref.at[1]), (r_hbm.at[2], r_ref.at[2]),
            (sh_hbm, sh_ref), (la_hbm, la_ref), (in_hbm, in_ref),
        ])
    ]
    for copy in copies:
        copy.start()
    bodies, width = msg_ref.shape[0], msg_ref.shape[1]
    blocks = own_ref.shape[0]
    odd_total = blocks // 2
    cap = width - odd_total
    pairs = table_ref.shape[1]
    points = own_ref.shape[2]
    lane = lax.broadcasted_iota(I32, (1, points), 1)
    row = lax.broadcasted_iota(I32, (8, points), 0)
    for copy in copies[:4]:
        copy.wait()
    for d in range(bodies):
        fill_ref[d] = 0

    def place(n, carry):
        dest = pair_ref[1, 0, n]
        rank = fill_ref[dest]
        fill_ref[dest] = rank + 1
        table_ref[0, dest * cap + rank] = pair_ref[0, 0, n]
        table_ref[1, dest * cap + rank] = pair_ref[2, 0, n]
        return carry

    lax.fori_loop(0, pairs, place, 0)
    blank = jnp.zeros((1, points), F32)
    for k in range(blocks):
        tile = jnp.concatenate([pt_ref[c, k : k + 1, :] for c in range(3)] + [blank], axis=0)
        own_ref[k] = jnp.where(lane < cnt_ref[k], tile, -FAR)
        sent_ref[k, 4:8, :] = jnp.where(lane < cnt_ref[k], tile, FAR)
        sent_ref[k, 3:4, :] = blank + 1.0
        move_ref[k, 3:4, :] = blank + 1.0
    for copy in copies[4:]:
        copy.wait()
    rows, depth = r_ref.shape[1] * r_ref.shape[2], r_ref.shape[3]

    def write(j, c, line):
        per = line.shape[1] // points
        for b in range(per):
            part = line[:, b * points : (b + 1) * points]
            move_ref[j * per + b, c : c + 1, :] = part
            sent_ref[j * per + b, c : c + 1, :] = part

    gather_into(lambda c: r_ref[c].reshape(rows, depth), rows, depth, map_ref, both_ref, write)

    def pack(d, carry):
        for s in range(cap):
            second = table_ref[1, d * cap + s].astype(F32)
            msg_ref[d, s] = jnp.where(row == 7, second, sent_ref[table_ref[0, d * cap + s]])
        for j in range(odd_total):
            msg_ref[d, cap + j] = sent_ref[2 * j + 1]
        return carry

    lax.fori_loop(0, bodies, pack, 0)
    sources = [(r_ref, 0), (r_ref, 1), (r_ref, 2), (sh_ref, None), (la_ref, None)]
    write_faces(sources, xe_ref, xo_ref, ye_ref, yo_ref)


def weigh(tile, target):
    columns = jnp.transpose(tile)
    squared = None
    for c in range(3):
        gap = columns[:, 4 + c : 5 + c] - target[c : c + 1, :]
        squared = gap * gap if squared is None else squared + gap * gap
    q = 1.0 - 1.0 / squared
    weight = barrier_scale * (-2.0 * jnp.log(squared) - 4.0 * q + q * q)
    return jnp.where(squared < barrier_reach, weight, 0.0)


def pair_part(moves, weights):
    points = moves.shape[1]
    high = moves.astype(BF16).astype(F32)
    lhs = jnp.concatenate([high, moves - high], axis=0).astype(BF16)
    out = jnp.dot(lhs, weights, preferred_element_type=F32)
    return (out[0:4, :points] + out[4:8, :points]) + (out[0:4, points:] + out[4:8, points:])


def forces_one_kernel(
    got_ref, own_ref, table_ref, move_ref, next_ref,
    force_ref, sum_ref, msg_ref, target_ref, w_hbm, w_ref, acc_ref, sem,
):
    bodies, width = got_ref.shape[0], got_ref.shape[1]
    blocks, _, points = move_ref.shape
    cap = width - blocks // 2
    acc_ref[...] = jnp.zeros_like(acc_ref)

    def keep(d):
        return pltpu.make_async_copy(w_ref.at[d], w_hbm.at[d], sem.at[d])

    def device(d, carry):
        work = []
        for s in range(cap):
            n = d * cap + s
            tile = got_ref[d, s]
            at = jnp.max(tile[7:8]).astype(I32)
            target_ref[n] = at
            work.append((tile, at))
            first = table_ref[0, n]
            odd = lax.shift_right_logical(table_ref[1, n], 1)
            work.append((got_ref[d, cap + odd], first))
        parts = []
        for k, (tile, at) in enumerate(work):
            high, low = split(weigh(tile, own_ref[at]))
            both = jnp.concatenate([high, low], axis=1)
            w_ref[d, k] = both
            parts.append(pair_part(tile[0:4], both))
        for (_, at), part in zip(work, parts):
            acc_ref[at] = acc_ref[at] + part
        keep(d).start()
        return carry

    lax.fori_loop(0, bodies, device, 0)
    row = lax.broadcasted_iota(I32, (4, points), 0)
    inner = jnp.zeros((4, points), F32)
    for k in range(blocks):
        acc = acc_ref[k]
        force = move_ref[k] * acc[3:4] - acc
        force_ref[k] = force
        sum_ref[k] = jnp.where(row < 3, next_ref[k] + force, 1.0)
        inner = inner + move_ref[k] * force
    inner = jnp.sum(inner[0:3], axis=0, keepdims=True)
    sum_ref[blocks] = next_ref[blocks] + jnp.where(row == 1, inner, 0.0)

    def pack(d, carry):
        for s in range(cap):
            n = d * cap + s
            msg_ref[d, s] = sum_ref[table_ref[0, n]]
            msg_ref[d, cap + s] = sum_ref[target_ref[n]]
        return carry

    lax.fori_loop(0, bodies, pack, 0)

    def finish(d, carry):
        keep(d).wait()
        return carry

    lax.fori_loop(0, bodies, finish, 0)


def scatter_sum(base, rows, depth, map_ref, force_ref, left_ref, right_ref):
    span = map_ref.shape[2]
    per = force_ref.shape[0] // map_ref.shape[0]
    depth_iota = lax.broadcasted_iota(I32, (depth, span), 0)
    row_iota = lax.broadcasted_iota(I32, (rows, span), 0)
    chunks = map_ref.shape[0]
    for j in range(chunks):
        row, deep = cell_parts(map_ref[j], depth)
        onehot = jnp.where(depth_iota == deep, 1.0, 0.0).astype(BF16)
        right_ref[:, j * span : (j + 1) * span] = onehot
        right_ref[:, (chunks + j) * span : (chunks + j + 1) * span] = onehot
        here = row_iota == row
        for c in range(3):
            line = jnp.concatenate(
                [force_ref[j * per + b, c : c + 1, :] for b in range(per)], axis=1
            )
            high = line.astype(BF16).astype(F32)
            at = slice(c * rows, (c + 1) * rows)
            left_ref[at, j * span : (j + 1) * span] = jnp.where(here, high, 0.0).astype(BF16)
            left_ref[at, (chunks + j) * span : (chunks + j + 1) * span] = jnp.where(
                here, line - high, 0.0
            ).astype(BF16)
    spread = lax.dot_general(
        left_ref[...], right_ref[...], (((1,), (1,)), ((), ())), preferred_element_type=F32
    )
    return [base(c) + spread[c * rows : (c + 1) * rows] for c in range(3)]


def scatter_one_kernel(
    e_ref, force_ref, map_ref, w1_ref, xe_ref, xo_ref, ye_ref, yo_ref, left_ref, right_ref
):
    shape = e_ref.shape[1:]
    rows, depth = shape[0] * shape[1], shape[2]
    sums = scatter_sum(
        lambda c: e_ref[c].reshape(rows, depth), rows, depth, map_ref, force_ref, left_ref, right_ref
    )
    for c in range(3):
        w1_ref[c] = sums[c].reshape(shape)
    write_faces([(w1_ref, 0), (w1_ref, 1), (w1_ref, 2)], xe_ref, xo_ref, ye_ref, yo_ref)


def scatter_two_kernel(
    e_ref, force_ref, map_ref, r_hbm, w2_ref, r_ref, left_ref, right_ref, sem
):
    copy = pltpu.make_async_copy(r_hbm, r_ref, sem)
    copy.start()
    shape = e_ref.shape[1:]
    rows, depth = shape[0] * shape[1], shape[2]
    sums = scatter_sum(
        lambda c: e_ref[c].reshape(rows, depth), rows, depth, map_ref, force_ref, left_ref, right_ref
    )
    for c in range(3):
        w2_ref[c] = sums[c].reshape(shape)
    copy.wait()


def elastic(v_ref, sh_ref, la_ref, in_ref, vector_halo, stiff_halo, emit):
    rows, cols, depth = sh_ref.shape
    b, a = lax.axis_index("body"), lax.axis_index("across")
    bodies, acrosses = lax.axis_size("body"), lax.axis_size("across")
    bpar, apar = lax.rem(b, 2), lax.rem(a, 2)
    cut = bodies // 4
    x_low = jnp.where(b != 0, 1.0, 0.0).astype(F32)
    x_high = jnp.where(b != bodies - 1, 1.0, 0.0).astype(F32)
    keep_low = jnp.where(b != cut, 1.0, 0.0).astype(F32)
    keep_high = jnp.where(b + 1 != cut, 1.0, 0.0).astype(F32)
    y_low = jnp.where(a != 0, 1.0, 0.0).astype(F32)
    y_high = jnp.where(a != acrosses - 1, 1.0, 0.0).astype(F32)
    vxe, vxo, vye, vyo = vector_halo
    sxe, sxo, sye, syo = stiff_halo
    row = lax.broadcasted_iota(I32, (cols, depth), 0)
    lane = lax.broadcasted_iota(I32, (cols, depth), 1)
    z_mask = jnp.where(lane == depth - 1, 0.0, 1.0)
    start = lane == 0
    top = row == cols - 1
    bottom = row == 0

    def stiffness(shear, lame):
        return 0.5 * shear, shear + 0.5 * lame

    def pick(parity, even, odd):
        return jnp.where(parity == 0, even, odd)

    def x_halo(high):
        e, o = (sxe, sxo) if high else (sxo, sxe)
        there = x_high if high else x_low
        shear, lame = pick(bpar, e[3], o[3]), pick(bpar, e[4], o[4])
        e, o = (vxe, vxo) if high else (vxo, vxe)
        values = [there * pick(bpar, e[c], o[c]) for c in range(3)]
        return stiffness(there * shear, there * lame), values

    def y_halo(high, x):
        e, o = (sye, syo) if high else (syo, sye)
        there = y_high if high else y_low
        at = slice(x, x + 1)
        shear, lame = pick(apar, e[3, at], o[3, at]), pick(apar, e[4, at], o[4, at])
        e, o = (vye, vyo) if high else (vyo, vye)
        values = [there * pick(apar, e[c, at], o[c, at]) for c in range(3)]
        return stiffness(there * shear, there * lame), values

    def slab(x):
        return stiffness(sh_ref[x], la_ref[x]), [v_ref[c, x] for c in range(3)]

    def flux(near, far, along, mask):
        (off, diag), values = near
        (far_off, far_diag), far_values = far
        side, front = off + far_off, diag + far_diag
        if mask is not None:
            side, front = side * mask, front * mask
        return [
            (front if c == along else side) * (values[c] - far_values[c]) for c in range(3)
        ]

    before = flux(x_halo(False), slab(0), 0, keep_low)
    here = slab(0)
    for x in range(rows):
        after = slab(x + 1) if x + 1 < rows else x_halo(True)
        out = flux(here, after, 0, None if x + 1 < rows else keep_high)
        (off, diag), values = here
        inertia = in_ref[x]
        total = [inertia * values[c] + (out[c] - before[c]) for c in range(3)]
        before = out

        def up(value, edge):
            return jnp.where(top, edge, pltpu.roll(value, cols - 1, 0))

        (h_off, h_diag), h_values = y_halo(True, x)
        shifted = (up(off, h_off), up(diag, h_diag)), [up(values[c], h_values[c]) for c in range(3)]
        out = flux(here, shifted, 1, None)
        first = (off[0:1], diag[0:1]), [values[c][0:1] for c in range(3)]
        edge = flux(y_halo(False, x), first, 1, None)
        total = [
            total[c] + (out[c] - jnp.where(bottom, edge[c], pltpu.roll(out[c], 1, 0)))
            for c in range(3)
        ]

        def right(value):
            return z_mask * pltpu.roll(value, depth - 1, 1)

        shifted = (right(off), right(diag)), [right(values[c]) for c in range(3)]
        out = flux(here, shifted, 2, None)
        edge = [-(diag if c == 2 else off) * values[c] for c in range(3)]
        total = [
            total[c] + (out[c] - jnp.where(start, edge[c], pltpu.roll(out[c], 1, 1)))
            for c in range(3)
        ]
        emit(x, total)
        here = after


def stencil_one_kernel(
    r_ref, sh_ref, la_ref, in_ref, xe, xo, ye, yo, map_ref, e_ref, next_ref, both_ref
):
    sums = [jnp.zeros((8, 128), F32) for _ in range(2)]

    def emit(x, total):
        for c in range(3):
            e_ref[c, x] = total[c]
            r = r_ref[c, x]
            sums[0] = sums[0] + fold(r * r)
            sums[1] = sums[1] + fold(r * total[c])

    elastic(r_ref, sh_ref, la_ref, in_ref, (xe, xo, ye, yo), (xe, xo, ye, yo), emit)
    rows, depth = e_ref.shape[1] * e_ref.shape[2], e_ref.shape[3]
    points = next_ref.shape[2]

    def write(j, c, line):
        per = line.shape[1] // points
        for b in range(per):
            next_ref[j * per + b, c : c + 1, :] = line[:, b * points : (b + 1) * points]

    blocks = next_ref.shape[0] - 1
    for k in range(blocks):
        next_ref[k, 3:4, :] = jnp.zeros((1, points), F32)
    lines = [jnp.sum(value, axis=0, keepdims=True) for value in sums]
    next_ref[blocks] = jnp.concatenate(lines + [jnp.zeros((2, points), F32)], axis=0)
    gather_into(lambda c: e_ref[c].reshape(rows, depth), rows, depth, map_ref, both_ref, write)


def fold(value):
    cols, depth = value.shape
    total = None
    for k in range(depth // 128):
        part = value[:, k * 128 : (k + 1) * 128]
        part = jnp.sum(part.reshape(cols // 8, 8, 128), axis=0)
        total = part if total is None else total + part
    return total


def apply_two_kernel(
    w1_ref, sh_ref, la_ref, in_ref, xe, xo, ye, yo, cxe, cxo, cye, cyo,
    got_ref, target_ref, table_ref, move_ref, w_hbm,
    e_ref, force_ref, red_ref, w_ref, acc_ref, sem,
):
    bodies, width = got_ref.shape[0], got_ref.shape[1]
    cap = width // 2
    blocks, points = move_ref.shape[0] - 1, move_ref.shape[2]

    def fetch(d):
        return pltpu.make_async_copy(w_hbm.at[d], w_ref.at[d], sem.at[d])

    def begin(d, carry):
        fetch(d).start()
        return carry

    lax.fori_loop(0, bodies, begin, 0)
    sums = [jnp.zeros((8, 128), F32) for _ in range(2)]

    def emit(x, total):
        for c in range(3):
            e_ref[c, x] = total[c]
            w = w1_ref[c, x]
            sums[0] = sums[0] + fold(w * w)
            sums[1] = sums[1] + fold(w * total[c])

    elastic(w1_ref, sh_ref, la_ref, in_ref, (xe, xo, ye, yo), (cxe, cxo, cye, cyo), emit)
    acc_ref[...] = jnp.zeros_like(acc_ref)

    def device(d, carry):
        fetch(d).wait()
        work = []
        for s in range(cap):
            n = d * cap + s
            work.append((target_ref[n], pair_part(got_ref[d, s], w_ref[d, 2 * s])))
            work.append((table_ref[0, n], pair_part(got_ref[d, cap + s], w_ref[d, 2 * s + 1])))
        for at, part in work:
            acc_ref[at] = acc_ref[at] + part
        return carry

    lax.fori_loop(0, bodies, device, 0)
    inner = jnp.zeros((4, points), F32)
    for k in range(blocks):
        acc = acc_ref[k]
        moved = move_ref[k]
        force = moved * acc[3:4] - acc
        force_ref[k] = force
        inner = inner + moved * force
    lines = [jnp.sum(value, axis=0, keepdims=True) for value in sums]
    lines[1] = lines[1] + jnp.sum(inner[0:3], axis=0, keepdims=True)
    line = jnp.concatenate([move_ref[blocks][0:2]] + lines, axis=0)
    for d in range(red_ref.shape[0]):
        red_ref[d] = line


def final_kernel(r_ref, w1_ref, w2_ref, red_ref, x_hbm, res_hbm, x_ref, res_ref, sem):
    line = jnp.sum(red_ref[...], axis=0)
    moment = [
        jnp.broadcast_to(jnp.sum(line[k : k + 1], axis=1, keepdims=True), (8, 128)) for k in range(4)
    ]
    m0, m1, m2, m3 = moment
    step = m0 / m1
    norm = (m0 - step * m1) + step * (step * m2 - m1)
    ratio = norm / m0
    grown = 1.0 + ratio
    curve = grown * (grown * m1 - 2.0 * step * m2) + step * step * m3
    next_step = norm / curve
    alpha = step + next_step * grown
    gamma = next_step * step
    cols, depth = r_ref.shape[2], r_ref.shape[3]
    alpha = jnp.broadcast_to(alpha[0:1, 0:1], (cols, depth))
    gamma = jnp.broadcast_to(gamma[0:1, 0:1], (cols, depth))
    copies = []
    for c in range(3):
        for x in range(r_ref.shape[1]):
            r, w1 = r_ref[c, x], w1_ref[c, x]
            x_ref[c, x] = alpha * r - gamma * w1
            res_ref[c, x] = r - alpha * w1 + gamma * w2_ref[c, x]
        copies.append(pltpu.make_async_copy(x_ref.at[c], x_hbm.at[c], sem.at[0, c]))
        copies.append(pltpu.make_async_copy(res_ref.at[c], res_hbm.at[c], sem.at[1, c]))
        for copy in copies[-2:]:
            copy.start()
    for copy in copies:
        copy.wait()


def exchange(xe, xo, ye, yo):
    def pairs(axis, start):
        count = lax.axis_size(axis)
        chosen = []
        for i in range(count):
            partner = i + 1 if (i - start) % 2 == 0 else i - 1
            chosen.append((i, partner if 0 <= partner < count else i))
        return chosen

    return (
        lax.ppermute(xe, "body", pairs("body", 0)),
        lax.ppermute(xo, "body", pairs("body", 1)),
        lax.ppermute(ye, "across", pairs("across", 0)),
        lax.ppermute(yo, "across", pairs("across", 1)),
    )


def on_device(
    cotangent, shear, lame, inertia, surface_points, point_counts, surface_maps, contact_pairs
):
    rows, cols, depth = shear.shape
    points = jnp.transpose(surface_points[0, 0], (1, 0, 2))
    counts = point_counts[0, 0]
    cell_maps = surface_maps[0, 0]
    pair_table = contact_pairs[0, 0][:, None, :]
    _, blocks, width = points.shape
    pairs = pair_table.shape[2]
    bodies, acrosses = lax.axis_size("body"), lax.axis_size("across")
    devices = bodies * acrosses
    cap = pairs // bodies
    slots = cap + blocks // 2
    chunks = blocks // 2
    cell_maps = cell_maps.reshape(chunks, 1, 2 * width)
    flat = rows * cols
    vector = sds((3, rows, cols, depth))

    def faces(count):
        return (
            sds((count, cols, depth)), sds((count, cols, depth)),
            sds((count, rows, depth)), sds((count, rows, depth)),
        )

    moves = sds((blocks, 4, width))
    both = pltpu.VMEM((3 * flat, 2 * depth), BF16)
    wide = 2 * blocks * width
    sides = (pltpu.VMEM((3 * flat, wide), BF16), pltpu.VMEM((depth, wide), BF16))
    total = pltpu.VMEM((blocks, 4, width), F32)
    kept = (bodies, 2 * cap, width, 2 * width)
    kept_mib = 10 + (8 * pairs * width * width >> 20) + (bodies >> 2)
    dma = pltpu.SemaphoreType.DMA
    cells = (sds((rows, cols, depth)),) * 3

    r, shear, lame, inertia, cell_maps, xe, xo, ye, yo, own, first_moves, message, table = call(
        open_kernel, "open", [HBM] * 8, [VMEM] * 12 + [SMEM],
        (vector,) + cells + (sds(cell_maps.shape, I32),) + faces(5)
        + (moves, moves, sds((bodies, slots, 8, width)), sds((2, pairs), I32)),
        scratch=(
            pltpu.VMEM(points.shape, F32), pltpu.SMEM(counts.shape, I32),
            pltpu.SMEM(pair_table.shape, I32), pltpu.SMEM((bodies,), I32),
            pltpu.VMEM((blocks, 8, width), F32), both, dma((10,)),
        ), cost=4.0,
    )(*in_hbm(cotangent, shear, lame, inertia, points, counts, pair_table, cell_maps))
    got = lax.all_to_all(message, "body", 0, 0, tiled=True)
    halo = exchange(xe, xo, ye, yo)
    grown = sds((blocks + 1, 4, width))
    elastic_one, next_moves = call(
        stencil_one_kernel, "stencil_one", [VMEM] * 9, [VMEM] * 2, (vector, grown),
        scratch=(both,), cost=5.0,
    )(r, shear, lame, inertia, *halo, cell_maps)
    force_one, second_moves, message, targets, weights = call(
        forces_one_kernel, "forces_one", [VMEM] * 2 + [SMEM] + [VMEM] * 2,
        [VMEM] * 3 + [SMEM, HBM],
        (moves, grown, sds((bodies, 2 * cap, 4, width)), sds((pairs,), I32), pltpu.HBM(kept, BF16)),
        scratch=(pltpu.VMEM(kept, BF16), total, dma((bodies,))), cost=6.0, mib=kept_mib,
    )(got, own, table, first_moves, next_moves)
    got = lax.all_to_all(message, "body", 0, 0, tiled=True)
    w1, xe, xo, ye, yo = call(
        scatter_one_kernel, "scatter_one", [VMEM] * 3, [VMEM] * 5, (vector,) + faces(3),
        scratch=sides, cost=3.0, mib=16,
    )(elastic_one, force_one, cell_maps)
    halo_two = exchange(xe, xo, ye, yo)
    elastic_two, force_two, partial = call(
        apply_two_kernel, "apply_two", [VMEM] * 13 + [SMEM] * 2 + [VMEM, HBM], [VMEM] * 3,
        (vector, moves, sds((devices, 4, 128))),
        scratch=(pltpu.VMEM(kept, BF16), total, dma((bodies,))), cost=2.0, mib=kept_mib,
    )(w1, shear, lame, inertia, *halo_two, *halo, got, targets, table, second_moves, *in_hbm(weights))
    sums = lax.all_to_all(partial, ("body", "across"), 0, 0, tiled=True)
    w2, r = call(
        scatter_two_kernel, "scatter_two", [VMEM] * 3 + [HBM], [VMEM] * 2, (vector, vector),
        scratch=sides + (dma(()),), cost=3.0, mib=16,
    )(elastic_two, force_two, cell_maps, *in_hbm(cotangent))
    out = pltpu.VMEM((3, rows, cols, depth), F32)
    return call(
        final_kernel, "final", [VMEM] * 4, [HBM] * 2, (vector, vector),
        scratch=(out, out, dma((2, 3))), cost=1.0,
    )(r, w1, w2, sums)


def solution(mesh):
    placed = (
        P(None, "body", "across", None),
        P("body", "across", None),
        P("body", "across", None),
        P("body", "across", None),
        P("body", "across", None, None, None),
        P("body", "across", None),
        P("body", "across", None, None),
        P("body", "across", None, None),
    )
    return jax.shard_map(
        on_device,
        mesh=mesh,
        in_specs=placed,
        out_specs=(P(None, "body", "across", None), P(None, "body", "across", None)),
        check_vma=False,
    )
```

time: 105 us -> 78.3 us (0.75)
  Pallas kernels: 48.3 us -> 28.8 us
  starting transfers between devices: 36.4 us -> 30.7 us
  local copies, waits for them, and re-layouts: 6.57 us -> 2 us
  waiting for transfers between devices: 11.6 us -> 15.5 us
    pallas_call x8 -> x5, Pallas kernels: 38.1 us -> 22.7 us  [the longest x1 9.9 us: on_device(): call(forces_one_kernel, 'forces_one', [VMEM] * 2 + [SMEM] + [VMEM] * 2, [...]
    unnamed x26 -> x4, local copies, waits for them, and re-layouts: 6.57 us -> 2 us
    ppermute x2, waiting for transfers between devices: 5.19 us -> 8.88 us  [exchange(): lax.ppermute(xe, 'body', pairs('body', 0))]
    all_to_all x3 -> x2, starting transfers between devices: 16.4 us -> 13.4 us  [on_device(): got = lax.all_to_all(message, 'body', 0, 0, tiled=True)]
    all_to_all x3 -> x2, waiting for transfers between devices: 2.89 us -> 0.01 us  [on_device(): got = lax.all_to_all(message, 'body', 0, 0, tiled=True)]
    pallas_call x1, Pallas kernels: 3.93 us -> 1.84 us  [on_device(): call(scatter_one_kernel, 'scatter_one', [VMEM] * 3, [VMEM] * 5, (vector,)...]
    all_to_all x1, waiting for transfers between devices: 3.54 us -> 5.56 us  [on_device(): sums = lax.all_to_all(partial, ('body', 'across'), 0, 0, tiled=True)]
    pallas_call x1, Pallas kernels: 6.21 us -> 4.23 us  [on_device(): call(stencil_one_kernel, 'stencil_one', [VMEM] * 9, [VMEM] * 2, (vector,...]
  transfers between devices with their start and end apart: 12 -> 11, of which waited for: 4 -> 5; matrix products, arithmetic and copies ran while one was open for 0% -> 0% of each run, Pallas kernels for 32% -> 10%
where the time goes in v2:
time: 78.3 us; the launch traced here: 77.8 us
  starting transfers between devices  30.7 us (39%)
  Pallas kernels  28.8 us (37%)
  waiting for transfers between devices  15.5 us (20%)
  local copies, waits for them, and re-layouts  2 us (3%)
    all_to_all x2, starting transfers between devices, on_device(): got = lax.all_to_all(message, 'body', 0, 0, tiled=True)  13.4 us
    all_to_all x1, starting transfers between devices, on_device(): sums = lax.all_to_all(partial, ('body', 'across'), 0, 0, tiled=True)  10.4 us
    pallas_call x1, Pallas kernels, on_device(): call(forces_one_kernel, 'forces_one', [VMEM] * 2 + [SMEM] + [VMEM] * 2, [...  9.9 us
    ppermute x2, waiting for transfers between devices, exchange(): lax.ppermute(xe, 'body', pairs('body', 0))  8.88 us
    pallas_call x1, Pallas kernels, on_device(): call(open_kernel, 'open', [HBM] * 8, [VMEM] * 12 + [SMEM], (vector,) + ce...  5.56 us
    all_to_all x1, waiting for transfers between devices, on_device(): sums = lax.all_to_all(partial, ('body', 'across'), 0, 0, tiled=True)  5.56 us
    pallas_call x1, Pallas kernels, on_device(): call(stencil_one_kernel, 'stencil_one', [VMEM] * 9, [VMEM] * 2, (vector,...  4.23 us
    ppermute x2, starting transfers between devices, exchange(): lax.ppermute(xe, 'body', pairs('body', 0))  4.09 us
  transfers between devices with their start and end apart: 11, of which 5 were waited for; matrix products, arithmetic and copies ran while one was open for 0% of the time, Pallas kernels for 10%

profile of v2, /device:TPU:0, one launch (start us, length us, event | category | flops | bytes accessed | tf_op | source)
XLA Modules:
  0.0 77.8 jit_solution(4592556667445457649)
XLA Ops:
  0.6 5.6 %open.1 = (f32[3,8,32,256]{3,2,1,0:T(8,128)S(1)}, f32[8,32,256]{2,1,0:T(8,128)S(1)}, f32[8,32,256]{2,1,0:T(8,128)S(1)}, f32[8,32,256]{2,1,0:T(8,128)S(1)}, s32[8...) custom-call(f32[3,8,32,256]{3,2,1,0:T(8,128)} %r_hbm.3, ...), custom_call_target="tpu_custom_call" | custom-call | flops 400000000 | bytes 12000000 | tf_op jit(solution)/shard_map/open/pallas_call | solution.py:582
  6.2 7.3 %all-to-all-start = ((f32[8,12,8,128]{3,2,1,0:T(8,128)}), f32[8,12,8,128]{3,2,1,0:T(8,128)S(1)}, u32[]{:S(2)}, u32[]{:S(2)}) async-start(f32[8,12,8,128]{3,2,1,0:T(8,128)} %get-tuple-element.42), calls=%async_computation | async-start | bytes 786432 | tf_op jit(solution)/shard_map/all_to_all | solution.py:592
  13.5 2.0 %collective-permute-start = (f32[5,32,256]{2,1,0:T(8,128)S(1)}, f32[5,32,256]{2,1,0:T(8,128)S(1)}, u32[]{:S(2)}, u32[]{:S(2)}) collective-permute-start(f32[5,32,256]{2,1,0:T(8,128)S(1)} %get-tuple-element.36), channel_id=1, source_target_pairs={{0,4},{4,0},{8,12},{12,8},{16,20},{20,16},{24,28},{28,24},{1,5},{5... | collective-permute-start | bytes 491528 | tf_op jit(solution)/shard_map/ppermute | solution.py:540
  15.5 0.7 collective-permute-start.1
  16.3 0.7 collective-permute-start.3
  17.0 0.5 collective-permute-done.2.ye.cye
  17.5 8.0 %collective-permute-done.xe.cxe = f32[5,32,256]{2,1,0:T(8,128)S(1)} collective-permute-done((f32[5,32,256]{2,1,0:T(8,128)S(1)}, f32[5,32,256]{2,1,0:T(8,128)S(1)}, u32[]{:S(2)}, u32[]{:S(2)}) %collective-permute-start) | collective-permute-done | bytes 163872 | tf_op jit(solution)/shard_map/ppermute | solution.py:540
  25.5 4.2 %stencil_one.1 = (f32[3,8,32,256]{3,2,1,0:T(8,128)S(1)}, f32[17,4,128]{2,1,0:T(4,128)S(1)}) custom-call(f32[3,8,32,256]{3,2,1,0:T(8,128)S(1)} %get-tuple-element.32.r_ref, f32[8,32,256]{2,1,0:T(8,128)S(1)} %get-tuple-element.33.sh_ref, f32[8,32,256]{2,1,0:T(8,128)S(1)} %get-tuple-element.34.la_ref, f32[8,32,256]{2,1,0:T(8,128)S(1)} %get-tuple-element.35.in_ref, ...), custom_call_target="tpu_custom_call" | custom-call | flops 500000000 | bytes 15000000 | tf_op jit(solution)/shard_map/stencil_one/pallas_call | solution.py:595
  29.8 0.9 %copy-done = f32[3,8,32,256]{3,2,1,0:T(8,128)} copy-done((f32[3,8,32,256]{3,2,1,0:T(8,128)}, f32[3,8,32,256]{3,2,1,0:T(8,128)S(1)}, u32[]{:S(2)}) %copy-start) | copy-done | bytes 786456
  30.7 9.9 %forces_one.1 = (f32[16,4,128]{2,1,0:T(4,128)S(1)}, f32[17,4,128]{2,1,0:T(4,128)S(1)}, f32[8,8,4,128]{3,2,1,0:T(4,128)}, s32[32]{0:T(128)S(1)}, bf16[8,8,128,256]{3,2,1,0:T(8,128)(2,1)}) custom-call(f32[8,12,8,128]{3,2,1,0:T(8,128)S(1)} %all-to-all-done.got_ref, f32[16,4,128]{2,1,0:T(4,128)S(1)} %get-tuple-element.43.own_ref, ...), custom_call_target="tpu_custom_call" | custom-call | flops 600000000 | bytes 18000000 | tf_op jit(solution)/shard_map/forces_one/pallas_call | solution.py:599
  40.6 6.1 %all-to-all-start.1 = ((f32[8,8,4,128]{3,2,1,0:T(4,128)}), f32[8,8,4,128]{3,2,1,0:T(4,128)S(1)}, u32[]{:S(2)}, u32[]{:S(2)}) async-start(f32[8,8,4,128]{3,2,1,0:T(4,128)} %get-tuple-element.53), calls=%async_computation.1 | async-start | bytes 262144 | tf_op jit(solution)/shard_map/all_to_all | solution.py:605
  46.7 1.1 %copy-done.1 = f32[3,8,32,256]{3,2,1,0:T(8,128)S(1)} copy-done((f32[3,8,32,256]{3,2,1,0:T(8,128)S(1)}, f32[3,8,32,256]{3,2,1,0:T(8,128)}, u32[]{:S(2)}) %copy-start.1) | copy-done | bytes 786456
  47.8 1.8 %scatter_one.1 = (f32[3,8,32,256]{3,2,1,0:T(8,128)S(1)}, f32[3,32,256]{2,1,0:T(8,128)S(1)}, f32[3,32,256]{2,1,0:T(8,128)S(1)}, f32[3,8,256]{2,1,0:T(8,128)S(1)}, f32[3,8,256]{2,1,0:T(8,128)S(1)}) custom-call(f32[3,8,32,256]{3,2,1,0:T(8,128)S(1)} %copy-done.1, f32[16,4,128]{2,1,0:T(4,128)S(1)} %get-tuple-element.47.force_ref, ...), custom_call_target="tpu_custom_call" | custom-call | flops 300000000 | bytes 9000000 | tf_op jit(solution)/shard_map/scatter_one/pallas_call | solution.py:606
  49.7 2.1 %collective-permute-start.4 = (f32[3,32,256]{2,1,0:T(8,128)S(1)}, f32[3,32,256]{2,1,0:T(8,128)S(1)}, u32[]{:S(2)}, u32[]{:S(2)}) collective-permute-start(f32[3,32,256]{2,1,0:T(8,128)S(1)} %get-tuple-element.49), channel_id=1, source_target_pairs={{0,4},{4,0},{8,12},{12,8},{16,20},{20,16},{24,28},{28,24},{1,5},{5... | collective-permute-start | bytes 294920 | tf_op jit(solution)/shard_map/ppermute | solution.py:540
  51.7 0.7 collective-permute-start.5
  52.4 0.1 collective-permute-start.6
  52.5 0.7 collective-permute-start.7
  53.1 0.5 collective-permute-done.6.ye
  53.7 0.9 %collective-permute-done.4.xe = f32[3,32,256]{2,1,0:T(8,128)S(1)} collective-permute-done((f32[3,32,256]{2,1,0:T(8,128)S(1)}, f32[3,32,256]{2,1,0:T(8,128)S(1)}, u32[]{:S(2)}, u32[]{:S(2)}) %collective-permute-start.4) | collective-permute-done | bytes 98336 | tf_op jit(solution)/shard_map/ppermute | solution.py:540
  54.5 4.0 %apply_two.1 = (f32[3,8,32,256]{3,2,1,0:T(8,128)S(1)}, f32[16,4,128]{2,1,0:T(4,128)S(1)}, f32[32,4,128]{2,1,0:T(4,128)}) custom-call(f32[3,8,32,256]{3,2,1,0:T(8,128)S(1)} %get-tuple-element.48.w1_ref, f32[8,32,256]{2,1,0:T(8,128)S(1)} %get-tuple-element.33.sh_ref, f32[8,32,256]{2,1,0:T(8,128)S(1)} %get-tuple-element.34.la_ref, ...), custom_call_target="tpu_custom_call" | custom-call | flops 200000000 | bytes 6000000 | tf_op jit(solution)/shard_map/apply_two/pallas_call | solution.py:611
  58.6 10.4 %all-to-all-start.2 = ((f32[32,4,128]{2,1,0:T(4,128)}), f32[32,4,128]{2,1,0:T(4,128)S(1)}, u32[]{:S(2)}, u32[]{:S(2)}) async-start(f32[32,4,128]{2,1,0:T(4,128)} %get-tuple-element.61), calls=%async_computation.2 | async-start | bytes 131072 | tf_op jit(solution)/shard_map/all_to_all | solution.py:616
  69.0 1.8 %scatter_two.1 = (f32[3,8,32,256]{3,2,1,0:T(8,128)S(1)}, f32[3,8,32,256]{3,2,1,0:T(8,128)S(1)}) custom-call(f32[3,8,32,256]{3,2,1,0:T(8,128)S(1)} %get-tuple-element.57.e_ref, f32[16,4,128]{2,1,0:T(4,128)S(1)} %get-tuple-element.58.force_ref, s32[8,1,256]{2,1,0:T(1,128)S(1)} %get-tuple-element.40.map_ref, f32[3,8,32,256]{3,2,1,0:T(8,128)} %r_hbm.3), custom_call_target="tpu_custom_call" | custom-call | flops 300000000 | bytes 9000000 | tf_op jit(solution)/shard_map/scatter_two/pallas_call | solution.py:617
  70.8 5.6 %all-to-all-done.2.red_ref = f32[32,4,128]{2,1,0:T(4,128)S(1)} async-done(((f32[32,4,128]{2,1,0:T(4,128)}), f32[32,4,128]{2,1,0:T(4,128)S(1)}, u32[]{:S(2)}, u32[]{:S(2)}) %all-to-all-start.2) | async-done | bytes 65568 | tf_op jit(solution)/shard_map/all_to_all | solution.py:616
  76.4 1.4 %final.1 = (f32[3,8,32,256]{3,2,1,0:T(8,128)}, f32[3,8,32,256]{3,2,1,0:T(8,128)}) custom-call(f32[3,8,32,256]{3,2,1,0:T(8,128)S(1)} %get-tuple-element.59.r_ref, f32[3,8,32,256]{3,2,1,0:T(8,128)S(1)} %get-tuple-element.48.w1_ref, f32[3,8,32,256]{3,2,1,0:T(8,128)S(1)} %get-tuple-element.60.w2_ref, f32[32,4,128]{2,1,0:T(4,128)S(1)} %all-to-all-done.2.red_ref), custom_call_target="tpu_custom_call" | custom-call | flops 100000000 | bytes 3000000 | tf_op jit(solution)/shard_map/final/pallas_call | solution.py:622
  (9 shorter events, 0.1 us)
Async XLA Ops:
  6.2 24.5 %all-to-all-start = ((f32[8,12,8,128]{3,2,1,0:T(8,128)}), f32[8,12,8,128]{3,2,1,0:T(8,128)S(1)}, u32[]{:S(2)}, u32[]{:S(2)}) async-start(f32[8,12,8,128]{3,2,1,0:T(8,128)} %get-tuple-element.42), calls=%async_computation | async-start | bytes 786432 | tf_op jit(solution)/shard_map/all_to_all | solution.py:592
  13.5 12.0 %collective-permute-start = (f32[5,32,256]{2,1,0:T(8,128)S(1)}, f32[5,32,256]{2,1,0:T(8,128)S(1)}, u32[]{:S(2)}, u32[]{:S(2)}) collective-permute-start(f32[5,32,256]{2,1,0:T(8,128)S(1)} %get-tuple-element.36), channel_id=1, source_target_pairs={{0,4},{4,0},{8,12},{12,8},{16,20},{20,16},{24,28},{28,24},{1,5},{5... | collective-permute-start | bytes 491528 | tf_op jit(solution)/shard_map/ppermute | solution.py:540
  15.5 10.0 %collective-permute-start.1 = (f32[5,32,256]{2,1,0:T(8,128)S(1)}, f32[5,32,256]{2,1,0:T(8,128)S(1)}, u32[]{:S(2)}, u32[]{:S(2)}) collective-permute-start(f32[5,32,256]{2,1,0:T(8,128)S(1)} %get-tuple-element.37), channel_id=1, source_target_pairs={{0,0},{4,8},{8,4},{12,16},{16,12},{20,24},{24,20},{28,28},{1,1},{5... | collective-permute-start | bytes 491528 | tf_op jit(solution)/shard_map/ppermute | solution.py:541
  16.2 1.3 %collective-permute-start.2 = (f32[5,8,256]{2,1,0:T(8,128)S(1)}, f32[5,8,256]{2,1,0:T(8,128)S(1)}, u32[]{:S(2)}, u32[]{:S(2)}) collective-permute-start(f32[5,8,256]{2,1,0:T(8,128)S(1)} %get-tuple-element.38), channel_id=1, source_target_pairs={{0,1},{1,0},{2,3},{3,2},{4,5},{5,4},{6,7},{7,6},{8,9},{9,8},{10,11... | collective-permute-start | bytes 122888 | tf_op jit(solution)/shard_map/ppermute | solution.py:542
  16.3 1.2 %collective-permute-start.3 = (f32[5,8,256]{2,1,0:T(8,128)S(1)}, f32[5,8,256]{2,1,0:T(8,128)S(1)}, u32[]{:S(2)}, u32[]{:S(2)}) collective-permute-start(f32[5,8,256]{2,1,0:T(8,128)S(1)} %get-tuple-element.39), channel_id=1, source_target_pairs={{0,0},{1,2},{2,1},{3,3},{4,4},{5,6},{6,5},{7,7},{8,8},{9,10},{10,9... | collective-permute-start | bytes 122888 | tf_op jit(solution)/shard_map/ppermute | solution.py:543
  29.8 0.9 %copy-start = (f32[3,8,32,256]{3,2,1,0:T(8,128)}, f32[3,8,32,256]{3,2,1,0:T(8,128)S(1)}, u32[]{:S(2)}) copy-start(f32[3,8,32,256]{3,2,1,0:T(8,128)S(1)} %get-tuple-element.41.e_ref) | copy-start | bytes 2359300
  40.6 13.9 %all-to-all-start.1 = ((f32[8,8,4,128]{3,2,1,0:T(4,128)}), f32[8,8,4,128]{3,2,1,0:T(4,128)S(1)}, u32[]{:S(2)}, u32[]{:S(2)}) async-start(f32[8,8,4,128]{3,2,1,0:T(4,128)} %get-tuple-element.53), calls=%async_computation.1 | async-start | bytes 262144 | tf_op jit(solution)/shard_map/all_to_all | solution.py:605
  46.7 1.1 %copy-start.1 = (f32[3,8,32,256]{3,2,1,0:T(8,128)S(1)}, f32[3,8,32,256]{3,2,1,0:T(8,128)}, u32[]{:S(2)}) copy-start(f32[3,8,32,256]{3,2,1,0:T(8,128)} %copy-done) | copy-start | bytes 2359300
  49.7 4.9 %collective-permute-start.4 = (f32[3,32,256]{2,1,0:T(8,128)S(1)}, f32[3,32,256]{2,1,0:T(8,128)S(1)}, u32[]{:S(2)}, u32[]{:S(2)}) collective-permute-start(f32[3,32,256]{2,1,0:T(8,128)S(1)} %get-tuple-element.49), channel_id=1, source_target_pairs={{0,4},{4,0},{8,12},{12,8},{16,20},{20,16},{24,28},{28,24},{1,5},{5... | collective-permute-start | bytes 294920 | tf_op jit(solution)/shard_map/ppermute | solution.py:540
  51.7 2.8 %collective-permute-start.5 = (f32[3,32,256]{2,1,0:T(8,128)S(1)}, f32[3,32,256]{2,1,0:T(8,128)S(1)}, u32[]{:S(2)}, u32[]{:S(2)}) collective-permute-start(f32[3,32,256]{2,1,0:T(8,128)S(1)} %get-tuple-element.50), channel_id=1, source_target_pairs={{0,0},{4,8},{8,4},{12,16},{16,12},{20,24},{24,20},{28,28},{1,1},{5... | collective-permute-start | bytes 294920 | tf_op jit(solution)/shard_map/ppermute | solution.py:541
  52.4 1.3 %collective-permute-start.6 = (f32[3,8,256]{2,1,0:T(8,128)S(1)}, f32[3,8,256]{2,1,0:T(8,128)S(1)}, u32[]{:S(2)}, u32[]{:S(2)}) collective-permute-start(f32[3,8,256]{2,1,0:T(8,128)S(1)} %get-tuple-element.51), channel_id=1, source_target_pairs={{0,1},{1,0},{2,3},{3,2},{4,5},{5,4},{6,7},{7,6},{8,9},{9,8},{10,11... | collective-permute-start | bytes 73736 | tf_op jit(solution)/shard_map/ppermute | solution.py:542
  52.5 1.2 %collective-permute-start.7 = (f32[3,8,256]{2,1,0:T(8,128)S(1)}, f32[3,8,256]{2,1,0:T(8,128)S(1)}, u32[]{:S(2)}, u32[]{:S(2)}) collective-permute-start(f32[3,8,256]{2,1,0:T(8,128)S(1)} %get-tuple-element.52), channel_id=1, source_target_pairs={{0,0},{1,2},{2,1},{3,3},{4,4},{5,6},{6,5},{7,7},{8,8},{9,10},{10,9... | collective-permute-start | bytes 73736 | tf_op jit(solution)/shard_map/ppermute | solution.py:543
  58.6 17.8 %all-to-all-start.2 = ((f32[32,4,128]{2,1,0:T(4,128)}), f32[32,4,128]{2,1,0:T(4,128)S(1)}, u32[]{:S(2)}, u32[]{:S(2)}) async-start(f32[32,4,128]{2,1,0:T(4,128)} %get-tuple-element.61), calls=%async_computation.2 | async-start | bytes 131072 | tf_op jit(solution)/shard_map/all_to_all | solution.py:616

commit v3 on v2

--- a/solution.py
+++ b/solution.py
@@ -124,6 +124,7 @@
     points = own_ref.shape[2]
     lane = lax.broadcasted_iota(I32, (1, points), 1)
     row = lax.broadcasted_iota(I32, (8, points), 0)
+    edge = lax.broadcasted_iota(I32, (4, points), 0) == 3
     for copy in copies[:4]:
         copy.wait()
     for d in range(bodies):
@@ -141,9 +142,9 @@
     blank = jnp.zeros((1, points), F32)
     for k in range(blocks):
         tile = jnp.concatenate([pt_ref[c, k : k + 1, :] for c in range(3)] + [blank], axis=0)
-        own_ref[k] = jnp.where(lane < cnt_ref[k], tile, -FAR)
-        sent_ref[k, 4:8, :] = jnp.where(lane < cnt_ref[k], tile, FAR)
-        sent_ref[k, 3:4, :] = blank + 1.0
+        own_ref[k] = target_rows(measured(jnp.where(lane < cnt_ref[k], tile, -FAR), edge))
+        sent_ref[k, 4:8, :] = measured(jnp.where(lane < cnt_ref[k], tile, FAR), edge)
+        sent_ref[k, 3:4, :] = blank
         move_ref[k, 3:4, :] = blank + 1.0
     for copy in copies[4:]:
         copy.wait()
@@ -161,7 +162,7 @@
     def pack(d, carry):
         for s in range(cap):
             second = table_ref[1, d * cap + s].astype(F32)
-            msg_ref[d, s] = jnp.where(row == 7, second, sent_ref[table_ref[0, d * cap + s]])
+            msg_ref[d, s] = jnp.where(row == 3, second, sent_ref[table_ref[0, d * cap + s]])
         for j in range(odd_total):
             msg_ref[d, cap + j] = sent_ref[2 * j + 1]
         return carry
@@ -171,12 +172,45 @@
     write_faces(sources, xe_ref, xo_ref, ye_ref, yo_ref)
 
 
+def measured(tile, edge):
+    square = jnp.where(edge, 0.0, tile * tile)
+    return jnp.where(edge, jnp.sum(square, axis=0, keepdims=True), tile)
+
+
+def three_parts(value):
+    high = value.astype(BF16).astype(F32)
+    rest = value - high
+    middle = rest.astype(BF16).astype(F32)
+    return high, middle, rest - middle
+
+
+def source_rows(tile):
+    row = lax.broadcasted_iota(I32, (8, tile.shape[1]), 0)
+    high, middle, low = three_parts(jnp.concatenate([tile, tile], axis=0))
+    first = jnp.where(row == 7, middle, high)
+    second = jnp.where(row == 3, low, jnp.where(row < 3, middle, high))
+    second = jnp.where(row == 7, 1.0, second)
+    third = jnp.where(row < 3, low, middle)
+    third = jnp.where((row == 3) | (row == 7), 1.0, third)
+    return jnp.concatenate([first, second, third, jnp.zeros_like(first)], axis=0).astype(BF16)
+
+
+def target_rows(tile):
+    row = lax.broadcasted_iota(I32, (8, tile.shape[1]), 0)
+    high, middle, low = three_parts(jnp.concatenate([tile, tile], axis=0))
+    first = -2.0 * jnp.where(row < 4, high, middle)
+    first = jnp.where((row == 3) | (row == 7), 1.0, first)
+    second = -2.0 * jnp.where(row < 4, high, low)
+    second = jnp.where(row == 3, 1.0, jnp.where(row == 7, high, second))
+    third = -2.0 * jnp.where(row < 4, high, middle)
+    third = jnp.where(row == 3, middle, jnp.where(row == 7, low, third))
+    return jnp.concatenate([first, second, third, jnp.zeros_like(first)], axis=0).astype(BF16)
+
+
 def weigh(tile, target):
-    columns = jnp.transpose(tile)
-    squared = None
-    for c in range(3):
-        gap = columns[:, 4 + c : 5 + c] - target[c : c + 1, :]
-        squared = gap * gap if squared is None else squared + gap * gap
+    squared = lax.dot_general(
+        source_rows(tile[4:8]), target, (((0,), (0,)), ((), ())), preferred_element_type=F32
+    )
     q = 1.0 - 1.0 / squared
     weight = barrier_scale * (-2.0 * jnp.log(squared) - 4.0 * q + q * q)
     return jnp.where(squared < barrier_reach, weight, 0.0)
@@ -199,17 +233,23 @@
     cap = width - blocks // 2
     acc_ref[...] = jnp.zeros_like(acc_ref)
 
+    edge = lax.broadcasted_iota(I32, (4, points), 0) == 3
+
     def keep(d):
         return pltpu.make_async_copy(w_ref.at[d], w_hbm.at[d], sem.at[d])
+
+    def find(d, carry):
+        for s in range(cap):
+            target_ref[d * cap + s] = jnp.max(got_ref[d, s, 3:4, :]).astype(I32)
+        return carry
+
+    lax.fori_loop(0, bodies, find, 0, unroll=8)
 
     def device(d, carry):
         work = []
         for s in range(cap):
             n = d * cap + s
-            tile = got_ref[d, s]
-            at = jnp.max(tile[7:8]).astype(I32)
-            target_ref[n] = at
-            work.append((tile, at))
+            work.append((got_ref[d, s], target_ref[n]))
             first = table_ref[0, n]
             odd = lax.shift_right_logical(table_ref[1, n], 1)
             work.append((got_ref[d, cap + odd], first))
@@ -218,7 +258,7 @@
             high, low = split(weigh(tile, own_ref[at]))
             both = jnp.concatenate([high, low], axis=1)
             w_ref[d, k] = both
-            parts.append(pair_part(tile[0:4], both))
+            parts.append(pair_part(jnp.where(edge, 1.0, tile[0:4]), both))
         for (_, at), part in zip(work, parts):
             acc_ref[at] = acc_ref[at] + part
         keep(d).start()
@@ -281,13 +321,19 @@
 
 
 def scatter_one_kernel(
-    e_ref, force_ref, map_ref, w1_ref, xe_ref, xo_ref, ye_ref, yo_ref, left_ref, right_ref
+    e_hbm, force_ref, map_ref, w1_ref, xe_ref, xo_ref, ye_ref, yo_ref, e_ref, left_ref, right_ref, sem
 ):
+    copy = pltpu.make_async_copy(e_hbm, e_ref, sem)
+    copy.start()
     shape = e_ref.shape[1:]
     rows, depth = shape[0] * shape[1], shape[2]
-    sums = scatter_sum(
-        lambda c: e_ref[c].reshape(rows, depth), rows, depth, map_ref, force_ref, left_ref, right_ref
-    )
+
+    def base(c):
+        if c == 0:
+            copy.wait()
+        return e_ref[c].reshape(rows, depth)
+
+    sums = scatter_sum(base, rows, depth, map_ref, force_ref, left_ref, right_ref)
     for c in range(3):
         w1_ref[c] = sums[c].reshape(shape)
     write_faces([(w1_ref, 0), (w1_ref, 1), (w1_ref, 2)], xe_ref, xo_ref, ye_ref, yo_ref)
@@ -403,7 +449,8 @@
 
 
 def stencil_one_kernel(
-    r_ref, sh_ref, la_ref, in_ref, xe, xo, ye, yo, map_ref, e_ref, next_ref, both_ref
+    r_ref, sh_ref, la_ref, in_ref, xe, xo, ye, yo, map_ref,
+    e_hbm, next_ref, e_ref, both_ref, sem,
 ):
     sums = [jnp.zeros((8, 128), F32) for _ in range(2)]
 
@@ -415,6 +462,8 @@
             sums[1] = sums[1] + fold(r * total[c])
 
     elastic(r_ref, sh_ref, la_ref, in_ref, (xe, xo, ye, yo), (xe, xo, ye, yo), emit)
+    copy = pltpu.make_async_copy(e_ref, e_hbm, sem)
+    copy.start()
     rows, depth = e_ref.shape[1] * e_ref.shape[2], e_ref.shape[3]
     points = next_ref.shape[2]
 
@@ -429,6 +478,7 @@
     lines = [jnp.sum(value, axis=0, keepdims=True) for value in sums]
     next_ref[blocks] = jnp.concatenate(lines + [jnp.zeros((2, points), F32)], axis=0)
     gather_into(lambda c: e_ref[c].reshape(rows, depth), rows, depth, map_ref, both_ref, write)
+    copy.wait()
 
 
 def fold(value):
@@ -441,10 +491,8 @@
     return total
 
 
-def apply_two_kernel(
-    w1_ref, sh_ref, la_ref, in_ref, xe, xo, ye, yo, cxe, cxo, cye, cyo,
-    got_ref, target_ref, table_ref, move_ref, w_hbm,
-    e_ref, force_ref, red_ref, w_ref, acc_ref, sem,
+def forces_two_kernel(
+    got_ref, target_ref, table_ref, move_ref, w_hbm, force_ref, dots_ref, w_ref, acc_ref, sem
 ):
     bodies, width = got_ref.shape[0], got_ref.shape[1]
     cap = width // 2
@@ -458,16 +506,6 @@
         return carry
 
     lax.fori_loop(0, bodies, begin, 0)
-    sums = [jnp.zeros((8, 128), F32) for _ in range(2)]
-
-    def emit(x, total):
-        for c in range(3):
-            e_ref[c, x] = total[c]
-            w = w1_ref[c, x]
-            sums[0] = sums[0] + fold(w * w)
-            sums[1] = sums[1] + fold(w * total[c])
-
-    elastic(w1_ref, sh_ref, la_ref, in_ref, (xe, xo, ye, yo), (cxe, cxo, cye, cyo), emit)
     acc_ref[...] = jnp.zeros_like(acc_ref)
 
     def device(d, carry):
@@ -489,9 +527,27 @@
         force = moved * acc[3:4] - acc
         force_ref[k] = force
         inner = inner + moved * force
+    inner = jnp.sum(inner[0:3], axis=0, keepdims=True)
+    blank = jnp.zeros_like(inner)
+    dots_ref[...] = jnp.concatenate([move_ref[blocks][0:2], blank, inner], axis=0)
+
+
+def stencil_two_kernel(
+    w1_ref, sh_ref, la_ref, in_ref, xe, xo, ye, yo, cxe, cxo, cye, cyo, dots_ref, e_ref, red_ref
+):
+    sums = [jnp.zeros((8, 128), F32) for _ in range(2)]
+
+    def emit(x, total):
+        for c in range(3):
+            e_ref[c, x] = total[c]
+            w = w1_ref[c, x]
+            sums[0] = sums[0] + fold(w * w)
+            sums[1] = sums[1] + fold(w * total[c])
+
+    elastic(w1_ref, sh_ref, la_ref, in_ref, (xe, xo, ye, yo), (cxe, cxo, cye, cyo), emit)
     lines = [jnp.sum(value, axis=0, keepdims=True) for value in sums]
-    lines[1] = lines[1] + jnp.sum(inner[0:3], axis=0, keepdims=True)
-    line = jnp.concatenate([move_ref[blocks][0:2]] + lines, axis=0)
+    blank = jnp.zeros_like(lines[0])
+    line = dots_ref[...] + jnp.concatenate([blank, blank] + lines, axis=0)
     for d in range(red_ref.shape[0]):
         red_ref[d] = line
 
@@ -533,14 +589,15 @@
         chosen = []
         for i in range(count):
             partner = i + 1 if (i - start) % 2 == 0 else i - 1
-            chosen.append((i, partner if 0 <= partner < count else i))
+            chosen.append((i, partner % count))
         return chosen
 
+    got_xo = lax.ppermute(xo, "body", pairs("body", 1))
+    got_xe = lax.ppermute(xe, "body", pairs("body", 0))
+    got_yo = lax.ppermute(yo, "across", pairs("across", 1))
+    got_ye = lax.ppermute(ye, "across", pairs("across", 0))
     return (
-        lax.ppermute(xe, "body", pairs("body", 0)),
-        lax.ppermute(xo, "body", pairs("body", 1)),
-        lax.ppermute(ye, "across", pairs("across", 0)),
-        lax.ppermute(yo, "across", pairs("across", 1)),
+        got_xe, got_xo, got_ye, got_yo
     )
 
 
@@ -582,7 +639,8 @@
     r, shear, lame, inertia, cell_maps, xe, xo, ye, yo, own, first_moves, message, table = call(
         open_kernel, "open", [HBM] * 8, [VMEM] * 12 + [SMEM],
         (vector,) + cells + (sds(cell_maps.shape, I32),) + faces(5)
-        + (moves, moves, sds((bodies, slots, 8, width)), sds((2, pairs), I32)),
+        + (sds((blocks, 32, width), BF16), moves)
+        + (sds((bodies, slots, 8, width)), sds((2, pairs), I32)),
         scratch=(
             pltpu.VMEM(points.shape, F32), pltpu.SMEM(counts.shape, I32),
             pltpu.SMEM(pair_table.shape, I32), pltpu.SMEM((bodies,), I32),
@@ -593,8 +651,9 @@
     halo = exchange(xe, xo, ye, yo)
     grown = sds((blocks + 1, 4, width))
     elastic_one, next_moves = call(
-        stencil_one_kernel, "stencil_one", [VMEM] * 9, [VMEM] * 2, (vector, grown),
-        scratch=(both,), cost=5.0,
+        stencil_one_kernel, "stencil_one", [VMEM] * 9, [HBM, VMEM],
+        (pltpu.HBM((3, rows, cols, depth), F32), grown),
+        scratch=(pltpu.VMEM((3, rows, cols, depth), F32), both, dma(())), cost=5.0,
     )(r, shear, lame, inertia, *halo, cell_maps)
     force_one, second_moves, message, targets, weights = call(
         forces_one_kernel, "forces_one", [VMEM] * 2 + [SMEM] + [VMEM] * 2,
@@ -604,15 +663,19 @@
     )(got, own, table, first_moves, next_moves)
     got = lax.all_to_all(message, "body", 0, 0, tiled=True)
     w1, xe, xo, ye, yo = call(
-        scatter_one_kernel, "scatter_one", [VMEM] * 3, [VMEM] * 5, (vector,) + faces(3),
-        scratch=sides, cost=3.0, mib=16,
-    )(elastic_one, force_one, cell_maps)
+        scatter_one_kernel, "scatter_one", [HBM] + [VMEM] * 2, [VMEM] * 5, (vector,) + faces(3),
+        scratch=(pltpu.VMEM((3, rows, cols, depth), F32),) + sides + (dma(()),), cost=3.0, mib=16,
+    )(*in_hbm(elastic_one), force_one, cell_maps)
     halo_two = exchange(xe, xo, ye, yo)
-    elastic_two, force_two, partial = call(
-        apply_two_kernel, "apply_two", [VMEM] * 13 + [SMEM] * 2 + [VMEM, HBM], [VMEM] * 3,
-        (vector, moves, sds((devices, 4, 128))),
-        scratch=(pltpu.VMEM(kept, BF16), total, dma((bodies,))), cost=2.0, mib=kept_mib,
-    )(w1, shear, lame, inertia, *halo_two, *halo, got, targets, table, second_moves, *in_hbm(weights))
+    force_two, dots = call(
+        forces_two_kernel, "forces_two", [VMEM] + [SMEM] * 2 + [VMEM, HBM], [VMEM] * 2,
+        (moves, sds((4, 128))),
+        scratch=(pltpu.VMEM(kept, BF16), total, dma((bodies,))), cost=3.0, mib=kept_mib,
+    )(got, targets, table, second_moves, *in_hbm(weights))
+    elastic_two, partial = call(
+        stencil_two_kernel, "stencil_two", [VMEM] * 13, [VMEM] * 2, (vector, sds((devices, 4, 128))),
+        cost=1.5,
+    )(w1, shear, lame, inertia, *halo_two, *halo, dots)
     sums = lax.all_to_all(partial, ("body", "across"), 0, 0, tiled=True)
     w2, r = call(
         scatter_two_kernel, "scatter_two", [VMEM] * 3 + [HBM], [VMEM] * 2, (vector, vector),

time: 78.3 us -> 70.9 us (0.905)
  starting transfers between devices: 30.7 us -> 28.2 us
  local copies, waits for them, and re-layouts: 2 us -> 0 us
  waiting for transfers between devices: 15.5 us -> 13.6 us
  Pallas kernels: 28.8 us -> 28 us
    ppermute x8, starting transfers between devices: 6.88 us -> 13.8 us  [the longest x2 6.55 us: exchange(): got_xo = lax.ppermute(xo, 'body', pairs('body', 1))]
    all_to_all x1, starting transfers between devices: 10.4 us -> 3.72 us  [on_device(): sums = lax.all_to_all(partial, ('body', 'across'), 0, 0, tiled=True)]
    pallas_call x1, Pallas kernels: 9.9 us -> 7.08 us  [on_device(): call(forces_one_kernel, 'forces_one', [VMEM] * 2 + [SMEM] + [VMEM] * 2, [...]
    all_to_all x2, starting transfers between devices: 13.4 us -> 10.7 us  [on_device(): got = lax.all_to_all(message, 'body', 0, 0, tiled=True)]
    pallas_call x3 -> x4, Pallas kernels: 10.1 us -> 12.2 us  [the longest x1 4.24 us: on_device(): call(stencil_one_kernel, 'stencil_one', [VMEM] * 9, [HBM, VMEM], (pltpu.H...]
    unnamed x4 -> x0, local copies, waits for them, and re-layouts: 2 us -> none
    ppermute x8, waiting for transfers between devices: 9.94 us -> 8.01 us  [the longest x2 3.29 us: exchange(): got_xe = lax.ppermute(xe, 'body', pairs('body', 0))]
  transfers between devices with their start and end apart: 11 -> 11, of which waited for: 5 -> 4; matrix products, arithmetic and copies ran while one was open for 0% -> 0% of each run, Pallas kernels for 10% -> 17%
where the time goes in v3:
time: 70.9 us; the launch traced here: 70.5 us
  starting transfers between devices  28.2 us (40%)
  Pallas kernels  28 us (39%)
  waiting for transfers between devices  13.6 us (19%)
  between operations  0.74 us (1%)
    all_to_all x2, starting transfers between devices, on_device(): got = lax.all_to_all(message, 'body', 0, 0, tiled=True)  10.7 us
    pallas_call x1, Pallas kernels, on_device(): call(forces_one_kernel, 'forces_one', [VMEM] * 2 + [SMEM] + [VMEM] * 2, [...  7.08 us
    ppermute x2, starting transfers between devices, exchange(): got_xo = lax.ppermute(xo, 'body', pairs('body', 1))  6.55 us
    pallas_call x1, Pallas kernels, on_device(): call(open_kernel, 'open', [HBM] * 8, [VMEM] * 12 + [SMEM], (vector,) + ce...  5.56 us
    all_to_all x1, waiting for transfers between devices, on_device(): sums = lax.all_to_all(partial, ('body', 'across'), 0, 0, tiled=True)  5.56 us
    pallas_call x1, Pallas kernels, on_device(): call(stencil_one_kernel, 'stencil_one', [VMEM] * 9, [HBM, VMEM], (pltpu.H...  4.24 us
    ppermute x2, starting transfers between devices, exchange(): got_xe = lax.ppermute(xe, 'body', pairs('body', 0))  4.01 us
    all_to_all x1, starting transfers between devices, on_device(): sums = lax.all_to_all(partial, ('body', 'across'), 0, 0, tiled=True)  3.72 us
  transfers between devices with their start and end apart: 11, of which 4 were waited for; matrix products, arithmetic and copies ran while one was open for 0% of the time, Pallas kernels for 17%

profile of v3, /device:TPU:0, one launch (start us, length us, event | category | flops | bytes accessed | tf_op | source)
XLA Modules:
  0.0 70.5 jit_solution(11411256484584266118)
XLA Ops:
  0.6 5.6 %open.1 = (f32[3,8,32,256]{3,2,1,0:T(8,128)S(1)}, f32[8,32,256]{2,1,0:T(8,128)S(1)}, f32[8,32,256]{2,1,0:T(8,128)S(1)}, f32[8,32,256]{2,1,0:T(8,128)S(1)}, s32[8...) custom-call(f32[3,8,32,256]{3,2,1,0:T(8,128)} %r_hbm.3, ...), custom_call_target="tpu_custom_call" | custom-call | flops 400000000 | bytes 12000000 | tf_op jit(solution)/shard_map/open/pallas_call | solution.py:639
  6.2 7.3 %all-to-all-start = ((f32[8,12,8,128]{3,2,1,0:T(8,128)}), f32[8,12,8,128]{3,2,1,0:T(8,128)S(1)}, u32[]{:S(2)}, u32[]{:S(2)}) async-start(f32[8,12,8,128]{3,2,1,0:T(8,128)} %get-tuple-element.43), calls=%async_computation | async-start | bytes 786432 | tf_op jit(solution)/shard_map/all_to_all | solution.py:650
  13.5 2.0 %collective-permute-start = (f32[5,32,256]{2,1,0:T(8,128)S(1)}, f32[5,32,256]{2,1,0:T(8,128)S(1)}, u32[]{:S(2)}, u32[]{:S(2)}) collective-permute-start(f32[5,32,256]{2,1,0:T(8,128)S(1)} %get-tuple-element.37), channel_id=1, source_target_pairs={{0,4},{4,0},{8,12},{12,8},{16,20},{20,16},{24,28},{28,24},{1,5},{5... | collective-permute-start | bytes 491528 | tf_op jit(solution)/shard_map/ppermute | solution.py:596
  15.5 3.3 %collective-permute-start.1 = (f32[5,32,256]{2,1,0:T(8,128)S(1)}, f32[5,32,256]{2,1,0:T(8,128)S(1)}, u32[]{:S(2)}, u32[]{:S(2)}) collective-permute-start(f32[5,32,256]{2,1,0:T(8,128)S(1)} %get-tuple-element.38), channel_id=1, source_target_pairs={{0,28},{4,8},{8,4},{12,16},{16,12},{20,24},{24,20},{28,0},{1,29},{... | collective-permute-start | bytes 491528 | tf_op jit(solution)/shard_map/ppermute | solution.py:595
  18.8 0.0 collective-permute-start.2
  18.8 1.6 %collective-permute-start.3 = (f32[5,8,256]{2,1,0:T(8,128)S(1)}, f32[5,8,256]{2,1,0:T(8,128)S(1)}, u32[]{:S(2)}, u32[]{:S(2)}) collective-permute-start(f32[5,8,256]{2,1,0:T(8,128)S(1)} %get-tuple-element.40), channel_id=1, source_target_pairs={{0,3},{1,2},{2,1},{3,0},{4,7},{5,6},{6,5},{7,4},{8,11},{9,10},{10,... | collective-permute-start | bytes 122888 | tf_op jit(solution)/shard_map/ppermute | solution.py:597
  20.4 0.0 collective-permute-done.2.ye.cye
  20.4 1.8 %collective-permute-done.3.yo.cyo = f32[5,8,256]{2,1,0:T(8,128)S(1)} collective-permute-done((f32[5,8,256]{2,1,0:T(8,128)S(1)}, f32[5,8,256]{2,1,0:T(8,128)S(1)}, u32[]{:S(2)}, u32[]{:S(2)}) %collective-permute-start.3) | collective-permute-done | bytes 40992 | tf_op jit(solution)/shard_map/ppermute | solution.py:597
  22.2 3.3 %collective-permute-done.xe.cxe = f32[5,32,256]{2,1,0:T(8,128)S(1)} collective-permute-done((f32[5,32,256]{2,1,0:T(8,128)S(1)}, f32[5,32,256]{2,1,0:T(8,128)S(1)}, u32[]{:S(2)}, u32[]{:S(2)}) %collective-permute-start) | collective-permute-done | bytes 163872 | tf_op jit(solution)/shard_map/ppermute | solution.py:596
  25.5 2.9 %collective-permute-done.1.xo.cxo = f32[5,32,256]{2,1,0:T(8,128)S(1)} collective-permute-done((f32[5,32,256]{2,1,0:T(8,128)S(1)}, f32[5,32,256]{2,1,0:T(8,128)S(1)}, u32[]{:S(2)}, u32[]{:S(2)}) %collective-permute-start.1) | collective-permute-done | bytes 163872 | tf_op jit(solution)/shard_map/ppermute | solution.py:595
  28.4 4.2 %stencil_one.1 = (f32[3,8,32,256]{3,2,1,0:T(8,128)}, f32[17,4,128]{2,1,0:T(4,128)S(1)}) custom-call(f32[3,8,32,256]{3,2,1,0:T(8,128)S(1)} %get-tuple-element.33.r_ref, f32[8,32,256]{2,1,0:T(8,128)S(1)} %get-tuple-element.34.sh_ref, f32[8,32,256]{2,1,0:T(8,128)S(1)} %get-tuple-element.35.la_ref, f32[8,32,256]{2,1,0:T(8,128)S(1)} %get-tuple-element.36.in_ref, ...), custom_call_target="tpu_custom_call" | custom-call | flops 500000000 | bytes 15000000 | tf_op jit(solution)/shard_map/stencil_one/pallas_call | solution.py:653
  32.6 7.1 %forces_one.1 = (f32[16,4,128]{2,1,0:T(4,128)S(1)}, f32[17,4,128]{2,1,0:T(4,128)S(1)}, f32[8,8,4,128]{3,2,1,0:T(4,128)}, s32[32]{0:T(128)S(1)}, bf16[8,8,128,256]{3,2,1,0:T(8,128)(2,1)}) custom-call(f32[8,12,8,128]{3,2,1,0:T(8,128)S(1)} %all-to-all-done.got_ref, bf16[16,32,128]{2,1,0:T(8,128)(2,1)S(1)} %get-tuple-element.44.own_ref, ...), custom_call_target="tpu_custom_call" | custom-call | flops 600000000 | bytes 18000000 | tf_op jit(solution)/shard_map/forces_one/pallas_call | solution.py:658
  39.7 3.4 %all-to-all-start.1 = ((f32[8,8,4,128]{3,2,1,0:T(4,128)}), f32[8,8,4,128]{3,2,1,0:T(4,128)S(1)}, u32[]{:S(2)}, u32[]{:S(2)}) async-start(f32[8,8,4,128]{3,2,1,0:T(4,128)} %get-tuple-element.54), calls=%async_computation.1 | async-start | bytes 262144 | tf_op jit(solution)/shard_map/all_to_all | solution.py:664
  43.1 2.9 %scatter_one.1 = (f32[3,8,32,256]{3,2,1,0:T(8,128)S(1)}, f32[3,32,256]{2,1,0:T(8,128)S(1)}, f32[3,32,256]{2,1,0:T(8,128)S(1)}, f32[3,8,256]{2,1,0:T(8,128)S(1)}, f32[3,8,256]{2,1,0:T(8,128)S(1)}) custom-call(f32[3,8,32,256]{3,2,1,0:T(8,128)} %get-tuple-element.42.e_hbm, f32[16,4,128]{2,1,0:T(4,128)S(1)} %get-tuple-element.48.force_ref, ...), custom_call_target="tpu_custom_call" | custom-call | flops 300000000 | bytes 9000000 | tf_op jit(solution)/shard_map/scatter_one/pallas_call | solution.py:665
  46.0 2.0 %collective-permute-start.4 = (f32[3,32,256]{2,1,0:T(8,128)S(1)}, f32[3,32,256]{2,1,0:T(8,128)S(1)}, u32[]{:S(2)}, u32[]{:S(2)}) collective-permute-start(f32[3,32,256]{2,1,0:T(8,128)S(1)} %get-tuple-element.50), channel_id=1, source_target_pairs={{0,4},{4,0},{8,12},{12,8},{16,20},{20,16},{24,28},{28,24},{1,5},{5... | collective-permute-start | bytes 294920 | tf_op jit(solution)/shard_map/ppermute | solution.py:596
  48.0 3.3 %collective-permute-start.5 = (f32[3,32,256]{2,1,0:T(8,128)S(1)}, f32[3,32,256]{2,1,0:T(8,128)S(1)}, u32[]{:S(2)}, u32[]{:S(2)}) collective-permute-start(f32[3,32,256]{2,1,0:T(8,128)S(1)} %get-tuple-element.51), channel_id=1, source_target_pairs={{0,28},{4,8},{8,4},{12,16},{16,12},{20,24},{24,20},{28,0},{1,29},{... | collective-permute-start | bytes 294920 | tf_op jit(solution)/shard_map/ppermute | solution.py:595
  51.3 0.0 collective-permute-start.6
  51.3 1.6 %collective-permute-start.7 = (f32[3,8,256]{2,1,0:T(8,128)S(1)}, f32[3,8,256]{2,1,0:T(8,128)S(1)}, u32[]{:S(2)}, u32[]{:S(2)}) collective-permute-start(f32[3,8,256]{2,1,0:T(8,128)S(1)} %get-tuple-element.53), channel_id=1, source_target_pairs={{0,3},{1,2},{2,1},{3,0},{4,7},{5,6},{6,5},{7,4},{8,11},{9,10},{10,... | collective-permute-start | bytes 73736 | tf_op jit(solution)/shard_map/ppermute | solution.py:597
  52.9 3.2 %forces_two.1 = (f32[16,4,128]{2,1,0:T(4,128)S(1)}, f32[4,128]{1,0:T(4,128)S(1)}) custom-call(f32[8,8,4,128]{3,2,1,0:T(4,128)S(1)} %all-to-all-done.1.got_ref, s32[32]{0:T(128)S(1)} %get-tuple-element.55.target_ref, s32[2,32]{1,0:T(2,128)S(1)} %get-tuple-element.45.table_ref, f32[17,4,128]{2,1,0:T(4,128)S(1)} %get-tuple-element.56.move_ref, ...), custom_call_target="tpu_custom_call" | custom-call | flops 300000000 | bytes 9000000 | tf_op jit(solution)/shard_map/forces_two/pallas_call | solution.py:670
  56.2 1.8 %stencil_two.1 = (f32[3,8,32,256]{3,2,1,0:T(8,128)S(1)}, f32[32,4,128]{2,1,0:T(4,128)}) custom-call(f32[3,8,32,256]{3,2,1,0:T(8,128)S(1)} %get-tuple-element.49.w1_ref, f32[8,32,256]{2,1,0:T(8,128)S(1)} %get-tuple-element.34.sh_ref, f32[8,32,256]{2,1,0:T(8,128)S(1)} %get-tuple-element.35.la_ref, f32[8,32,256]{2,1,0:T(8,128)S(1)} %get-tuple-element.36.in_ref, ...), custom_call_target="tpu_custom_call" | custom-call | flops 150000000 | bytes 4500000 | tf_op jit(solution)/shard_map/stencil_two/pallas_call | solution.py:675
  58.0 3.7 %all-to-all-start.2 = ((f32[32,4,128]{2,1,0:T(4,128)}), f32[32,4,128]{2,1,0:T(4,128)S(1)}, u32[]{:S(2)}, u32[]{:S(2)}) async-start(f32[32,4,128]{2,1,0:T(4,128)} %get-tuple-element.63), calls=%async_computation.2 | async-start | bytes 131072 | tf_op jit(solution)/shard_map/all_to_all | solution.py:679
  61.7 1.8 %scatter_two.1 = (f32[3,8,32,256]{3,2,1,0:T(8,128)S(1)}, f32[3,8,32,256]{3,2,1,0:T(8,128)S(1)}) custom-call(f32[3,8,32,256]{3,2,1,0:T(8,128)S(1)} %get-tuple-element.59.e_ref, f32[16,4,128]{2,1,0:T(4,128)S(1)} %get-tuple-element.60.force_ref, s32[8,1,256]{2,1,0:T(1,128)S(1)} %get-tuple-element.41.map_ref, f32[3,8,32,256]{3,2,1,0:T(8,128)} %r_hbm.3), custom_call_target="tpu_custom_call" | custom-call | flops 300000000 | bytes 9000000 | tf_op jit(solution)/shard_map/scatter_two/pallas_call | solution.py:680
  63.6 5.6 %all-to-all-done.2.red_ref = f32[32,4,128]{2,1,0:T(4,128)S(1)} async-done(((f32[32,4,128]{2,1,0:T(4,128)}), f32[32,4,128]{2,1,0:T(4,128)S(1)}, u32[]{:S(2)}, u32[]{:S(2)}) %all-to-all-start.2) | async-done | bytes 65568 | tf_op jit(solution)/shard_map/all_to_all | solution.py:679
  69.2 1.4 %final.1 = (f32[3,8,32,256]{3,2,1,0:T(8,128)}, f32[3,8,32,256]{3,2,1,0:T(8,128)}) custom-call(f32[3,8,32,256]{3,2,1,0:T(8,128)S(1)} %get-tuple-element.61.r_ref, f32[3,8,32,256]{3,2,1,0:T(8,128)S(1)} %get-tuple-element.49.w1_ref, f32[3,8,32,256]{3,2,1,0:T(8,128)S(1)} %get-tuple-element.62.w2_ref, f32[32,4,128]{2,1,0:T(4,128)S(1)} %all-to-all-done.2.red_ref), custom_call_target="tpu_custom_call" | custom-call | flops 100000000 | bytes 3000000 | tf_op jit(solution)/shard_map/final/pallas_call | solution.py:685
  (6 shorter events, 0.0 us)
Async XLA Ops:
  6.2 26.4 %all-to-all-start = ((f32[8,12,8,128]{3,2,1,0:T(8,128)}), f32[8,12,8,128]{3,2,1,0:T(8,128)S(1)}, u32[]{:S(2)}, u32[]{:S(2)}) async-start(f32[8,12,8,128]{3,2,1,0:T(8,128)} %get-tuple-element.43), calls=%async_computation | async-start | bytes 786432 | tf_op jit(solution)/shard_map/all_to_all | solution.py:650
  13.5 12.0 %collective-permute-start = (f32[5,32,256]{2,1,0:T(8,128)S(1)}, f32[5,32,256]{2,1,0:T(8,128)S(1)}, u32[]{:S(2)}, u32[]{:S(2)}) collective-permute-start(f32[5,32,256]{2,1,0:T(8,128)S(1)} %get-tuple-element.37), channel_id=1, source_target_pairs={{0,4},{4,0},{8,12},{12,8},{16,20},{20,16},{24,28},{28,24},{1,5},{5... | collective-permute-start | bytes 491528 | tf_op jit(solution)/shard_map/ppermute | solution.py:596
  15.5 12.8 %collective-permute-start.1 = (f32[5,32,256]{2,1,0:T(8,128)S(1)}, f32[5,32,256]{2,1,0:T(8,128)S(1)}, u32[]{:S(2)}, u32[]{:S(2)}) collective-permute-start(f32[5,32,256]{2,1,0:T(8,128)S(1)} %get-tuple-element.38), channel_id=1, source_target_pairs={{0,28},{4,8},{8,4},{12,16},{16,12},{20,24},{24,20},{28,0},{1,29},{... | collective-permute-start | bytes 491528 | tf_op jit(solution)/shard_map/ppermute | solution.py:595
  18.8 1.6 %collective-permute-start.2 = (f32[5,8,256]{2,1,0:T(8,128)S(1)}, f32[5,8,256]{2,1,0:T(8,128)S(1)}, u32[]{:S(2)}, u32[]{:S(2)}) collective-permute-start(f32[5,8,256]{2,1,0:T(8,128)S(1)} %get-tuple-element.39), channel_id=1, source_target_pairs={{0,1},{1,0},{2,3},{3,2},{4,5},{5,4},{6,7},{7,6},{8,9},{9,8},{10,11... | collective-permute-start | bytes 122888 | tf_op jit(solution)/shard_map/ppermute | solution.py:598
  18.8 3.4 %collective-permute-start.3 = (f32[5,8,256]{2,1,0:T(8,128)S(1)}, f32[5,8,256]{2,1,0:T(8,128)S(1)}, u32[]{:S(2)}, u32[]{:S(2)}) collective-permute-start(f32[5,8,256]{2,1,0:T(8,128)S(1)} %get-tuple-element.40), channel_id=1, source_target_pairs={{0,3},{1,2},{2,1},{3,0},{4,7},{5,6},{6,5},{7,4},{8,11},{9,10},{10,... | collective-permute-start | bytes 122888 | tf_op jit(solution)/shard_map/ppermute | solution.py:597
  39.7 13.2 %all-to-all-start.1 = ((f32[8,8,4,128]{3,2,1,0:T(4,128)}), f32[8,8,4,128]{3,2,1,0:T(4,128)S(1)}, u32[]{:S(2)}, u32[]{:S(2)}) async-start(f32[8,8,4,128]{3,2,1,0:T(4,128)} %get-tuple-element.54), calls=%async_computation.1 | async-start | bytes 262144 | tf_op jit(solution)/shard_map/all_to_all | solution.py:664
  46.0 10.2 %collective-permute-start.4 = (f32[3,32,256]{2,1,0:T(8,128)S(1)}, f32[3,32,256]{2,1,0:T(8,128)S(1)}, u32[]{:S(2)}, u32[]{:S(2)}) collective-permute-start(f32[3,32,256]{2,1,0:T(8,128)S(1)} %get-tuple-element.50), channel_id=1, source_target_pairs={{0,4},{4,0},{8,12},{12,8},{16,20},{20,16},{24,28},{28,24},{1,5},{5... | collective-permute-start | bytes 294920 | tf_op jit(solution)/shard_map/ppermute | solution.py:596
  48.0 8.2 %collective-permute-start.5 = (f32[3,32,256]{2,1,0:T(8,128)S(1)}, f32[3,32,256]{2,1,0:T(8,128)S(1)}, u32[]{:S(2)}, u32[]{:S(2)}) collective-permute-start(f32[3,32,256]{2,1,0:T(8,128)S(1)} %get-tuple-element.51), channel_id=1, source_target_pairs={{0,28},{4,8},{8,4},{12,16},{16,12},{20,24},{24,20},{28,0},{1,29},{... | collective-permute-start | bytes 294920 | tf_op jit(solution)/shard_map/ppermute | solution.py:595
  51.3 4.9 %collective-permute-start.6 = (f32[3,8,256]{2,1,0:T(8,128)S(1)}, f32[3,8,256]{2,1,0:T(8,128)S(1)}, u32[]{:S(2)}, u32[]{:S(2)}) collective-permute-start(f32[3,8,256]{2,1,0:T(8,128)S(1)} %get-tuple-element.52), channel_id=1, source_target_pairs={{0,1},{1,0},{2,3},{3,2},{4,5},{5,4},{6,7},{7,6},{8,9},{9,8},{10,11... | collective-permute-start | bytes 73736 | tf_op jit(solution)/shard_map/ppermute | solution.py:598
  51.3 4.9 %collective-permute-start.7 = (f32[3,8,256]{2,1,0:T(8,128)S(1)}, f32[3,8,256]{2,1,0:T(8,128)S(1)}, u32[]{:S(2)}, u32[]{:S(2)}) collective-permute-start(f32[3,8,256]{2,1,0:T(8,128)S(1)} %get-tuple-element.53), channel_id=1, source_target_pairs={{0,3},{1,2},{2,1},{3,0},{4,7},{5,6},{6,5},{7,4},{8,11},{9,10},{10,... | collective-permute-start | bytes 73736 | tf_op jit(solution)/shard_map/ppermute | solution.py:597
  58.0 11.1 %all-to-all-start.2 = ((f32[32,4,128]{2,1,0:T(4,128)}), f32[32,4,128]{2,1,0:T(4,128)S(1)}, u32[]{:S(2)}, u32[]{:S(2)}) async-start(f32[32,4,128]{2,1,0:T(4,128)} %get-tuple-element.63), calls=%async_computation.2 | async-start | bytes 131072 | tf_op jit(solution)/shard_map/all_to_all | solution.py:679

commit v4 on v3

--- a/solution.py
+++ b/solution.py
@@ -97,7 +97,7 @@
             write(j, c, jnp.sum(part, axis=0, keepdims=True))
         return carry
 
-    lax.fori_loop(0, chunks, chunk, 0)
+    lax.fori_loop(0, chunks, chunk, 0, unroll=8)
 
 
 def open_kernel(
@@ -264,7 +264,7 @@
         keep(d).start()
         return carry
 
-    lax.fori_loop(0, bodies, device, 0)
+    lax.fori_loop(0, bodies, device, 0, unroll=4)
     row = lax.broadcasted_iota(I32, (4, points), 0)
     inner = jnp.zeros((4, points), F32)
     for k in range(blocks):
@@ -292,7 +292,7 @@
     lax.fori_loop(0, bodies, finish, 0)
 
 
-def scatter_sum(base, rows, depth, map_ref, force_ref, left_ref, right_ref):
+def scatter_parts(rows, depth, map_ref, force_ref, left_ref, right_ref):
     span = map_ref.shape[2]
     per = force_ref.shape[0] // map_ref.shape[0]
     depth_iota = lax.broadcasted_iota(I32, (depth, span), 0)
@@ -314,28 +314,23 @@
             left_ref[at, (chunks + j) * span : (chunks + j + 1) * span] = jnp.where(
                 here, line - high, 0.0
             ).astype(BF16)
-    spread = lax.dot_general(
-        left_ref[...], right_ref[...], (((1,), (1,)), ((), ())), preferred_element_type=F32
-    )
-    return [base(c) + spread[c * rows : (c + 1) * rows] for c in range(3)]
+    def spread(c):
+        return lax.dot_general(
+            left_ref[c * rows : (c + 1) * rows], right_ref[...], (((1,), (1,)), ((), ())),
+            preferred_element_type=F32,
+        )
+
+    return spread
 
 
 def scatter_one_kernel(
-    e_hbm, force_ref, map_ref, w1_ref, xe_ref, xo_ref, ye_ref, yo_ref, e_ref, left_ref, right_ref, sem
+    e0_ref, e1_ref, e2_ref, force_ref, map_ref,
+    w1_ref, xe_ref, xo_ref, ye_ref, yo_ref, left_ref, right_ref,
 ):
-    copy = pltpu.make_async_copy(e_hbm, e_ref, sem)
-    copy.start()
-    shape = e_ref.shape[1:]
-    rows, depth = shape[0] * shape[1], shape[2]
-
-    def base(c):
-        if c == 0:
-            copy.wait()
-        return e_ref[c].reshape(rows, depth)
-
-    sums = scatter_sum(base, rows, depth, map_ref, force_ref, left_ref, right_ref)
-    for c in range(3):
-        w1_ref[c] = sums[c].reshape(shape)
+    shape = e0_ref.shape
+    spread = scatter_parts(shape[0] * shape[1], shape[2], map_ref, force_ref, left_ref, right_ref)
+    for c, e_ref in enumerate((e0_ref, e1_ref, e2_ref)):
+        w1_ref[c] = e_ref[...] + spread(c).reshape(shape)
     write_faces([(w1_ref, 0), (w1_ref, 1), (w1_ref, 2)], xe_ref, xo_ref, ye_ref, yo_ref)
 
 
@@ -345,12 +340,9 @@
     copy = pltpu.make_async_copy(r_hbm, r_ref, sem)
     copy.start()
     shape = e_ref.shape[1:]
-    rows, depth = shape[0] * shape[1], shape[2]
-    sums = scatter_sum(
-        lambda c: e_ref[c].reshape(rows, depth), rows, depth, map_ref, force_ref, left_ref, right_ref
-    )
+    spread = scatter_parts(shape[0] * shape[1], shape[2], map_ref, force_ref, left_ref, right_ref)
     for c in range(3):
-        w2_ref[c] = sums[c].reshape(shape)
+        w2_ref[c] = e_ref[c] + spread(c).reshape(shape)
     copy.wait()
 
 
@@ -450,21 +442,20 @@
 
 def stencil_one_kernel(
     r_ref, sh_ref, la_ref, in_ref, xe, xo, ye, yo, map_ref,
-    e_hbm, next_ref, e_ref, both_ref, sem,
+    e0_ref, e1_ref, e2_ref, next_ref, both_ref,
 ):
+    e_refs = (e0_ref, e1_ref, e2_ref)
     sums = [jnp.zeros((8, 128), F32) for _ in range(2)]
 
     def emit(x, total):
         for c in range(3):
-            e_ref[c, x] = total[c]
+            e_refs[c][x] = total[c]
             r = r_ref[c, x]
             sums[0] = sums[0] + fold(r * r)
             sums[1] = sums[1] + fold(r * total[c])
 
     elastic(r_ref, sh_ref, la_ref, in_ref, (xe, xo, ye, yo), (xe, xo, ye, yo), emit)
-    copy = pltpu.make_async_copy(e_ref, e_hbm, sem)
-    copy.start()
-    rows, depth = e_ref.shape[1] * e_ref.shape[2], e_ref.shape[3]
+    rows, depth = e0_ref.shape[0] * e0_ref.shape[1], e0_ref.shape[2]
     points = next_ref.shape[2]
 
     def write(j, c, line):
@@ -477,8 +468,7 @@
         next_ref[k, 3:4, :] = jnp.zeros((1, points), F32)
     lines = [jnp.sum(value, axis=0, keepdims=True) for value in sums]
     next_ref[blocks] = jnp.concatenate(lines + [jnp.zeros((2, points), F32)], axis=0)
-    gather_into(lambda c: e_ref[c].reshape(rows, depth), rows, depth, map_ref, both_ref, write)
-    copy.wait()
+    gather_into(lambda c: e_refs[c][...].reshape(rows, depth), rows, depth, map_ref, both_ref, write)
 
 
 def fold(value):
@@ -492,7 +482,8 @@
 
 
 def forces_two_kernel(
-    got_ref, target_ref, table_ref, move_ref, w_hbm, force_ref, dots_ref, w_ref, acc_ref, sem
+    got_ref, target_ref, table_ref, move_ref, w_hbm, sh_hbm, la_hbm, in_hbm_ref,
+    force_ref, dots_ref, sh_ref, la_ref, in_ref, w_ref, acc_ref, sem, cell_sem,
 ):
     bodies, width = got_ref.shape[0], got_ref.shape[1]
     cap = width // 2
@@ -506,6 +497,14 @@
         return carry
 
     lax.fori_loop(0, bodies, begin, 0)
+    cells = [
+        pltpu.make_async_copy(source, target, cell_sem.at[k])
+        for k, (source, target) in enumerate(
+            [(sh_hbm, sh_ref), (la_hbm, la_ref), (in_hbm_ref, in_ref)]
+        )
+    ]
+    for copy in cells:
+        copy.start()
     acc_ref[...] = jnp.zeros_like(acc_ref)
 
     def device(d, carry):
@@ -530,6 +529,8 @@
     inner = jnp.sum(inner[0:3], axis=0, keepdims=True)
     blank = jnp.zeros_like(inner)
     dots_ref[...] = jnp.concatenate([move_ref[blocks][0:2], blank, inner], axis=0)
+    for copy in cells:
+        copy.wait()
 
 
 def stencil_two_kernel(
@@ -636,6 +637,7 @@
     dma = pltpu.SemaphoreType.DMA
     cells = (sds((rows, cols, depth)),) * 3
 
+    given = (shear, lame, inertia)
     r, shear, lame, inertia, cell_maps, xe, xo, ye, yo, own, first_moves, message, table = call(
         open_kernel, "open", [HBM] * 8, [VMEM] * 12 + [SMEM],
         (vector,) + cells + (sds(cell_maps.shape, I32),) + faces(5)
@@ -650,10 +652,9 @@
     got = lax.all_to_all(message, "body", 0, 0, tiled=True)
     halo = exchange(xe, xo, ye, yo)
     grown = sds((blocks + 1, 4, width))
-    elastic_one, next_moves = call(
-        stencil_one_kernel, "stencil_one", [VMEM] * 9, [HBM, VMEM],
-        (pltpu.HBM((3, rows, cols, depth), F32), grown),
-        scratch=(pltpu.VMEM((3, rows, cols, depth), F32), both, dma(())), cost=5.0,
+    *elastic_one, next_moves = call(
+        stencil_one_kernel, "stencil_one", [VMEM] * 9, [VMEM] * 4, cells + (grown,),
+        scratch=(both,), cost=5.0,
     )(r, shear, lame, inertia, *halo, cell_maps)
     force_one, second_moves, message, targets, weights = call(
         forces_one_kernel, "forces_one", [VMEM] * 2 + [SMEM] + [VMEM] * 2,
@@ -663,15 +664,15 @@
     )(got, own, table, first_moves, next_moves)
     got = lax.all_to_all(message, "body", 0, 0, tiled=True)
     w1, xe, xo, ye, yo = call(
-        scatter_one_kernel, "scatter_one", [HBM] + [VMEM] * 2, [VMEM] * 5, (vector,) + faces(3),
-        scratch=(pltpu.VMEM((3, rows, cols, depth), F32),) + sides + (dma(()),), cost=3.0, mib=16,
-    )(*in_hbm(elastic_one), force_one, cell_maps)
+        scatter_one_kernel, "scatter_one", [VMEM] * 5, [VMEM] * 5, (vector,) + faces(3),
+        scratch=sides, cost=3.0, mib=16,
+    )(*elastic_one, force_one, cell_maps)
     halo_two = exchange(xe, xo, ye, yo)
-    force_two, dots = call(
-        forces_two_kernel, "forces_two", [VMEM] + [SMEM] * 2 + [VMEM, HBM], [VMEM] * 2,
-        (moves, sds((4, 128))),
-        scratch=(pltpu.VMEM(kept, BF16), total, dma((bodies,))), cost=3.0, mib=kept_mib,
-    )(got, targets, table, second_moves, *in_hbm(weights))
+    force_two, dots, shear, lame, inertia = call(
+        forces_two_kernel, "forces_two", [VMEM] + [SMEM] * 2 + [VMEM] + [HBM] * 4, [VMEM] * 5,
+        (moves, sds((4, 128))) + cells,
+        scratch=(pltpu.VMEM(kept, BF16), total, dma((bodies,)), dma((3,))), cost=3.0, mib=kept_mib,
+    )(got, targets, table, second_moves, *in_hbm(weights, *given))
     elastic_two, partial = call(
         stencil_two_kernel, "stencil_two", [VMEM] * 13, [VMEM] * 2, (vector, sds((devices, 4, 128))),
         cost=1.5,

time: 70.9 us -> 65.9 us (0.929)
  Pallas kernels: 28 us -> 23.1 us
    pallas_call x3, Pallas kernels: 10.4 us -> 8.22 us  [the longest x1 3.25 us: on_device(): call(forces_two_kernel, 'forces_two', [VMEM] + [SMEM] * 2 + [VMEM] + [HBM...]
    pallas_call x1, Pallas kernels: 7.08 us -> 5.35 us  [on_device(): call(forces_one_kernel, 'forces_one', [VMEM] * 2 + [SMEM] + [VMEM] * 2, [...]
    pallas_call x1, Pallas kernels: 5.56 us -> 4.48 us  [on_device(): call(open_kernel, 'open', [HBM] * 8, [VMEM] * 12 + [SMEM], (vector,) + ce...]
  transfers between devices with their start and end apart: 11 -> 11, of which waited for: 4 -> 4; matrix products, arithmetic and copies ran while one was open for 0% -> 0% of each run, Pallas kernels for 17% -> 15%
where the time goes in v4:
time: 65.9 us; the launch traced here: 65.6 us
  starting transfers between devices  28.2 us (43%)
  Pallas kernels  23.1 us (35%)
  waiting for transfers between devices  13.6 us (21%)
  between operations  0.74 us (1%)
    all_to_all x2, starting transfers between devices, on_device(): got = lax.all_to_all(message, 'body', 0, 0, tiled=True)  10.7 us
    ppermute x2, starting transfers between devices, exchange(): got_xo = lax.ppermute(xo, 'body', pairs('body', 1))  6.56 us
    all_to_all x1, waiting for transfers between devices, on_device(): sums = lax.all_to_all(partial, ('body', 'across'), 0, 0, tiled=True)  5.54 us
    pallas_call x1, Pallas kernels, on_device(): call(forces_one_kernel, 'forces_one', [VMEM] * 2 + [SMEM] + [VMEM] * 2, [...  5.35 us
    pallas_call x1, Pallas kernels, on_device(): call(open_kernel, 'open', [HBM] * 8, [VMEM] * 12 + [SMEM], (vector,) + ce...  4.48 us
    ppermute x2, starting transfers between devices, exchange(): got_xe = lax.ppermute(xe, 'body', pairs('body', 0))  4 us
    all_to_all x1, starting transfers between devices, on_device(): sums = lax.all_to_all(partial, ('body', 'across'), 0, 0, tiled=True)  3.69 us
    ppermute x2, waiting for transfers between devices, exchange(): got_xe = lax.ppermute(xe, 'body', pairs('body', 0))  3.29 us
  transfers between devices with their start and end apart: 11, of which 4 were waited for; matrix products, arithmetic and copies ran while one was open for 0% of the time, Pallas kernels for 15%

profile of v4, /device:TPU:0, one launch (start us, length us, event | category | flops | bytes accessed | tf_op | source)
XLA Modules:
  0.0 65.6 jit_solution(7514094062567325101)
XLA Ops:
  0.6 4.5 %open.1 = (f32[3,8,32,256]{3,2,1,0:T(8,128)S(1)}, f32[8,32,256]{2,1,0:T(8,128)S(1)}, f32[8,32,256]{2,1,0:T(8,128)S(1)}, f32[8,32,256]{2,1,0:T(8,128)S(1)}, s32[8...) custom-call(f32[3,8,32,256]{3,2,1,0:T(8,128)} %r_hbm.3, ...), custom_call_target="tpu_custom_call" | custom-call | flops 400000000 | bytes 12000000 | tf_op jit(solution)/shard_map/open/pallas_call | solution.py:641
  5.1 7.3 %all-to-all-start = ((f32[8,12,8,128]{3,2,1,0:T(8,128)}), f32[8,12,8,128]{3,2,1,0:T(8,128)S(1)}, u32[]{:S(2)}, u32[]{:S(2)}) async-start(f32[8,12,8,128]{3,2,1,0:T(8,128)} %get-tuple-element.50), calls=%async_computation | async-start | bytes 786432 | tf_op jit(solution)/shard_map/all_to_all | solution.py:652
  12.4 2.0 %collective-permute-start = (f32[5,32,256]{2,1,0:T(8,128)S(1)}, f32[5,32,256]{2,1,0:T(8,128)S(1)}, u32[]{:S(2)}, u32[]{:S(2)}) collective-permute-start(f32[5,32,256]{2,1,0:T(8,128)S(1)} %get-tuple-element.42), channel_id=1, source_target_pairs={{0,4},{4,0},{8,12},{12,8},{16,20},{20,16},{24,28},{28,24},{1,5},{5... | collective-permute-start | bytes 491528 | tf_op jit(solution)/shard_map/ppermute | solution.py:597
  14.5 3.3 %collective-permute-start.1 = (f32[5,32,256]{2,1,0:T(8,128)S(1)}, f32[5,32,256]{2,1,0:T(8,128)S(1)}, u32[]{:S(2)}, u32[]{:S(2)}) collective-permute-start(f32[5,32,256]{2,1,0:T(8,128)S(1)} %get-tuple-element.43), channel_id=1, source_target_pairs={{0,28},{4,8},{8,4},{12,16},{16,12},{20,24},{24,20},{28,0},{1,29},{... | collective-permute-start | bytes 491528 | tf_op jit(solution)/shard_map/ppermute | solution.py:596
  17.7 0.0 collective-permute-start.2
  17.7 1.6 %collective-permute-start.3 = (f32[5,8,256]{2,1,0:T(8,128)S(1)}, f32[5,8,256]{2,1,0:T(8,128)S(1)}, u32[]{:S(2)}, u32[]{:S(2)}) collective-permute-start(f32[5,8,256]{2,1,0:T(8,128)S(1)} %get-tuple-element.45), channel_id=1, source_target_pairs={{0,3},{1,2},{2,1},{3,0},{4,7},{5,6},{6,5},{7,4},{8,11},{9,10},{10,... | collective-permute-start | bytes 122888 | tf_op jit(solution)/shard_map/ppermute | solution.py:598
  19.3 0.0 collective-permute-done.2.ye.cye
  19.3 1.8 %collective-permute-done.3.yo.cyo = f32[5,8,256]{2,1,0:T(8,128)S(1)} collective-permute-done((f32[5,8,256]{2,1,0:T(8,128)S(1)}, f32[5,8,256]{2,1,0:T(8,128)S(1)}, u32[]{:S(2)}, u32[]{:S(2)}) %collective-permute-start.3) | collective-permute-done | bytes 40992 | tf_op jit(solution)/shard_map/ppermute | solution.py:598
  21.2 3.3 %collective-permute-done.xe.cxe = f32[5,32,256]{2,1,0:T(8,128)S(1)} collective-permute-done((f32[5,32,256]{2,1,0:T(8,128)S(1)}, f32[5,32,256]{2,1,0:T(8,128)S(1)}, u32[]{:S(2)}, u32[]{:S(2)}) %collective-permute-start) | collective-permute-done | bytes 163872 | tf_op jit(solution)/shard_map/ppermute | solution.py:597
  24.4 2.9 %collective-permute-done.1.xo.cxo = f32[5,32,256]{2,1,0:T(8,128)S(1)} collective-permute-done((f32[5,32,256]{2,1,0:T(8,128)S(1)}, f32[5,32,256]{2,1,0:T(8,128)S(1)}, u32[]{:S(2)}, u32[]{:S(2)}) %collective-permute-start.1) | collective-permute-done | bytes 163872 | tf_op jit(solution)/shard_map/ppermute | solution.py:596
  27.3 3.1 %stencil_one.1 = (f32[8,32,256]{2,1,0:T(8,128)S(1)}, f32[8,32,256]{2,1,0:T(8,128)S(1)}, f32[8,32,256]{2,1,0:T(8,128)S(1)}, f32[17,4,128]{2,1,0:T(4,128)S(1)}) custom-call(f32[3,8,32,256]{3,2,1,0:T(8,128)S(1)} %get-tuple-element.38.r_ref, f32[8,32,256]{2,1,0:T(8,128)S(1)} %get-tuple-element.39.sh_ref, f32[8,32,256]{2,1,0:T(8,128)S(1)} %get-tuple-element.40.la_ref, ...), custom_call_target="tpu_custom_call" | custom-call | flops 500000000 | bytes 15000000 | tf_op jit(solution)/shard_map/stencil_one/pallas_call | solution.py:655
  30.4 0.0 all-to-all-done.got_ref
  30.4 5.4 %forces_one.1 = (f32[16,4,128]{2,1,0:T(4,128)S(1)}, f32[17,4,128]{2,1,0:T(4,128)S(1)}, f32[8,8,4,128]{3,2,1,0:T(4,128)}, s32[32]{0:T(128)S(1)}, bf16[8,8,128,256]{3,2,1,0:T(8,128)(2,1)}) custom-call(f32[8,12,8,128]{3,2,1,0:T(8,128)S(1)} %all-to-all-done.got_ref, bf16[16,32,128]{2,1,0:T(8,128)(2,1)S(1)} %get-tuple-element.51.own_ref, ...), custom_call_target="tpu_custom_call" | custom-call | flops 600000000 | bytes 18000000 | tf_op jit(solution)/shard_map/forces_one/pallas_call | solution.py:659
  35.8 3.4 %all-to-all-start.1 = ((f32[8,8,4,128]{3,2,1,0:T(4,128)}), f32[8,8,4,128]{3,2,1,0:T(4,128)S(1)}, u32[]{:S(2)}, u32[]{:S(2)}) async-start(f32[8,8,4,128]{3,2,1,0:T(4,128)} %get-tuple-element.57), calls=%async_computation.1 | async-start | bytes 262144 | tf_op jit(solution)/shard_map/all_to_all | solution.py:665
  39.2 1.9 %scatter_one.1 = (f32[3,8,32,256]{3,2,1,0:T(8,128)S(1)}, f32[3,32,256]{2,1,0:T(8,128)S(1)}, f32[3,32,256]{2,1,0:T(8,128)S(1)}, f32[3,8,256]{2,1,0:T(8,128)S(1)}, f32[3,8,256]{2,1,0:T(8,128)S(1)}) custom-call(f32[8,32,256]{2,1,0:T(8,128)S(1)} %get-tuple-element.47.e0_ref, f32[8,32,256]{2,1,0:T(8,128)S(1)} %get-tuple-element.48.e1_ref, ...), custom_call_target="tpu_custom_call" | custom-call | flops 300000000 | bytes 9000000 | tf_op jit(solution)/shard_map/scatter_one/pallas_call | solution.py:666
  41.1 2.0 %collective-permute-start.4 = (f32[3,32,256]{2,1,0:T(8,128)S(1)}, f32[3,32,256]{2,1,0:T(8,128)S(1)}, u32[]{:S(2)}, u32[]{:S(2)}) collective-permute-start(f32[3,32,256]{2,1,0:T(8,128)S(1)} %get-tuple-element.64), channel_id=1, source_target_pairs={{0,4},{4,0},{8,12},{12,8},{16,20},{20,16},{24,28},{28,24},{1,5},{5... | collective-permute-start | bytes 294920 | tf_op jit(solution)/shard_map/ppermute | solution.py:597
  43.1 3.3 %collective-permute-start.5 = (f32[3,32,256]{2,1,0:T(8,128)S(1)}, f32[3,32,256]{2,1,0:T(8,128)S(1)}, u32[]{:S(2)}, u32[]{:S(2)}) collective-permute-start(f32[3,32,256]{2,1,0:T(8,128)S(1)} %get-tuple-element.65), channel_id=1, source_target_pairs={{0,28},{4,8},{8,4},{12,16},{16,12},{20,24},{24,20},{28,0},{1,29},{... | collective-permute-start | bytes 294920 | tf_op jit(solution)/shard_map/ppermute | solution.py:596
  46.4 1.6 %collective-permute-start.7 = (f32[3,8,256]{2,1,0:T(8,128)S(1)}, f32[3,8,256]{2,1,0:T(8,128)S(1)}, u32[]{:S(2)}, u32[]{:S(2)}) collective-permute-start(f32[3,8,256]{2,1,0:T(8,128)S(1)} %get-tuple-element.67), channel_id=1, source_target_pairs={{0,3},{1,2},{2,1},{3,0},{4,7},{5,6},{6,5},{7,4},{8,11},{9,10},{10,... | collective-permute-start | bytes 73736 | tf_op jit(solution)/shard_map/ppermute | solution.py:598
  48.0 3.2 %forces_two.1 = (f32[16,4,128]{2,1,0:T(4,128)S(1)}, f32[4,128]{1,0:T(4,128)S(1)}, f32[8,32,256]{2,1,0:T(8,128)S(1)}, f32[8,32,256]{2,1,0:T(8,128)S(1)}, f32[8,32,256]{2,1,0:T(8,128)S(1)}) custom-call(f32[8,8,4,128]{3,2,1,0:T(4,128)S(1)} %all-to-all-done.1.got_ref, s32[32]{0:T(128)S(1)} %get-tuple-element.58.target_ref, ...), custom_call_target="tpu_custom_call" | custom-call | flops 300000000 | bytes 9000000 | tf_op jit(solution)/shard_map/forces_two/pallas_call | solution.py:671
  51.3 1.8 %stencil_two.1 = (f32[3,8,32,256]{3,2,1,0:T(8,128)S(1)}, f32[32,4,128]{2,1,0:T(4,128)}) custom-call(f32[3,8,32,256]{3,2,1,0:T(8,128)S(1)} %get-tuple-element.56.w1_ref, f32[8,32,256]{2,1,0:T(8,128)S(1)} %get-tuple-element.61.sh_ref, f32[8,32,256]{2,1,0:T(8,128)S(1)} %get-tuple-element.62.la_ref, f32[8,32,256]{2,1,0:T(8,128)S(1)} %get-tuple-element.63.in_ref, ...), custom_call_target="tpu_custom_call" | custom-call | flops 150000000 | bytes 4500000 | tf_op jit(solution)/shard_map/stencil_two/pallas_call | solution.py:676
  53.1 3.7 %all-to-all-start.2 = ((f32[32,4,128]{2,1,0:T(4,128)}), f32[32,4,128]{2,1,0:T(4,128)S(1)}, u32[]{:S(2)}, u32[]{:S(2)}) async-start(f32[32,4,128]{2,1,0:T(4,128)} %get-tuple-element.73), calls=%async_computation.2 | async-start | bytes 131072 | tf_op jit(solution)/shard_map/all_to_all | solution.py:680
  56.8 1.9 %scatter_two.1 = (f32[3,8,32,256]{3,2,1,0:T(8,128)S(1)}, f32[3,8,32,256]{3,2,1,0:T(8,128)S(1)}) custom-call(f32[3,8,32,256]{3,2,1,0:T(8,128)S(1)} %get-tuple-element.69.e_ref, f32[16,4,128]{2,1,0:T(4,128)S(1)} %get-tuple-element.70.force_ref, s32[8,1,256]{2,1,0:T(1,128)S(1)} %get-tuple-element.46.map_ref, f32[3,8,32,256]{3,2,1,0:T(8,128)} %r_hbm.3), custom_call_target="tpu_custom_call" | custom-call | flops 300000000 | bytes 9000000 | tf_op jit(solution)/shard_map/scatter_two/pallas_call | solution.py:681
  58.6 5.5 %all-to-all-done.2.red_ref = f32[32,4,128]{2,1,0:T(4,128)S(1)} async-done(((f32[32,4,128]{2,1,0:T(4,128)}), f32[32,4,128]{2,1,0:T(4,128)S(1)}, u32[]{:S(2)}, u32[]{:S(2)}) %all-to-all-start.2) | async-done | bytes 65568 | tf_op jit(solution)/shard_map/all_to_all | solution.py:680
  64.2 1.4 %final.1 = (f32[3,8,32,256]{3,2,1,0:T(8,128)}, f32[3,8,32,256]{3,2,1,0:T(8,128)}) custom-call(f32[3,8,32,256]{3,2,1,0:T(8,128)S(1)} %get-tuple-element.71.r_ref, f32[3,8,32,256]{3,2,1,0:T(8,128)S(1)} %get-tuple-element.56.w1_ref, f32[3,8,32,256]{3,2,1,0:T(8,128)S(1)} %get-tuple-element.72.w2_ref, f32[32,4,128]{2,1,0:T(4,128)S(1)} %all-to-all-done.2.red_ref), custom_call_target="tpu_custom_call" | custom-call | flops 100000000 | bytes 3000000 | tf_op jit(solution)/shard_map/final/pallas_call | solution.py:686
  (6 shorter events, 0.0 us)
Async XLA Ops:
  5.1 25.3 %all-to-all-start = ((f32[8,12,8,128]{3,2,1,0:T(8,128)}), f32[8,12,8,128]{3,2,1,0:T(8,128)S(1)}, u32[]{:S(2)}, u32[]{:S(2)}) async-start(f32[8,12,8,128]{3,2,1,0:T(8,128)} %get-tuple-element.50), calls=%async_computation | async-start | bytes 786432 | tf_op jit(solution)/shard_map/all_to_all | solution.py:652
  12.4 12.0 %collective-permute-start = (f32[5,32,256]{2,1,0:T(8,128)S(1)}, f32[5,32,256]{2,1,0:T(8,128)S(1)}, u32[]{:S(2)}, u32[]{:S(2)}) collective-permute-start(f32[5,32,256]{2,1,0:T(8,128)S(1)} %get-tuple-element.42), channel_id=1, source_target_pairs={{0,4},{4,0},{8,12},{12,8},{16,20},{20,16},{24,28},{28,24},{1,5},{5... | collective-permute-start | bytes 491528 | tf_op jit(solution)/shard_map/ppermute | solution.py:597
  14.5 12.9 %collective-permute-start.1 = (f32[5,32,256]{2,1,0:T(8,128)S(1)}, f32[5,32,256]{2,1,0:T(8,128)S(1)}, u32[]{:S(2)}, u32[]{:S(2)}) collective-permute-start(f32[5,32,256]{2,1,0:T(8,128)S(1)} %get-tuple-element.43), channel_id=1, source_target_pairs={{0,28},{4,8},{8,4},{12,16},{16,12},{20,24},{24,20},{28,0},{1,29},{... | collective-permute-start | bytes 491528 | tf_op jit(solution)/shard_map/ppermute | solution.py:596
  17.7 1.6 %collective-permute-start.2 = (f32[5,8,256]{2,1,0:T(8,128)S(1)}, f32[5,8,256]{2,1,0:T(8,128)S(1)}, u32[]{:S(2)}, u32[]{:S(2)}) collective-permute-start(f32[5,8,256]{2,1,0:T(8,128)S(1)} %get-tuple-element.44), channel_id=1, source_target_pairs={{0,1},{1,0},{2,3},{3,2},{4,5},{5,4},{6,7},{7,6},{8,9},{9,8},{10,11... | collective-permute-start | bytes 122888 | tf_op jit(solution)/shard_map/ppermute | solution.py:599
  17.7 3.4 %collective-permute-start.3 = (f32[5,8,256]{2,1,0:T(8,128)S(1)}, f32[5,8,256]{2,1,0:T(8,128)S(1)}, u32[]{:S(2)}, u32[]{:S(2)}) collective-permute-start(f32[5,8,256]{2,1,0:T(8,128)S(1)} %get-tuple-element.45), channel_id=1, source_target_pairs={{0,3},{1,2},{2,1},{3,0},{4,7},{5,6},{6,5},{7,4},{8,11},{9,10},{10,... | collective-permute-start | bytes 122888 | tf_op jit(solution)/shard_map/ppermute | solution.py:598
  35.8 12.2 %all-to-all-start.1 = ((f32[8,8,4,128]{3,2,1,0:T(4,128)}), f32[8,8,4,128]{3,2,1,0:T(4,128)S(1)}, u32[]{:S(2)}, u32[]{:S(2)}) async-start(f32[8,8,4,128]{3,2,1,0:T(4,128)} %get-tuple-element.57), calls=%async_computation.1 | async-start | bytes 262144 | tf_op jit(solution)/shard_map/all_to_all | solution.py:665
  41.1 10.2 %collective-permute-start.4 = (f32[3,32,256]{2,1,0:T(8,128)S(1)}, f32[3,32,256]{2,1,0:T(8,128)S(1)}, u32[]{:S(2)}, u32[]{:S(2)}) collective-permute-start(f32[3,32,256]{2,1,0:T(8,128)S(1)} %get-tuple-element.64), channel_id=1, source_target_pairs={{0,4},{4,0},{8,12},{12,8},{16,20},{20,16},{24,28},{28,24},{1,5},{5... | collective-permute-start | bytes 294920 | tf_op jit(solution)/shard_map/ppermute | solution.py:597
  43.1 8.2 %collective-permute-start.5 = (f32[3,32,256]{2,1,0:T(8,128)S(1)}, f32[3,32,256]{2,1,0:T(8,128)S(1)}, u32[]{:S(2)}, u32[]{:S(2)}) collective-permute-start(f32[3,32,256]{2,1,0:T(8,128)S(1)} %get-tuple-element.65), channel_id=1, source_target_pairs={{0,28},{4,8},{8,4},{12,16},{16,12},{20,24},{24,20},{28,0},{1,29},{... | collective-permute-start | bytes 294920 | tf_op jit(solution)/shard_map/ppermute | solution.py:596
  46.4 4.9 %collective-permute-start.6 = (f32[3,8,256]{2,1,0:T(8,128)S(1)}, f32[3,8,256]{2,1,0:T(8,128)S(1)}, u32[]{:S(2)}, u32[]{:S(2)}) collective-permute-start(f32[3,8,256]{2,1,0:T(8,128)S(1)} %get-tuple-element.66), channel_id=1, source_target_pairs={{0,1},{1,0},{2,3},{3,2},{4,5},{5,4},{6,7},{7,6},{8,9},{9,8},{10,11... | collective-permute-start | bytes 73736 | tf_op jit(solution)/shard_map/ppermute | solution.py:599
  46.4 4.9 %collective-permute-start.7 = (f32[3,8,256]{2,1,0:T(8,128)S(1)}, f32[3,8,256]{2,1,0:T(8,128)S(1)}, u32[]{:S(2)}, u32[]{:S(2)}) collective-permute-start(f32[3,8,256]{2,1,0:T(8,128)S(1)} %get-tuple-element.67), channel_id=1, source_target_pairs={{0,3},{1,2},{2,1},{3,0},{4,7},{5,6},{6,5},{7,4},{8,11},{9,10},{10,... | collective-permute-start | bytes 73736 | tf_op jit(solution)/shard_map/ppermute | solution.py:598
  53.1 11.1 %all-to-all-start.2 = ((f32[32,4,128]{2,1,0:T(4,128)}), f32[32,4,128]{2,1,0:T(4,128)S(1)}, u32[]{:S(2)}, u32[]{:S(2)}) async-start(f32[32,4,128]{2,1,0:T(4,128)} %get-tuple-element.73), calls=%async_computation.2 | async-start | bytes 131072 | tf_op jit(solution)/shard_map/all_to_all | solution.py:680

commit v5 on v4

--- a/solution.py
+++ b/solution.py
@@ -116,14 +116,14 @@
     ]
     for copy in copies:
         copy.start()
-    bodies, width = msg_ref.shape[0], msg_ref.shape[1]
+    bodies = msg_ref.shape[0]
     blocks = own_ref.shape[0]
     odd_total = blocks // 2
-    cap = width - odd_total
     pairs = table_ref.shape[1]
+    cap = pairs // bodies
+    slots = cap + odd_total
     points = own_ref.shape[2]
     lane = lax.broadcasted_iota(I32, (1, points), 1)
-    row = lax.broadcasted_iota(I32, (8, points), 0)
     edge = lax.broadcasted_iota(I32, (4, points), 0) == 3
     for copy in copies[:4]:
         copy.wait()
@@ -143,8 +143,9 @@
     for k in range(blocks):
         tile = jnp.concatenate([pt_ref[c, k : k + 1, :] for c in range(3)] + [blank], axis=0)
         own_ref[k] = target_rows(measured(jnp.where(lane < cnt_ref[k], tile, -FAR), edge))
-        sent_ref[k, 4:8, :] = measured(jnp.where(lane < cnt_ref[k], tile, FAR), edge)
-        sent_ref[k, 3:4, :] = blank
+        tile = jnp.where(lane < cnt_ref[k], tile, FAR)
+        sent_ref[k, 1, 1:2, :] = tile[0:1]
+        sent_ref[k, 2] = tile[1:3]
         move_ref[k, 3:4, :] = blank + 1.0
     for copy in copies[4:]:
         copy.wait()
@@ -155,16 +156,17 @@
         for b in range(per):
             part = line[:, b * points : (b + 1) * points]
             move_ref[j * per + b, c : c + 1, :] = part
-            sent_ref[j * per + b, c : c + 1, :] = part
+            sent_ref[j * per + b, c // 2, c % 2 : c % 2 + 1, :] = part
 
     gather_into(lambda c: r_ref[c].reshape(rows, depth), rows, depth, map_ref, both_ref, write)
 
     def pack(d, carry):
         for s in range(cap):
             second = table_ref[1, d * cap + s].astype(F32)
-            msg_ref[d, s] = jnp.where(row == 3, second, sent_ref[table_ref[0, d * cap + s]])
+            msg_ref[d, 3 * s : 3 * s + 3] = sent_ref[table_ref[0, d * cap + s]]
+            msg_ref[d, 3 * slots + s // 2, s % 2 : s % 2 + 1, :] = jnp.full((1, points), second)
         for j in range(odd_total):
-            msg_ref[d, cap + j] = sent_ref[2 * j + 1]
+            msg_ref[d, 3 * (cap + j) : 3 * (cap + j) + 3] = sent_ref[2 * j + 1]
         return carry
 
     lax.fori_loop(0, bodies, pack, 0)
@@ -209,7 +211,7 @@
 
 def weigh(tile, target):
     squared = lax.dot_general(
-        source_rows(tile[4:8]), target, (((0,), (0,)), ((), ())), preferred_element_type=F32
+        source_rows(tile), target, (((0,), (0,)), ((), ())), preferred_element_type=F32
     )
     q = 1.0 - 1.0 / squared
     weight = barrier_scale * (-2.0 * jnp.log(squared) - 4.0 * q + q * q)
@@ -228,9 +230,18 @@
     got_ref, own_ref, table_ref, move_ref, next_ref,
     force_ref, sum_ref, msg_ref, target_ref, w_hbm, w_ref, acc_ref, sem,
 ):
-    bodies, width = got_ref.shape[0], got_ref.shape[1]
+    bodies = got_ref.shape[0]
     blocks, _, points = move_ref.shape
-    cap = width - blocks // 2
+    cap = table_ref.shape[1] // bodies
+    slots = cap + blocks // 2
+    one = jnp.ones((1, points), F32)
+
+    def received(d, slot):
+        parts = got_ref[d, pl.ds(3 * slot, 3)]
+        moves = jnp.concatenate([parts[0], parts[1, 0:1], one], axis=0)
+        tile = jnp.concatenate([parts[1, 1:2], parts[2], one], axis=0)
+        return moves, measured(tile, edge)
+
     acc_ref[...] = jnp.zeros_like(acc_ref)
 
     edge = lax.broadcasted_iota(I32, (4, points), 0) == 3
@@ -240,7 +251,9 @@
 
     def find(d, carry):
         for s in range(cap):
-            target_ref[d * cap + s] = jnp.max(got_ref[d, s, 3:4, :]).astype(I32)
+            target_ref[d * cap + s] = jnp.max(
+                got_ref[d, 3 * slots + s // 2, s % 2 : s % 2 + 1, :]
+            ).astype(I32)
         return carry
 
     lax.fori_loop(0, bodies, find, 0, unroll=8)
@@ -249,16 +262,16 @@
         work = []
         for s in range(cap):
             n = d * cap + s
-            work.append((got_ref[d, s], target_ref[n]))
+            work.append((received(d, s), target_ref[n]))
             first = table_ref[0, n]
             odd = lax.shift_right_logical(table_ref[1, n], 1)
-            work.append((got_ref[d, cap + odd], first))
+            work.append((received(d, cap + odd), first))
         parts = []
-        for k, (tile, at) in enumerate(work):
+        for k, ((moves, tile), at) in enumerate(work):
             high, low = split(weigh(tile, own_ref[at]))
             both = jnp.concatenate([high, low], axis=1)
             w_ref[d, k] = both
-            parts.append(pair_part(jnp.where(edge, 1.0, tile[0:4]), both))
+            parts.append(pair_part(moves, both))
         for (_, at), part in zip(work, parts):
             acc_ref[at] = acc_ref[at] + part
         keep(d).start()
@@ -642,11 +655,11 @@
         open_kernel, "open", [HBM] * 8, [VMEM] * 12 + [SMEM],
         (vector,) + cells + (sds(cell_maps.shape, I32),) + faces(5)
         + (sds((blocks, 32, width), BF16), moves)
-        + (sds((bodies, slots, 8, width)), sds((2, pairs), I32)),
+        + (sds((bodies, 3 * slots + (cap + 1) // 2, 2, width)), sds((2, pairs), I32)),
         scratch=(
             pltpu.VMEM(points.shape, F32), pltpu.SMEM(counts.shape, I32),
             pltpu.SMEM(pair_table.shape, I32), pltpu.SMEM((bodies,), I32),
-            pltpu.VMEM((blocks, 8, width), F32), both, dma((10,)),
+            pltpu.VMEM((blocks, 3, 2, width), F32), both, dma((10,)),
         ), cost=4.0,
     )(*in_hbm(cotangent, shear, lame, inertia, points, counts, pair_table, cell_maps))
     got = lax.all_to_all(message, "body", 0, 0, tiled=True)

time: 65.9 us -> 65.2 us (0.989)
  waiting for transfers between devices: 13.6 us -> 12.2 us
    ppermute x2, waiting for transfers between devices: 3.29 us -> 2.52 us  [exchange(): got_xe = lax.ppermute(xe, 'body', pairs('body', 0))]
  transfers between devices with their start and end apart: 11 -> 11, of which waited for: 4 -> 4; matrix products, arithmetic and copies ran while one was open for 0% -> 0% of each run, Pallas kernels for 15% -> 16%
where the time goes in v5:
time: 65.2 us; the launch traced here: 64.8 us
  starting transfers between devices  28.6 us (44%)
  Pallas kernels  23.3 us (36%)
  waiting for transfers between devices  12.2 us (19%)
  between operations  0.73 us (1%)
    all_to_all x2, starting transfers between devices, on_device(): got = lax.all_to_all(message, 'body', 0, 0, tiled=True)  11 us
    ppermute x2, starting transfers between devices, exchange(): got_xo = lax.ppermute(xo, 'body', pairs('body', 1))  6.53 us
    pallas_call x1, Pallas kernels, on_device(): call(forces_one_kernel, 'forces_one', [VMEM] * 2 + [SMEM] + [VMEM] * 2, [...  5.58 us
    all_to_all x1, waiting for transfers between devices, on_device(): sums = lax.all_to_all(partial, ('body', 'across'), 0, 0, tiled=True)  5.54 us
    pallas_call x1, Pallas kernels, on_device(): call(open_kernel, 'open', [HBM] * 8, [VMEM] * 12 + [SMEM], (vector,) + ce...  4.48 us
    ppermute x2, starting transfers between devices, exchange(): got_xe = lax.ppermute(xe, 'body', pairs('body', 0))  4.11 us
    all_to_all x1, starting transfers between devices, on_device(): sums = lax.all_to_all(partial, ('body', 'across'), 0, 0, tiled=True)  3.69 us
    pallas_call x1, Pallas kernels, on_device(): call(forces_two_kernel, 'forces_two', [VMEM] + [SMEM] * 2 + [VMEM] + [HBM...  3.25 us
  transfers between devices with their start and end apart: 11, of which 4 were waited for; matrix products, arithmetic and copies ran while one was open for 0% of the time, Pallas kernels for 16%

profile of v5, /device:TPU:0, one launch (start us, length us, event | category | flops | bytes accessed | tf_op | source)
XLA Modules:
  0.0 64.8 jit_solution(7058359633240621760)
XLA Ops:
  0.6 4.5 %open.1 = (f32[3,8,32,256]{3,2,1,0:T(8,128)S(1)}, f32[8,32,256]{2,1,0:T(8,128)S(1)}, f32[8,32,256]{2,1,0:T(8,128)S(1)}, f32[8,32,256]{2,1,0:T(8,128)S(1)}, s32[8...) custom-call(f32[3,8,32,256]{3,2,1,0:T(8,128)} %r_hbm.3, ...), custom_call_target="tpu_custom_call" | custom-call | flops 400000000 | bytes 12000000 | tf_op jit(solution)/shard_map/open/pallas_call | solution.py:654
  5.1 7.3 %all-to-all-start = ((f32[8,38,2,128]{3,2,1,0:T(2,128)}), f32[8,38,2,128]{3,2,1,0:T(2,128)S(1)}, u32[]{:S(2)}, u32[]{:S(2)}) async-start(f32[8,38,2,128]{3,2,1,0:T(2,128)} %get-tuple-element.50), calls=%async_computation | async-start | bytes 622592 | tf_op jit(solution)/shard_map/all_to_all | solution.py:665
  12.4 2.0 %collective-permute-start = (f32[5,32,256]{2,1,0:T(8,128)S(1)}, f32[5,32,256]{2,1,0:T(8,128)S(1)}, u32[]{:S(2)}, u32[]{:S(2)}) collective-permute-start(f32[5,32,256]{2,1,0:T(8,128)S(1)} %get-tuple-element.42), channel_id=1, source_target_pairs={{0,4},{4,0},{8,12},{12,8},{16,20},{20,16},{24,28},{28,24},{1,5},{5... | collective-permute-start | bytes 491528 | tf_op jit(solution)/shard_map/ppermute | solution.py:610
  14.5 3.3 %collective-permute-start.1 = (f32[5,32,256]{2,1,0:T(8,128)S(1)}, f32[5,32,256]{2,1,0:T(8,128)S(1)}, u32[]{:S(2)}, u32[]{:S(2)}) collective-permute-start(f32[5,32,256]{2,1,0:T(8,128)S(1)} %get-tuple-element.43), channel_id=1, source_target_pairs={{0,28},{4,8},{8,4},{12,16},{16,12},{20,24},{24,20},{28,0},{1,29},{... | collective-permute-start | bytes 491528 | tf_op jit(solution)/shard_map/ppermute | solution.py:609
  17.7 0.0 collective-permute-start.2
  17.7 1.6 %collective-permute-start.3 = (f32[5,8,256]{2,1,0:T(8,128)S(1)}, f32[5,8,256]{2,1,0:T(8,128)S(1)}, u32[]{:S(2)}, u32[]{:S(2)}) collective-permute-start(f32[5,8,256]{2,1,0:T(8,128)S(1)} %get-tuple-element.45), channel_id=1, source_target_pairs={{0,3},{1,2},{2,1},{3,0},{4,7},{5,6},{6,5},{7,4},{8,11},{9,10},{10,... | collective-permute-start | bytes 122888 | tf_op jit(solution)/shard_map/ppermute | solution.py:611
  19.3 0.0 collective-permute-done.2.ye.cye
  19.3 1.8 %collective-permute-done.3.yo.cyo = f32[5,8,256]{2,1,0:T(8,128)S(1)} collective-permute-done((f32[5,8,256]{2,1,0:T(8,128)S(1)}, f32[5,8,256]{2,1,0:T(8,128)S(1)}, u32[]{:S(2)}, u32[]{:S(2)}) %collective-permute-start.3) | collective-permute-done | bytes 40992 | tf_op jit(solution)/shard_map/ppermute | solution.py:611
  21.2 2.5 %collective-permute-done.xe.cxe = f32[5,32,256]{2,1,0:T(8,128)S(1)} collective-permute-done((f32[5,32,256]{2,1,0:T(8,128)S(1)}, f32[5,32,256]{2,1,0:T(8,128)S(1)}, u32[]{:S(2)}, u32[]{:S(2)}) %collective-permute-start) | collective-permute-done | bytes 163872 | tf_op jit(solution)/shard_map/ppermute | solution.py:610
  23.7 2.3 %collective-permute-done.1.xo.cxo = f32[5,32,256]{2,1,0:T(8,128)S(1)} collective-permute-done((f32[5,32,256]{2,1,0:T(8,128)S(1)}, f32[5,32,256]{2,1,0:T(8,128)S(1)}, u32[]{:S(2)}, u32[]{:S(2)}) %collective-permute-start.1) | collective-permute-done | bytes 163872 | tf_op jit(solution)/shard_map/ppermute | solution.py:609
  26.0 3.1 %stencil_one.1 = (f32[8,32,256]{2,1,0:T(8,128)S(1)}, f32[8,32,256]{2,1,0:T(8,128)S(1)}, f32[8,32,256]{2,1,0:T(8,128)S(1)}, f32[17,4,128]{2,1,0:T(4,128)S(1)}) custom-call(f32[3,8,32,256]{3,2,1,0:T(8,128)S(1)} %get-tuple-element.38.r_ref, f32[8,32,256]{2,1,0:T(8,128)S(1)} %get-tuple-element.39.sh_ref, f32[8,32,256]{2,1,0:T(8,128)S(1)} %get-tuple-element.40.la_ref, ...), custom_call_target="tpu_custom_call" | custom-call | flops 500000000 | bytes 15000000 | tf_op jit(solution)/shard_map/stencil_one/pallas_call | solution.py:668
  29.1 0.0 all-to-all-done.got_ref
  29.1 5.6 %forces_one.1 = (f32[16,4,128]{2,1,0:T(4,128)S(1)}, f32[17,4,128]{2,1,0:T(4,128)S(1)}, f32[8,8,4,128]{3,2,1,0:T(4,128)}, s32[32]{0:T(128)S(1)}, bf16[8,8,128,256]{3,2,1,0:T(8,128)(2,1)}) custom-call(f32[8,38,2,128]{3,2,1,0:T(2,128)S(1)} %all-to-all-done.got_ref, bf16[16,32,128]{2,1,0:T(8,128)(2,1)S(1)} %get-tuple-element.51.own_ref, ...), custom_call_target="tpu_custom_call" | custom-call | flops 600000000 | bytes 18000000 | tf_op jit(solution)/shard_map/forces_one/pallas_call | solution.py:672
  34.7 3.7 %all-to-all-start.1 = ((f32[8,8,4,128]{3,2,1,0:T(4,128)}), f32[8,8,4,128]{3,2,1,0:T(4,128)S(1)}, u32[]{:S(2)}, u32[]{:S(2)}) async-start(f32[8,8,4,128]{3,2,1,0:T(4,128)} %get-tuple-element.57), calls=%async_computation.1 | async-start | bytes 262144 | tf_op jit(solution)/shard_map/all_to_all | solution.py:678
  38.4 1.9 %scatter_one.1 = (f32[3,8,32,256]{3,2,1,0:T(8,128)S(1)}, f32[3,32,256]{2,1,0:T(8,128)S(1)}, f32[3,32,256]{2,1,0:T(8,128)S(1)}, f32[3,8,256]{2,1,0:T(8,128)S(1)}, f32[3,8,256]{2,1,0:T(8,128)S(1)}) custom-call(f32[8,32,256]{2,1,0:T(8,128)S(1)} %get-tuple-element.47.e0_ref, f32[8,32,256]{2,1,0:T(8,128)S(1)} %get-tuple-element.48.e1_ref, ...), custom_call_target="tpu_custom_call" | custom-call | flops 300000000 | bytes 9000000 | tf_op jit(solution)/shard_map/scatter_one/pallas_call | solution.py:679
  40.3 2.1 %collective-permute-start.4 = (f32[3,32,256]{2,1,0:T(8,128)S(1)}, f32[3,32,256]{2,1,0:T(8,128)S(1)}, u32[]{:S(2)}, u32[]{:S(2)}) collective-permute-start(f32[3,32,256]{2,1,0:T(8,128)S(1)} %get-tuple-element.64), channel_id=1, source_target_pairs={{0,4},{4,0},{8,12},{12,8},{16,20},{20,16},{24,28},{28,24},{1,5},{5... | collective-permute-start | bytes 294920 | tf_op jit(solution)/shard_map/ppermute | solution.py:610
  42.4 3.3 %collective-permute-start.5 = (f32[3,32,256]{2,1,0:T(8,128)S(1)}, f32[3,32,256]{2,1,0:T(8,128)S(1)}, u32[]{:S(2)}, u32[]{:S(2)}) collective-permute-start(f32[3,32,256]{2,1,0:T(8,128)S(1)} %get-tuple-element.65), channel_id=1, source_target_pairs={{0,28},{4,8},{8,4},{12,16},{16,12},{20,24},{24,20},{28,0},{1,29},{... | collective-permute-start | bytes 294920 | tf_op jit(solution)/shard_map/ppermute | solution.py:609
  45.6 1.6 %collective-permute-start.7 = (f32[3,8,256]{2,1,0:T(8,128)S(1)}, f32[3,8,256]{2,1,0:T(8,128)S(1)}, u32[]{:S(2)}, u32[]{:S(2)}) collective-permute-start(f32[3,8,256]{2,1,0:T(8,128)S(1)} %get-tuple-element.67), channel_id=1, source_target_pairs={{0,3},{1,2},{2,1},{3,0},{4,7},{5,6},{6,5},{7,4},{8,11},{9,10},{10,... | collective-permute-start | bytes 73736 | tf_op jit(solution)/shard_map/ppermute | solution.py:611
  47.2 3.3 %forces_two.1 = (f32[16,4,128]{2,1,0:T(4,128)S(1)}, f32[4,128]{1,0:T(4,128)S(1)}, f32[8,32,256]{2,1,0:T(8,128)S(1)}, f32[8,32,256]{2,1,0:T(8,128)S(1)}, f32[8,32,256]{2,1,0:T(8,128)S(1)}) custom-call(f32[8,8,4,128]{3,2,1,0:T(4,128)S(1)} %all-to-all-done.1.got_ref, s32[32]{0:T(128)S(1)} %get-tuple-element.58.target_ref, ...), custom_call_target="tpu_custom_call" | custom-call | flops 300000000 | bytes 9000000 | tf_op jit(solution)/shard_map/forces_two/pallas_call | solution.py:684
  50.6 1.8 %stencil_two.1 = (f32[3,8,32,256]{3,2,1,0:T(8,128)S(1)}, f32[32,4,128]{2,1,0:T(4,128)}) custom-call(f32[3,8,32,256]{3,2,1,0:T(8,128)S(1)} %get-tuple-element.56.w1_ref, f32[8,32,256]{2,1,0:T(8,128)S(1)} %get-tuple-element.61.sh_ref, f32[8,32,256]{2,1,0:T(8,128)S(1)} %get-tuple-element.62.la_ref, f32[8,32,256]{2,1,0:T(8,128)S(1)} %get-tuple-element.63.in_ref, ...), custom_call_target="tpu_custom_call" | custom-call | flops 150000000 | bytes 4500000 | tf_op jit(solution)/shard_map/stencil_two/pallas_call | solution.py:689
  52.4 3.7 %all-to-all-start.2 = ((f32[32,4,128]{2,1,0:T(4,128)}), f32[32,4,128]{2,1,0:T(4,128)S(1)}, u32[]{:S(2)}, u32[]{:S(2)}) async-start(f32[32,4,128]{2,1,0:T(4,128)} %get-tuple-element.73), calls=%async_computation.2 | async-start | bytes 131072 | tf_op jit(solution)/shard_map/all_to_all | solution.py:693
  56.1 1.9 %scatter_two.1 = (f32[3,8,32,256]{3,2,1,0:T(8,128)S(1)}, f32[3,8,32,256]{3,2,1,0:T(8,128)S(1)}) custom-call(f32[3,8,32,256]{3,2,1,0:T(8,128)S(1)} %get-tuple-element.69.e_ref, f32[16,4,128]{2,1,0:T(4,128)S(1)} %get-tuple-element.70.force_ref, s32[8,1,256]{2,1,0:T(1,128)S(1)} %get-tuple-element.46.map_ref, f32[3,8,32,256]{3,2,1,0:T(8,128)} %r_hbm.3), custom_call_target="tpu_custom_call" | custom-call | flops 300000000 | bytes 9000000 | tf_op jit(solution)/shard_map/scatter_two/pallas_call | solution.py:694
  57.9 5.5 %all-to-all-done.2.red_ref = f32[32,4,128]{2,1,0:T(4,128)S(1)} async-done(((f32[32,4,128]{2,1,0:T(4,128)}), f32[32,4,128]{2,1,0:T(4,128)S(1)}, u32[]{:S(2)}, u32[]{:S(2)}) %all-to-all-start.2) | async-done | bytes 65568 | tf_op jit(solution)/shard_map/all_to_all | solution.py:693
  63.5 1.4 %final.1 = (f32[3,8,32,256]{3,2,1,0:T(8,128)}, f32[3,8,32,256]{3,2,1,0:T(8,128)}) custom-call(f32[3,8,32,256]{3,2,1,0:T(8,128)S(1)} %get-tuple-element.71.r_ref, f32[3,8,32,256]{3,2,1,0:T(8,128)S(1)} %get-tuple-element.56.w1_ref, f32[3,8,32,256]{3,2,1,0:T(8,128)S(1)} %get-tuple-element.72.w2_ref, f32[32,4,128]{2,1,0:T(4,128)S(1)} %all-to-all-done.2.red_ref), custom_call_target="tpu_custom_call" | custom-call | flops 100000000 | bytes 3000000 | tf_op jit(solution)/shard_map/final/pallas_call | solution.py:699
  (6 shorter events, 0.0 us)
Async XLA Ops:
  5.1 24.0 %all-to-all-start = ((f32[8,38,2,128]{3,2,1,0:T(2,128)}), f32[8,38,2,128]{3,2,1,0:T(2,128)S(1)}, u32[]{:S(2)}, u32[]{:S(2)}) async-start(f32[8,38,2,128]{3,2,1,0:T(2,128)} %get-tuple-element.50), calls=%async_computation | async-start | bytes 622592 | tf_op jit(solution)/shard_map/all_to_all | solution.py:665
  12.4 11.2 %collective-permute-start = (f32[5,32,256]{2,1,0:T(8,128)S(1)}, f32[5,32,256]{2,1,0:T(8,128)S(1)}, u32[]{:S(2)}, u32[]{:S(2)}) collective-permute-start(f32[5,32,256]{2,1,0:T(8,128)S(1)} %get-tuple-element.42), channel_id=1, source_target_pairs={{0,4},{4,0},{8,12},{12,8},{16,20},{20,16},{24,28},{28,24},{1,5},{5... | collective-permute-start | bytes 491528 | tf_op jit(solution)/shard_map/ppermute | solution.py:610
  14.5 11.5 %collective-permute-start.1 = (f32[5,32,256]{2,1,0:T(8,128)S(1)}, f32[5,32,256]{2,1,0:T(8,128)S(1)}, u32[]{:S(2)}, u32[]{:S(2)}) collective-permute-start(f32[5,32,256]{2,1,0:T(8,128)S(1)} %get-tuple-element.43), channel_id=1, source_target_pairs={{0,28},{4,8},{8,4},{12,16},{16,12},{20,24},{24,20},{28,0},{1,29},{... | collective-permute-start | bytes 491528 | tf_op jit(solution)/shard_map/ppermute | solution.py:609
  17.7 1.6 %collective-permute-start.2 = (f32[5,8,256]{2,1,0:T(8,128)S(1)}, f32[5,8,256]{2,1,0:T(8,128)S(1)}, u32[]{:S(2)}, u32[]{:S(2)}) collective-permute-start(f32[5,8,256]{2,1,0:T(8,128)S(1)} %get-tuple-element.44), channel_id=1, source_target_pairs={{0,1},{1,0},{2,3},{3,2},{4,5},{5,4},{6,7},{7,6},{8,9},{9,8},{10,11... | collective-permute-start | bytes 122888 | tf_op jit(solution)/shard_map/ppermute | solution.py:612
  17.7 3.4 %collective-permute-start.3 = (f32[5,8,256]{2,1,0:T(8,128)S(1)}, f32[5,8,256]{2,1,0:T(8,128)S(1)}, u32[]{:S(2)}, u32[]{:S(2)}) collective-permute-start(f32[5,8,256]{2,1,0:T(8,128)S(1)} %get-tuple-element.45), channel_id=1, source_target_pairs={{0,3},{1,2},{2,1},{3,0},{4,7},{5,6},{6,5},{7,4},{8,11},{9,10},{10,... | collective-permute-start | bytes 122888 | tf_op jit(solution)/shard_map/ppermute | solution.py:611
  34.7 12.5 %all-to-all-start.1 = ((f32[8,8,4,128]{3,2,1,0:T(4,128)}), f32[8,8,4,128]{3,2,1,0:T(4,128)S(1)}, u32[]{:S(2)}, u32[]{:S(2)}) async-start(f32[8,8,4,128]{3,2,1,0:T(4,128)} %get-tuple-element.57), calls=%async_computation.1 | async-start | bytes 262144 | tf_op jit(solution)/shard_map/all_to_all | solution.py:678
  40.3 10.3 %collective-permute-start.4 = (f32[3,32,256]{2,1,0:T(8,128)S(1)}, f32[3,32,256]{2,1,0:T(8,128)S(1)}, u32[]{:S(2)}, u32[]{:S(2)}) collective-permute-start(f32[3,32,256]{2,1,0:T(8,128)S(1)} %get-tuple-element.64), channel_id=1, source_target_pairs={{0,4},{4,0},{8,12},{12,8},{16,20},{20,16},{24,28},{28,24},{1,5},{5... | collective-permute-start | bytes 294920 | tf_op jit(solution)/shard_map/ppermute | solution.py:610
  42.4 8.2 %collective-permute-start.5 = (f32[3,32,256]{2,1,0:T(8,128)S(1)}, f32[3,32,256]{2,1,0:T(8,128)S(1)}, u32[]{:S(2)}, u32[]{:S(2)}) collective-permute-start(f32[3,32,256]{2,1,0:T(8,128)S(1)} %get-tuple-element.65), channel_id=1, source_target_pairs={{0,28},{4,8},{8,4},{12,16},{16,12},{20,24},{24,20},{28,0},{1,29},{... | collective-permute-start | bytes 294920 | tf_op jit(solution)/shard_map/ppermute | solution.py:609
  45.6 4.9 %collective-permute-start.6 = (f32[3,8,256]{2,1,0:T(8,128)S(1)}, f32[3,8,256]{2,1,0:T(8,128)S(1)}, u32[]{:S(2)}, u32[]{:S(2)}) collective-permute-start(f32[3,8,256]{2,1,0:T(8,128)S(1)} %get-tuple-element.66), channel_id=1, source_target_pairs={{0,1},{1,0},{2,3},{3,2},{4,5},{5,4},{6,7},{7,6},{8,9},{9,8},{10,11... | collective-permute-start | bytes 73736 | tf_op jit(solution)/shard_map/ppermute | solution.py:612
  45.6 4.9 %collective-permute-start.7 = (f32[3,8,256]{2,1,0:T(8,128)S(1)}, f32[3,8,256]{2,1,0:T(8,128)S(1)}, u32[]{:S(2)}, u32[]{:S(2)}) collective-permute-start(f32[3,8,256]{2,1,0:T(8,128)S(1)} %get-tuple-element.67), channel_id=1, source_target_pairs={{0,3},{1,2},{2,1},{3,0},{4,7},{5,6},{6,5},{7,4},{8,11},{9,10},{10,... | collective-permute-start | bytes 73736 | tf_op jit(solution)/shard_map/ppermute | solution.py:611
  52.4 11.1 %all-to-all-start.2 = ((f32[32,4,128]{2,1,0:T(4,128)}), f32[32,4,128]{2,1,0:T(4,128)S(1)}, u32[]{:S(2)}, u32[]{:S(2)}) async-start(f32[32,4,128]{2,1,0:T(4,128)} %get-tuple-element.73), calls=%async_computation.2 | async-start | bytes 131072 | tf_op jit(solution)/shard_map/all_to_all | solution.py:693

commit v6 on v5

--- a/solution.py
+++ b/solution.py
@@ -77,7 +77,7 @@
     return row, cells - row * depth
 
 
-def gather_into(load, rows, depth, map_ref, both_ref, write):
+def gather_into(load, rows, depth, map_ref, both_ref, write, place=None):
     for c in range(3):
         high, low = split(load(c))
         both_ref[c * rows : (c + 1) * rows, 0:depth] = high
@@ -90,6 +90,7 @@
         row, deep = cell_parts(map_ref[j], depth)
         onehot = jnp.where(depth_iota == deep, 1.0, 0.0).astype(BF16)
         onehot = jnp.concatenate([onehot, onehot], axis=0)
+        row = row if place is None else place(row)
         picked = jnp.dot(both_ref[...], onehot, preferred_element_type=F32)
         here = row_iota == row
         for c in range(3):
@@ -337,13 +338,20 @@
 
 
 def scatter_one_kernel(
-    e0_ref, e1_ref, e2_ref, force_ref, map_ref,
+    e0_ref, e1_ref, e2_ref, face_ref, force_ref, map_ref,
     w1_ref, xe_ref, xo_ref, ye_ref, yo_ref, left_ref, right_ref,
 ):
     shape = e0_ref.shape
     spread = scatter_parts(shape[0] * shape[1], shape[2], map_ref, force_ref, left_ref, right_ref)
     for c, e_ref in enumerate((e0_ref, e1_ref, e2_ref)):
         w1_ref[c] = e_ref[...] + spread(c).reshape(shape)
+    rows, cols, _ = shape
+    for c in range(3):
+        w1_ref[c, 0] = w1_ref[c, 0] + face_ref[c, 0:cols]
+        w1_ref[c, rows - 1] = w1_ref[c, rows - 1] + face_ref[c, cols : 2 * cols]
+        for x in range(1, rows - 1):
+            for y, at in ((0, 2 * cols + x), (cols - 1, 2 * cols + rows + x)):
+                w1_ref[c, x, y : y + 1] = w1_ref[c, x, y : y + 1] + face_ref[c, at : at + 1]
     write_faces([(w1_ref, 0), (w1_ref, 1), (w1_ref, 2)], xe_ref, xo_ref, ye_ref, yo_ref)
 
 
@@ -359,7 +367,7 @@
     copy.wait()
 
 
-def elastic(v_ref, sh_ref, la_ref, in_ref, vector_halo, stiff_halo, emit):
+def elastic(v_ref, sh_ref, la_ref, in_ref, vector_halo, stiff_halo, emit, at_shear=3):
     rows, cols, depth = sh_ref.shape
     b, a = lax.axis_index("body"), lax.axis_index("across")
     bodies, acrosses = lax.axis_size("body"), lax.axis_size("across")
@@ -371,8 +379,9 @@
     keep_high = jnp.where(b + 1 != cut, 1.0, 0.0).astype(F32)
     y_low = jnp.where(a != 0, 1.0, 0.0).astype(F32)
     y_high = jnp.where(a != acrosses - 1, 1.0, 0.0).astype(F32)
-    vxe, vxo, vye, vyo = vector_halo
-    sxe, sxo, sye, syo = stiff_halo
+    inner = vector_halo is None
+    vxe, vxo, vye, vyo = (None,) * 4 if inner else vector_halo
+    sxe, sxo, sye, syo = (None,) * 4 if inner else stiff_halo
     row = lax.broadcasted_iota(I32, (cols, depth), 0)
     lane = lax.broadcasted_iota(I32, (cols, depth), 1)
     z_mask = jnp.where(lane == depth - 1, 0.0, 1.0)
@@ -389,7 +398,7 @@
     def x_halo(high):
         e, o = (sxe, sxo) if high else (sxo, sxe)
         there = x_high if high else x_low
-        shear, lame = pick(bpar, e[3], o[3]), pick(bpar, e[4], o[4])
+        shear, lame = pick(bpar, e[at_shear], o[at_shear]), pick(bpar, e[at_shear + 1], o[at_shear + 1])
         e, o = (vxe, vxo) if high else (vxo, vxe)
         values = [there * pick(bpar, e[c], o[c]) for c in range(3)]
         return stiffness(there * shear, there * lame), values
@@ -398,7 +407,7 @@
         e, o = (sye, syo) if high else (syo, sye)
         there = y_high if high else y_low
         at = slice(x, x + 1)
-        shear, lame = pick(apar, e[3, at], o[3, at]), pick(apar, e[4, at], o[4, at])
+        shear, lame = pick(apar, e[at_shear, at], o[at_shear, at]), pick(apar, e[at_shear + 1, at], o[at_shear + 1, at])
         e, o = (vye, vyo) if high else (vyo, vye)
         values = [there * pick(apar, e[c, at], o[c, at]) for c in range(3)]
         return stiffness(there * shear, there * lame), values
@@ -416,28 +425,74 @@
             (front if c == along else side) * (values[c] - far_values[c]) for c in range(3)
         ]
 
-    before = flux(x_halo(False), slab(0), 0, keep_low)
+    if in_ref is None:
+
+        def edge_rows(ref, y, lead=None):
+            at = (lambda x: ref[x, y : y + 1]) if lead is None else (lambda x: ref[lead, x, y : y + 1])
+            return jnp.concatenate([at(x) for x in range(rows)], axis=0)
+
+        def near(y):
+            stiff = stiffness(edge_rows(sh_ref, y), edge_rows(la_ref, y))
+            return stiff, [edge_rows(v_ref, y, c) for c in range(3)]
+
+        def far(high):
+            there = y_high if high else y_low
+            e, o = (sye, syo) if high else (syo, sye)
+            shear, lame = pick(apar, e[at_shear], o[at_shear]), pick(apar, e[at_shear + 1], o[at_shear + 1])
+            e, o = (vye, vyo) if high else (vyo, vye)
+            return stiffness(there * shear, there * lame), [there * pick(apar, e[c], o[c]) for c in range(3)]
+
+        x_first = [-value for value in flux(x_halo(False), slab(0), 0, keep_low)]
+        x_last = flux(slab(rows - 1), x_halo(True), 0, keep_high)
+        y_first, y_last = flux(near(0), far(False), 1, None), flux(near(cols - 1), far(True), 1, None)
+
+        def joined(value, c, x):
+            value = value + jnp.where(bottom, y_first[c][x : x + 1], 0.0)
+            return value + jnp.where(top, y_last[c][x : x + 1], 0.0)
+
+        x_first = [joined(x_first[c], c, 0) for c in range(3)]
+        x_last = [joined(x_last[c], c, rows - 1) for c in range(3)]
+        return x_first, x_last, y_first, y_last
+
+    before = None if inner else flux(x_halo(False), slab(0), 0, keep_low)
     here = slab(0)
     for x in range(rows):
-        after = slab(x + 1) if x + 1 < rows else x_halo(True)
-        out = flux(here, after, 0, None if x + 1 < rows else keep_high)
+        out = after = None
+        if x + 1 < rows or not inner:
+            after = slab(x + 1) if x + 1 < rows else x_halo(True)
+            out = flux(here, after, 0, None if x + 1 < rows else keep_high)
         (off, diag), values = here
         inertia = in_ref[x]
-        total = [inertia * values[c] + (out[c] - before[c]) for c in range(3)]
+        total = [inertia * values[c] for c in range(3)]
+        if out is not None:
+            total = [total[c] + out[c] for c in range(3)]
+        if before is not None:
+            total = [total[c] - before[c] for c in range(3)]
         before = out
 
         def up(value, edge):
             return jnp.where(top, edge, pltpu.roll(value, cols - 1, 0))
 
-        (h_off, h_diag), h_values = y_halo(True, x)
-        shifted = (up(off, h_off), up(diag, h_diag)), [up(values[c], h_values[c]) for c in range(3)]
-        out = flux(here, shifted, 1, None)
-        first = (off[0:1], diag[0:1]), [values[c][0:1] for c in range(3)]
-        edge = flux(y_halo(False, x), first, 1, None)
-        total = [
-            total[c] + (out[c] - jnp.where(bottom, edge[c], pltpu.roll(out[c], 1, 0)))
-            for c in range(3)
-        ]
+        if inner:
+
+            def down(value):
+                return pltpu.roll(value, cols - 1, 0)
+
+            shifted = (down(off), down(diag)), [down(values[c]) for c in range(3)]
+            out = [jnp.where(top, 0.0, value) for value in flux(here, shifted, 1, None)]
+            total = [total[c] + (out[c] - pltpu.roll(out[c], 1, 0)) for c in range(3)]
+        else:
+            (h_off, h_diag), h_values = y_halo(True, x)
+            shifted = (up(off, h_off), up(diag, h_diag)), [
+                up(values[c], h_values[c]) for c in range(3)
+            ]
+            out = flux(here, shifted, 1, None)
+            first = (off[0:1], diag[0:1]), [values[c][0:1] for c in range(3)]
+            edge = flux(y_halo(False, x), first, 1, None)
+            total = [
+                total[c] + (out[c] - jnp.where(bottom, edge[c], pltpu.roll(out[c], 1, 0)))
+                for c in range(3)
+            ]
 
         def right(value):
             return z_mask * pltpu.roll(value, depth - 1, 1)
@@ -454,7 +509,7 @@
 
 
 def stencil_one_kernel(
-    r_ref, sh_ref, la_ref, in_ref, xe, xo, ye, yo, map_ref,
+    r_ref, sh_ref, la_ref, in_ref, map_ref,
     e0_ref, e1_ref, e2_ref, next_ref, both_ref,
 ):
     e_refs = (e0_ref, e1_ref, e2_ref)
@@ -467,7 +522,7 @@
             sums[0] = sums[0] + fold(r * r)
             sums[1] = sums[1] + fold(r * total[c])
 
-    elastic(r_ref, sh_ref, la_ref, in_ref, (xe, xo, ye, yo), (xe, xo, ye, yo), emit)
+    elastic(r_ref, sh_ref, la_ref, in_ref, None, None, emit)
     rows, depth = e0_ref.shape[0] * e0_ref.shape[1], e0_ref.shape[2]
     points = next_ref.shape[2]
 
@@ -482,6 +537,56 @@
     lines = [jnp.sum(value, axis=0, keepdims=True) for value in sums]
     next_ref[blocks] = jnp.concatenate(lines + [jnp.zeros((2, points), F32)], axis=0)
     gather_into(lambda c: e_refs[c][...].reshape(rows, depth), rows, depth, map_ref, both_ref, write)
+
+
+def faces_one_kernel(
+    r_ref, sh_ref, la_ref, xe, xo, ye, yo, map_ref, inner_ref,
+    face_ref, next_ref, sxe, sxo, sye, syo, both_ref,
+):
+    _, rows, cols, depth = r_ref.shape
+    halo = (xe, xo, ye, yo)
+    for source, target in zip(halo, (sxe, sxo, sye, syo)):
+        for k in range(2):
+            target[k] = source[3 + k]
+    x_first, x_last, y_first, y_last = elastic(r_ref, sh_ref, la_ref, None, halo, halo, None)
+    blocks, points = next_ref.shape[0] - 1, next_ref.shape[2]
+    between = lax.broadcasted_iota(I32, (rows, depth), 0)
+    between = (between > 0) & (between < rows - 1)
+    product = jnp.zeros((1, 128), F32)
+    for c in range(3):
+        face_ref[c, 0:cols] = x_first[c]
+        face_ref[c, cols : 2 * cols] = x_last[c]
+        face_ref[c, 2 * cols : 2 * cols + rows] = y_first[c]
+        face_ref[c, 2 * cols + rows :] = y_last[c]
+        ends = r_ref[c, 0] * x_first[c] + r_ref[c, rows - 1] * x_last[c]
+        low = jnp.concatenate([r_ref[c, x, 0:1] for x in range(rows)], axis=0)
+        high = jnp.concatenate([r_ref[c, x, cols - 1 : cols] for x in range(rows)], axis=0)
+        sides = jnp.where(between, low * y_first[c] + high * y_last[c], 0.0)
+        for value in (ends, sides):
+            line = jnp.sum(value, axis=0, keepdims=True)
+            for k in range(depth // 128):
+                product = product + line[:, k * 128 : (k + 1) * 128]
+
+    def place(row):
+        x, y = cell_parts(row, cols)
+        at = jnp.where(y == cols - 1, 2 * cols + rows + x, -1)
+        at = jnp.where(y == 0, 2 * cols + x, at)
+        at = jnp.where(x == rows - 1, cols + y, at)
+        return jnp.where(x == 0, y, at)
+
+    def write(j, c, line):
+        per = line.shape[1] // points
+        for b in range(per):
+            k = j * per + b
+            next_ref[k, c : c + 1, :] = inner_ref[k, c : c + 1, :] + line[:, b * points : (b + 1) * points]
+
+    for k in range(blocks):
+        next_ref[k, 3:4, :] = jnp.zeros((1, points), F32)
+    line = lax.broadcasted_iota(I32, (4, points), 0)
+    next_ref[blocks] = inner_ref[blocks] + jnp.where(line == 1, product, 0.0)
+    gather_into(
+        lambda c: face_ref[c], face_ref.shape[1], depth, map_ref, both_ref, write, place
+    )
 
 
 def fold(value):
@@ -558,7 +663,7 @@
             sums[0] = sums[0] + fold(w * w)
             sums[1] = sums[1] + fold(w * total[c])
 
-    elastic(w1_ref, sh_ref, la_ref, in_ref, (xe, xo, ye, yo), (cxe, cxo, cye, cyo), emit)
+    elastic(w1_ref, sh_ref, la_ref, in_ref, (xe, xo, ye, yo), (cxe, cxo, cye, cyo), emit, 0)
     lines = [jnp.sum(value, axis=0, keepdims=True) for value in sums]
     blank = jnp.zeros_like(lines[0])
     line = dots_ref[...] + jnp.concatenate([blank, blank] + lines, axis=0)
@@ -665,10 +770,16 @@
     got = lax.all_to_all(message, "body", 0, 0, tiled=True)
     halo = exchange(xe, xo, ye, yo)
     grown = sds((blocks + 1, 4, width))
-    *elastic_one, next_moves = call(
-        stencil_one_kernel, "stencil_one", [VMEM] * 9, [VMEM] * 4, cells + (grown,),
+    *elastic_one, inner_moves = call(
+        stencil_one_kernel, "stencil_one", [VMEM] * 5, [VMEM] * 4, cells + (grown,),
         scratch=(both,), cost=5.0,
-    )(r, shear, lame, inertia, *halo, cell_maps)
+    )(r, shear, lame, inertia, cell_maps)
+    rim = 2 * (rows + cols)
+    face_one, next_moves, *stiff = call(
+        faces_one_kernel, "faces_one", [VMEM] * 9, [VMEM] * 6,
+        (sds((3, rim, depth)), grown) + faces(2),
+        scratch=(pltpu.VMEM((3 * rim, 2 * depth), BF16),), cost=1.0,
+    )(r, shear, lame, *halo, cell_maps, inner_moves)
     force_one, second_moves, message, targets, weights = call(
         forces_one_kernel, "forces_one", [VMEM] * 2 + [SMEM] + [VMEM] * 2,
         [VMEM] * 3 + [SMEM, HBM],
@@ -677,9 +788,9 @@
     )(got, own, table, first_moves, next_moves)
     got = lax.all_to_all(message, "body", 0, 0, tiled=True)
     w1, xe, xo, ye, yo = call(
-        scatter_one_kernel, "scatter_one", [VMEM] * 5, [VMEM] * 5, (vector,) + faces(3),
+        scatter_one_kernel, "scatter_one", [VMEM] * 6, [VMEM] * 5, (vector,) + faces(3),
         scratch=sides, cost=3.0, mib=16,
-    )(*elastic_one, force_one, cell_maps)
+    )(*elastic_one, face_one, force_one, cell_maps)
     halo_two = exchange(xe, xo, ye, yo)
     force_two, dots, shear, lame, inertia = call(
         forces_two_kernel, "forces_two", [VMEM] + [SMEM] * 2 + [VMEM] + [HBM] * 4, [VMEM] * 5,
@@ -689,7 +800,7 @@
     elastic_two, partial = call(
         stencil_two_kernel, "stencil_two", [VMEM] * 13, [VMEM] * 2, (vector, sds((devices, 4, 128))),
         cost=1.5,
-    )(w1, shear, lame, inertia, *halo_two, *halo, dots)
+    )(w1, shear, lame, inertia, *halo_two, *stiff, dots)
     sums = lax.all_to_all(partial, ("body", "across"), 0, 0, tiled=True)
     w2, r = call(
         scatter_two_kernel, "scatter_two", [VMEM] * 3 + [HBM], [VMEM] * 2, (vector, vector),

time: 65.2 us -> 63.2 us (0.969)
  waiting for transfers between devices: 12.2 us -> 9.26 us
  Pallas kernels: 23.3 us -> 24.3 us
    ppermute x2, waiting for transfers between devices: 1.82 us -> 0.01 us  [exchange(): got_yo = lax.ppermute(yo, 'across', pairs('across', 1))]
    ppermute x2, waiting for transfers between devices: 2.52 us -> 1.37 us  [exchange(): got_xe = lax.ppermute(xe, 'body', pairs('body', 0))]
    pallas_call x2 -> x3, Pallas kernels: 4.97 us -> 5.94 us  [the longest x1 2.94 us: on_device(): call(stencil_one_kernel, 'stencil_one', [VMEM] * 5, [VMEM] * 4, cells + (...]
  transfers between devices with their start and end apart: 11 -> 11, of which waited for: 4 -> 3; matrix products, arithmetic and copies ran while one was open for 0% -> 0% of each run, Pallas kernels for 16% -> 18%
where the time goes in v6:
time: 63.2 us; the launch traced here: 62.9 us
  starting transfers between devices  28.6 us (45%)
  Pallas kernels  24.3 us (38%)
  waiting for transfers between devices  9.26 us (15%)
  between operations  0.75 us (1%)
    all_to_all x2, starting transfers between devices, on_device(): got = lax.all_to_all(message, 'body', 0, 0, tiled=True)  11 us
    ppermute x2, starting transfers between devices, exchange(): got_xo = lax.ppermute(xo, 'body', pairs('body', 1))  6.53 us
    pallas_call x1, Pallas kernels, on_device(): call(forces_one_kernel, 'forces_one', [VMEM] * 2 + [SMEM] + [VMEM] * 2, [...  5.58 us
    all_to_all x1, waiting for transfers between devices, on_device(): sums = lax.all_to_all(partial, ('body', 'across'), 0, 0, tiled=True)  5.54 us
    pallas_call x1, Pallas kernels, on_device(): call(open_kernel, 'open', [HBM] * 8, [VMEM] * 12 + [SMEM], (vector,) + ce...  4.48 us
    ppermute x2, starting transfers between devices, exchange(): got_xe = lax.ppermute(xe, 'body', pairs('body', 0))  4.11 us
    all_to_all x1, starting transfers between devices, on_device(): sums = lax.all_to_all(partial, ('body', 'across'), 0, 0, tiled=True)  3.69 us
    pallas_call x1, Pallas kernels, on_device(): call(forces_two_kernel, 'forces_two', [VMEM] + [SMEM] * 2 + [VMEM] + [HBM...  3.25 us
  transfers between devices with their start and end apart: 11, of which 3 were waited for; matrix products, arithmetic and copies ran while one was open for 0% of the time, Pallas kernels for 18%

profile of v6, /device:TPU:0, one launch (start us, length us, event | category | flops | bytes accessed | tf_op | source)
XLA Modules:
  0.0 62.9 jit_solution(13661712784025176793)
XLA Ops:
  0.6 4.5 %open.1 = (f32[3,8,32,256]{3,2,1,0:T(8,128)S(1)}, f32[8,32,256]{2,1,0:T(8,128)S(1)}, f32[8,32,256]{2,1,0:T(8,128)S(1)}, f32[8,32,256]{2,1,0:T(8,128)S(1)}, s32[8...) custom-call(f32[3,8,32,256]{3,2,1,0:T(8,128)} %r_hbm.3, ...), custom_call_target="tpu_custom_call" | custom-call | flops 400000000 | bytes 12000000 | tf_op jit(solution)/shard_map/open/pallas_call | solution.py:759
  5.1 7.3 %all-to-all-start = ((f32[8,38,2,128]{3,2,1,0:T(2,128)}), f32[8,38,2,128]{3,2,1,0:T(2,128)S(1)}, u32[]{:S(2)}, u32[]{:S(2)}) async-start(f32[8,38,2,128]{3,2,1,0:T(2,128)} %get-tuple-element.58), calls=%async_computation | async-start | bytes 622592 | tf_op jit(solution)/shard_map/all_to_all | solution.py:770
  12.4 2.0 %collective-permute-start = (f32[5,32,256]{2,1,0:T(8,128)S(1)}, f32[5,32,256]{2,1,0:T(8,128)S(1)}, u32[]{:S(2)}, u32[]{:S(2)}) collective-permute-start(f32[5,32,256]{2,1,0:T(8,128)S(1)} %get-tuple-element.52), channel_id=1, source_target_pairs={{0,4},{4,0},{8,12},{12,8},{16,20},{20,16},{24,28},{28,24},{1,5},{5... | collective-permute-start | bytes 491528 | tf_op jit(solution)/shard_map/ppermute | solution.py:715
  14.5 3.3 %collective-permute-start.1 = (f32[5,32,256]{2,1,0:T(8,128)S(1)}, f32[5,32,256]{2,1,0:T(8,128)S(1)}, u32[]{:S(2)}, u32[]{:S(2)}) collective-permute-start(f32[5,32,256]{2,1,0:T(8,128)S(1)} %get-tuple-element.53), channel_id=1, source_target_pairs={{0,28},{4,8},{8,4},{12,16},{16,12},{20,24},{24,20},{28,0},{1,29},{... | collective-permute-start | bytes 491528 | tf_op jit(solution)/shard_map/ppermute | solution.py:714
  17.7 0.0 collective-permute-start.2
  17.7 1.6 %collective-permute-start.3 = (f32[5,8,256]{2,1,0:T(8,128)S(1)}, f32[5,8,256]{2,1,0:T(8,128)S(1)}, u32[]{:S(2)}, u32[]{:S(2)}) collective-permute-start(f32[5,8,256]{2,1,0:T(8,128)S(1)} %get-tuple-element.55), channel_id=1, source_target_pairs={{0,3},{1,2},{2,1},{3,0},{4,7},{5,6},{6,5},{7,4},{8,11},{9,10},{10,... | collective-permute-start | bytes 122888 | tf_op jit(solution)/shard_map/ppermute | solution.py:716
  19.3 2.9 %stencil_one.1 = (f32[8,32,256]{2,1,0:T(8,128)S(1)}, f32[8,32,256]{2,1,0:T(8,128)S(1)}, f32[8,32,256]{2,1,0:T(8,128)S(1)}, f32[17,4,128]{2,1,0:T(4,128)S(1)}) custom-call(f32[3,8,32,256]{3,2,1,0:T(8,128)S(1)} %get-tuple-element.44.r_ref, f32[8,32,256]{2,1,0:T(8,128)S(1)} %get-tuple-element.45.sh_ref, f32[8,32,256]{2,1,0:T(8,128)S(1)} %get-tuple-element.46.la_ref, ...), custom_call_target="tpu_custom_call" | custom-call | flops 500000000 | bytes 15000000 | tf_op jit(solution)/shard_map/stencil_one/pallas_call | solution.py:773
  22.3 0.0 collective-permute-done.3.yo
  22.3 1.4 %collective-permute-done.xe = f32[5,32,256]{2,1,0:T(8,128)S(1)} collective-permute-done((f32[5,32,256]{2,1,0:T(8,128)S(1)}, f32[5,32,256]{2,1,0:T(8,128)S(1)}, u32[]{:S(2)}, u32[]{:S(2)}) %collective-permute-start) | collective-permute-done | bytes 163872 | tf_op jit(solution)/shard_map/ppermute | solution.py:715
  23.7 2.3 %collective-permute-done.1.xo = f32[5,32,256]{2,1,0:T(8,128)S(1)} collective-permute-done((f32[5,32,256]{2,1,0:T(8,128)S(1)}, f32[5,32,256]{2,1,0:T(8,128)S(1)}, u32[]{:S(2)}, u32[]{:S(2)}) %collective-permute-start.1) | collective-permute-done | bytes 163872 | tf_op jit(solution)/shard_map/ppermute | solution.py:714
  26.0 1.1 %faces_one.1 = (f32[3,80,256]{2,1,0:T(8,128)S(1)}, f32[17,4,128]{2,1,0:T(4,128)S(1)}, f32[2,32,256]{2,1,0:T(8,128)S(1)}, f32[2,32,256]{2,1,0:T(8,128)S(1)}, f32[...) custom-call(f32[3,8,32,256]{3,2,1,0:T(8,128)S(1)} %get-tuple-element.44.r_ref, ...), custom_call_target="tpu_custom_call" | custom-call | flops 100000000 | bytes 3000000 | tf_op jit(solution)/shard_map/faces_one/pallas_call | solution.py:778
  27.1 0.0 all-to-all-done.got_ref
  27.1 5.6 %forces_one.1 = (f32[16,4,128]{2,1,0:T(4,128)S(1)}, f32[17,4,128]{2,1,0:T(4,128)S(1)}, f32[8,8,4,128]{3,2,1,0:T(4,128)}, s32[32]{0:T(128)S(1)}, bf16[8,8,128,256]{3,2,1,0:T(8,128)(2,1)}) custom-call(f32[8,38,2,128]{3,2,1,0:T(2,128)S(1)} %all-to-all-done.got_ref, bf16[16,32,128]{2,1,0:T(8,128)(2,1)S(1)} %get-tuple-element.59.own_ref, ...), custom_call_target="tpu_custom_call" | custom-call | flops 600000000 | bytes 18000000 | tf_op jit(solution)/shard_map/forces_one/pallas_call | solution.py:783
  32.7 3.7 %all-to-all-start.1 = ((f32[8,8,4,128]{3,2,1,0:T(4,128)}), f32[8,8,4,128]{3,2,1,0:T(4,128)S(1)}, u32[]{:S(2)}, u32[]{:S(2)}) async-start(f32[8,8,4,128]{3,2,1,0:T(4,128)} %get-tuple-element.65), calls=%async_computation.1 | async-start | bytes 262144 | tf_op jit(solution)/shard_map/all_to_all | solution.py:789
  36.4 1.9 %scatter_one.1 = (f32[3,8,32,256]{3,2,1,0:T(8,128)S(1)}, f32[3,32,256]{2,1,0:T(8,128)S(1)}, f32[3,32,256]{2,1,0:T(8,128)S(1)}, f32[3,8,256]{2,1,0:T(8,128)S(1)}, f32[3,8,256]{2,1,0:T(8,128)S(1)}) custom-call(f32[8,32,256]{2,1,0:T(8,128)S(1)} %get-tuple-element.49.e0_ref, f32[8,32,256]{2,1,0:T(8,128)S(1)} %get-tuple-element.50.e1_ref, ...), custom_call_target="tpu_custom_call" | custom-call | flops 300000000 | bytes 9000000 | tf_op jit(solution)/shard_map/scatter_one/pallas_call | solution.py:790
  38.3 2.1 %collective-permute-start.4 = (f32[3,32,256]{2,1,0:T(8,128)S(1)}, f32[3,32,256]{2,1,0:T(8,128)S(1)}, u32[]{:S(2)}, u32[]{:S(2)}) collective-permute-start(f32[3,32,256]{2,1,0:T(8,128)S(1)} %get-tuple-element.72), channel_id=1, source_target_pairs={{0,4},{4,0},{8,12},{12,8},{16,20},{20,16},{24,28},{28,24},{1,5},{5... | collective-permute-start | bytes 294920 | tf_op jit(solution)/shard_map/ppermute | solution.py:715
  40.4 3.3 %collective-permute-start.5 = (f32[3,32,256]{2,1,0:T(8,128)S(1)}, f32[3,32,256]{2,1,0:T(8,128)S(1)}, u32[]{:S(2)}, u32[]{:S(2)}) collective-permute-start(f32[3,32,256]{2,1,0:T(8,128)S(1)} %get-tuple-element.73), channel_id=1, source_target_pairs={{0,28},{4,8},{8,4},{12,16},{16,12},{20,24},{24,20},{28,0},{1,29},{... | collective-permute-start | bytes 294920 | tf_op jit(solution)/shard_map/ppermute | solution.py:714
  43.7 1.6 %collective-permute-start.7 = (f32[3,8,256]{2,1,0:T(8,128)S(1)}, f32[3,8,256]{2,1,0:T(8,128)S(1)}, u32[]{:S(2)}, u32[]{:S(2)}) collective-permute-start(f32[3,8,256]{2,1,0:T(8,128)S(1)} %get-tuple-element.75), channel_id=1, source_target_pairs={{0,3},{1,2},{2,1},{3,0},{4,7},{5,6},{6,5},{7,4},{8,11},{9,10},{10,... | collective-permute-start | bytes 73736 | tf_op jit(solution)/shard_map/ppermute | solution.py:716
  45.3 3.3 %forces_two.1 = (f32[16,4,128]{2,1,0:T(4,128)S(1)}, f32[4,128]{1,0:T(4,128)S(1)}, f32[8,32,256]{2,1,0:T(8,128)S(1)}, f32[8,32,256]{2,1,0:T(8,128)S(1)}, f32[8,32,256]{2,1,0:T(8,128)S(1)}) custom-call(f32[8,8,4,128]{3,2,1,0:T(4,128)S(1)} %all-to-all-done.1.got_ref, s32[32]{0:T(128)S(1)} %get-tuple-element.66.target_ref, ...), custom_call_target="tpu_custom_call" | custom-call | flops 300000000 | bytes 9000000 | tf_op jit(solution)/shard_map/forces_two/pallas_call | solution.py:795
  48.6 1.8 %stencil_two.1 = (f32[3,8,32,256]{3,2,1,0:T(8,128)S(1)}, f32[32,4,128]{2,1,0:T(4,128)}) custom-call(f32[3,8,32,256]{3,2,1,0:T(8,128)S(1)} %get-tuple-element.64.w1_ref, f32[8,32,256]{2,1,0:T(8,128)S(1)} %get-tuple-element.69.sh_ref, f32[8,32,256]{2,1,0:T(8,128)S(1)} %get-tuple-element.70.la_ref, f32[8,32,256]{2,1,0:T(8,128)S(1)} %get-tuple-element.71.in_ref, ...), custom_call_target="tpu_custom_call" | custom-call | flops 150000000 | bytes 4500000 | tf_op jit(solution)/shard_map/stencil_two/pallas_call | solution.py:800
  50.4 3.7 %all-to-all-start.2 = ((f32[32,4,128]{2,1,0:T(4,128)}), f32[32,4,128]{2,1,0:T(4,128)S(1)}, u32[]{:S(2)}, u32[]{:S(2)}) async-start(f32[32,4,128]{2,1,0:T(4,128)} %get-tuple-element.85), calls=%async_computation.2 | async-start | bytes 131072 | tf_op jit(solution)/shard_map/all_to_all | solution.py:804
  54.1 1.9 %scatter_two.1 = (f32[3,8,32,256]{3,2,1,0:T(8,128)S(1)}, f32[3,8,32,256]{3,2,1,0:T(8,128)S(1)}) custom-call(f32[3,8,32,256]{3,2,1,0:T(8,128)S(1)} %get-tuple-element.81.e_ref, f32[16,4,128]{2,1,0:T(4,128)S(1)} %get-tuple-element.82.force_ref, s32[8,1,256]{2,1,0:T(1,128)S(1)} %get-tuple-element.48.map_ref, f32[3,8,32,256]{3,2,1,0:T(8,128)} %r_hbm.3), custom_call_target="tpu_custom_call" | custom-call | flops 300000000 | bytes 9000000 | tf_op jit(solution)/shard_map/scatter_two/pallas_call | solution.py:805
  55.9 5.5 %all-to-all-done.2.red_ref = f32[32,4,128]{2,1,0:T(4,128)S(1)} async-done(((f32[32,4,128]{2,1,0:T(4,128)}), f32[32,4,128]{2,1,0:T(4,128)S(1)}, u32[]{:S(2)}, u32[]{:S(2)}) %all-to-all-start.2) | async-done | bytes 65568 | tf_op jit(solution)/shard_map/all_to_all | solution.py:804
  61.5 1.4 %final.1 = (f32[3,8,32,256]{3,2,1,0:T(8,128)}, f32[3,8,32,256]{3,2,1,0:T(8,128)}) custom-call(f32[3,8,32,256]{3,2,1,0:T(8,128)S(1)} %get-tuple-element.83.r_ref, f32[3,8,32,256]{3,2,1,0:T(8,128)S(1)} %get-tuple-element.64.w1_ref, f32[3,8,32,256]{3,2,1,0:T(8,128)S(1)} %get-tuple-element.84.w2_ref, f32[32,4,128]{2,1,0:T(4,128)S(1)} %all-to-all-done.2.red_ref), custom_call_target="tpu_custom_call" | custom-call | flops 100000000 | bytes 3000000 | tf_op jit(solution)/shard_map/final/pallas_call | solution.py:810
  (7 shorter events, 0.0 us)
Async XLA Ops:
  5.1 22.0 %all-to-all-start = ((f32[8,38,2,128]{3,2,1,0:T(2,128)}), f32[8,38,2,128]{3,2,1,0:T(2,128)S(1)}, u32[]{:S(2)}, u32[]{:S(2)}) async-start(f32[8,38,2,128]{3,2,1,0:T(2,128)} %get-tuple-element.58), calls=%async_computation | async-start | bytes 622592 | tf_op jit(solution)/shard_map/all_to_all | solution.py:770
  12.4 11.2 %collective-permute-start = (f32[5,32,256]{2,1,0:T(8,128)S(1)}, f32[5,32,256]{2,1,0:T(8,128)S(1)}, u32[]{:S(2)}, u32[]{:S(2)}) collective-permute-start(f32[5,32,256]{2,1,0:T(8,128)S(1)} %get-tuple-element.52), channel_id=1, source_target_pairs={{0,4},{4,0},{8,12},{12,8},{16,20},{20,16},{24,28},{28,24},{1,5},{5... | collective-permute-start | bytes 491528 | tf_op jit(solution)/shard_map/ppermute | solution.py:715
  14.5 11.5 %collective-permute-start.1 = (f32[5,32,256]{2,1,0:T(8,128)S(1)}, f32[5,32,256]{2,1,0:T(8,128)S(1)}, u32[]{:S(2)}, u32[]{:S(2)}) collective-permute-start(f32[5,32,256]{2,1,0:T(8,128)S(1)} %get-tuple-element.53), channel_id=1, source_target_pairs={{0,28},{4,8},{8,4},{12,16},{16,12},{20,24},{24,20},{28,0},{1,29},{... | collective-permute-start | bytes 491528 | tf_op jit(solution)/shard_map/ppermute | solution.py:714
  17.7 4.6 %collective-permute-start.2 = (f32[5,8,256]{2,1,0:T(8,128)S(1)}, f32[5,8,256]{2,1,0:T(8,128)S(1)}, u32[]{:S(2)}, u32[]{:S(2)}) collective-permute-start(f32[5,8,256]{2,1,0:T(8,128)S(1)} %get-tuple-element.54), channel_id=1, source_target_pairs={{0,1},{1,0},{2,3},{3,2},{4,5},{5,4},{6,7},{7,6},{8,9},{9,8},{10,11... | collective-permute-start | bytes 122888 | tf_op jit(solution)/shard_map/ppermute | solution.py:717
  17.7 4.6 %collective-permute-start.3 = (f32[5,8,256]{2,1,0:T(8,128)S(1)}, f32[5,8,256]{2,1,0:T(8,128)S(1)}, u32[]{:S(2)}, u32[]{:S(2)}) collective-permute-start(f32[5,8,256]{2,1,0:T(8,128)S(1)} %get-tuple-element.55), channel_id=1, source_target_pairs={{0,3},{1,2},{2,1},{3,0},{4,7},{5,6},{6,5},{7,4},{8,11},{9,10},{10,... | collective-permute-start | bytes 122888 | tf_op jit(solution)/shard_map/ppermute | solution.py:716
  32.7 12.6 %all-to-all-start.1 = ((f32[8,8,4,128]{3,2,1,0:T(4,128)}), f32[8,8,4,128]{3,2,1,0:T(4,128)S(1)}, u32[]{:S(2)}, u32[]{:S(2)}) async-start(f32[8,8,4,128]{3,2,1,0:T(4,128)} %get-tuple-element.65), calls=%async_computation.1 | async-start | bytes 262144 | tf_op jit(solution)/shard_map/all_to_all | solution.py:789
  38.3 10.3 %collective-permute-start.4 = (f32[3,32,256]{2,1,0:T(8,128)S(1)}, f32[3,32,256]{2,1,0:T(8,128)S(1)}, u32[]{:S(2)}, u32[]{:S(2)}) collective-permute-start(f32[3,32,256]{2,1,0:T(8,128)S(1)} %get-tuple-element.72), channel_id=1, source_target_pairs={{0,4},{4,0},{8,12},{12,8},{16,20},{20,16},{24,28},{28,24},{1,5},{5... | collective-permute-start | bytes 294920 | tf_op jit(solution)/shard_map/ppermute | solution.py:715
  40.4 8.2 %collective-permute-start.5 = (f32[3,32,256]{2,1,0:T(8,128)S(1)}, f32[3,32,256]{2,1,0:T(8,128)S(1)}, u32[]{:S(2)}, u32[]{:S(2)}) collective-permute-start(f32[3,32,256]{2,1,0:T(8,128)S(1)} %get-tuple-element.73), channel_id=1, source_target_pairs={{0,28},{4,8},{8,4},{12,16},{16,12},{20,24},{24,20},{28,0},{1,29},{... | collective-permute-start | bytes 294920 | tf_op jit(solution)/shard_map/ppermute | solution.py:714
  43.7 4.9 %collective-permute-start.6 = (f32[3,8,256]{2,1,0:T(8,128)S(1)}, f32[3,8,256]{2,1,0:T(8,128)S(1)}, u32[]{:S(2)}, u32[]{:S(2)}) collective-permute-start(f32[3,8,256]{2,1,0:T(8,128)S(1)} %get-tuple-element.74), channel_id=1, source_target_pairs={{0,1},{1,0},{2,3},{3,2},{4,5},{5,4},{6,7},{7,6},{8,9},{9,8},{10,11... | collective-permute-start | bytes 73736 | tf_op jit(solution)/shard_map/ppermute | solution.py:717
  43.7 4.9 %collective-permute-start.7 = (f32[3,8,256]{2,1,0:T(8,128)S(1)}, f32[3,8,256]{2,1,0:T(8,128)S(1)}, u32[]{:S(2)}, u32[]{:S(2)}) collective-permute-start(f32[3,8,256]{2,1,0:T(8,128)S(1)} %get-tuple-element.75), channel_id=1, source_target_pairs={{0,3},{1,2},{2,1},{3,0},{4,7},{5,6},{6,5},{7,4},{8,11},{9,10},{10,... | collective-permute-start | bytes 73736 | tf_op jit(solution)/shard_map/ppermute | solution.py:716
  50.4 11.1 %all-to-all-start.2 = ((f32[32,4,128]{2,1,0:T(4,128)}), f32[32,4,128]{2,1,0:T(4,128)S(1)}, u32[]{:S(2)}, u32[]{:S(2)}) async-start(f32[32,4,128]{2,1,0:T(4,128)} %get-tuple-element.85), calls=%async_computation.2 | async-start | bytes 131072 | tf_op jit(solution)/shard_map/all_to_all | solution.py:804

commit v7 on v6

--- a/solution.py
+++ b/solution.py
@@ -143,7 +143,7 @@
     blank = jnp.zeros((1, points), F32)
     for k in range(blocks):
         tile = jnp.concatenate([pt_ref[c, k : k + 1, :] for c in range(3)] + [blank], axis=0)
-        own_ref[k] = target_rows(measured(jnp.where(lane < cnt_ref[k], tile, -FAR), edge))
+        own_ref[k] = measured(jnp.where(lane < cnt_ref[k], tile, -FAR), edge)
         tile = jnp.where(lane < cnt_ref[k], tile, FAR)
         sent_ref[k, 1, 1:2, :] = tile[0:1]
         sent_ref[k, 2] = tile[1:3]
@@ -229,7 +229,7 @@
 
 def forces_one_kernel(
     got_ref, own_ref, table_ref, move_ref, next_ref,
-    force_ref, sum_ref, msg_ref, target_ref, w_hbm, w_ref, acc_ref, sem,
+    force_ref, sum_ref, msg_ref, target_ref, w_hbm, w_ref, acc_ref, right_ref, sem,
 ):
     bodies = got_ref.shape[0]
     blocks, _, points = move_ref.shape
@@ -243,6 +243,8 @@
         tile = jnp.concatenate([parts[1, 1:2], parts[2], one], axis=0)
         return moves, measured(tile, edge)
 
+    for k in range(blocks):
+        right_ref[k] = target_rows(own_ref[k])
     acc_ref[...] = jnp.zeros_like(acc_ref)
 
     edge = lax.broadcasted_iota(I32, (4, points), 0) == 3
@@ -269,7 +271,7 @@
             work.append((received(d, cap + odd), first))
         parts = []
         for k, ((moves, tile), at) in enumerate(work):
-            high, low = split(weigh(tile, own_ref[at]))
+            high, low = split(weigh(tile, right_ref[at]))
             both = jnp.concatenate([high, low], axis=1)
             w_ref[d, k] = both
             parts.append(pair_part(moves, both))
@@ -338,33 +340,44 @@
 
 
 def scatter_one_kernel(
-    e0_ref, e1_ref, e2_ref, face_ref, force_ref, map_ref,
-    w1_ref, xe_ref, xo_ref, ye_ref, yo_ref, left_ref, right_ref,
-):
+    e0_ref, e1_ref, e2_ref, face_ref, force_ref, map_ref, sh_hbm, la_hbm, in_hbm_ref,
+    w1_ref, xe_ref, xo_ref, ye_ref, yo_ref, sh_ref, la_ref, in_ref, left_ref, right_ref, sem,
+):
+    cells = [
+        pltpu.make_async_copy(source, target, sem.at[k])
+        for k, (source, target) in enumerate(
+            [(sh_hbm, sh_ref), (la_hbm, la_ref), (in_hbm_ref, in_ref)]
+        )
+    ]
+    for copy in cells:
+        copy.start()
     shape = e0_ref.shape
     spread = scatter_parts(shape[0] * shape[1], shape[2], map_ref, force_ref, left_ref, right_ref)
     for c, e_ref in enumerate((e0_ref, e1_ref, e2_ref)):
         w1_ref[c] = e_ref[...] + spread(c).reshape(shape)
-    rows, cols, _ = shape
-    for c in range(3):
-        w1_ref[c, 0] = w1_ref[c, 0] + face_ref[c, 0:cols]
-        w1_ref[c, rows - 1] = w1_ref[c, rows - 1] + face_ref[c, cols : 2 * cols]
-        for x in range(1, rows - 1):
-            for y, at in ((0, 2 * cols + x), (cols - 1, 2 * cols + rows + x)):
-                w1_ref[c, x, y : y + 1] = w1_ref[c, x, y : y + 1] + face_ref[c, at : at + 1]
+    add_faces(w1_ref, face_ref)
     write_faces([(w1_ref, 0), (w1_ref, 1), (w1_ref, 2)], xe_ref, xo_ref, ye_ref, yo_ref)
+    for copy in cells:
+        copy.wait()
 
 
 def scatter_two_kernel(
-    e_ref, force_ref, map_ref, r_hbm, w2_ref, r_ref, left_ref, right_ref, sem
-):
-    copy = pltpu.make_async_copy(r_hbm, r_ref, sem)
-    copy.start()
+    e_ref, face_ref, force_ref, map_ref, r_hbm,
+    w2_ref, r0_ref, r1_ref, r2_ref, left_ref, right_ref, sem,
+):
+    copies = [
+        pltpu.make_async_copy(r_hbm.at[c], target, sem.at[c])
+        for c, target in enumerate((r0_ref, r1_ref, r2_ref))
+    ]
+    for copy in copies:
+        copy.start()
     shape = e_ref.shape[1:]
     spread = scatter_parts(shape[0] * shape[1], shape[2], map_ref, force_ref, left_ref, right_ref)
     for c in range(3):
         w2_ref[c] = e_ref[c] + spread(c).reshape(shape)
-    copy.wait()
+    add_faces(w2_ref, face_ref)
+    for copy in copies:
+        copy.wait()
 
 
 def elastic(v_ref, sh_ref, la_ref, in_ref, vector_halo, stiff_halo, emit, at_shear=3):
@@ -539,17 +552,9 @@
     gather_into(lambda c: e_refs[c][...].reshape(rows, depth), rows, depth, map_ref, both_ref, write)
 
 
-def faces_one_kernel(
-    r_ref, sh_ref, la_ref, xe, xo, ye, yo, map_ref, inner_ref,
-    face_ref, next_ref, sxe, sxo, sye, syo, both_ref,
-):
-    _, rows, cols, depth = r_ref.shape
-    halo = (xe, xo, ye, yo)
-    for source, target in zip(halo, (sxe, sxo, sye, syo)):
-        for k in range(2):
-            target[k] = source[3 + k]
-    x_first, x_last, y_first, y_last = elastic(r_ref, sh_ref, la_ref, None, halo, halo, None)
-    blocks, points = next_ref.shape[0] - 1, next_ref.shape[2]
+def store_faces(v_ref, parts, face_ref):
+    _, rows, cols, depth = v_ref.shape
+    x_first, x_last, y_first, y_last = parts
     between = lax.broadcasted_iota(I32, (rows, depth), 0)
     between = (between > 0) & (between < rows - 1)
     product = jnp.zeros((1, 128), F32)
@@ -558,14 +563,39 @@
         face_ref[c, cols : 2 * cols] = x_last[c]
         face_ref[c, 2 * cols : 2 * cols + rows] = y_first[c]
         face_ref[c, 2 * cols + rows :] = y_last[c]
-        ends = r_ref[c, 0] * x_first[c] + r_ref[c, rows - 1] * x_last[c]
-        low = jnp.concatenate([r_ref[c, x, 0:1] for x in range(rows)], axis=0)
-        high = jnp.concatenate([r_ref[c, x, cols - 1 : cols] for x in range(rows)], axis=0)
+        ends = v_ref[c, 0] * x_first[c] + v_ref[c, rows - 1] * x_last[c]
+        low = jnp.concatenate([v_ref[c, x, 0:1] for x in range(rows)], axis=0)
+        high = jnp.concatenate([v_ref[c, x, cols - 1 : cols] for x in range(rows)], axis=0)
         sides = jnp.where(between, low * y_first[c] + high * y_last[c], 0.0)
         for value in (ends, sides):
             line = jnp.sum(value, axis=0, keepdims=True)
             for k in range(depth // 128):
                 product = product + line[:, k * 128 : (k + 1) * 128]
+    return product
+
+
+def add_faces(out_ref, face_ref):
+    _, rows, cols, _ = out_ref.shape
+    for c in range(3):
+        out_ref[c, 0] = out_ref[c, 0] + face_ref[c, 0:cols]
+        out_ref[c, rows - 1] = out_ref[c, rows - 1] + face_ref[c, cols : 2 * cols]
+        for x in range(1, rows - 1):
+            for y, at in ((0, 2 * cols + x), (cols - 1, 2 * cols + rows + x)):
+                out_ref[c, x, y : y + 1] = out_ref[c, x, y : y + 1] + face_ref[c, at : at + 1]
+
+
+def faces_one_kernel(
+    r_ref, sh_ref, la_ref, xe, xo, ye, yo, map_ref, inner_ref,
+    face_ref, next_ref, sxe, sxo, sye, syo, both_ref,
+):
+    _, rows, cols, depth = r_ref.shape
+    halo = (xe, xo, ye, yo)
+    for source, target in zip(halo, (sxe, sxo, sye, syo)):
+        for k in range(2):
+            target[k] = source[3 + k]
+    parts = elastic(r_ref, sh_ref, la_ref, None, halo, halo, None)
+    blocks, points = next_ref.shape[0] - 1, next_ref.shape[2]
+    product = store_faces(r_ref, parts, face_ref)
 
     def place(row):
         x, y = cell_parts(row, cols)
@@ -599,9 +629,9 @@
     return total
 
 
-def forces_two_kernel(
-    got_ref, target_ref, table_ref, move_ref, w_hbm, sh_hbm, la_hbm, in_hbm_ref,
-    force_ref, dots_ref, sh_ref, la_ref, in_ref, w_ref, acc_ref, sem, cell_sem,
+def apply_two_kernel(
+    w1_ref, sh_ref, la_ref, in_ref, got_ref, target_ref, table_ref, move_ref, w_hbm,
+    e_ref, force_ref, dots_ref, w_ref, acc_ref, sem,
 ):
     bodies, width = got_ref.shape[0], got_ref.shape[1]
     cap = width // 2
@@ -615,14 +645,16 @@
         return carry
 
     lax.fori_loop(0, bodies, begin, 0)
-    cells = [
-        pltpu.make_async_copy(source, target, cell_sem.at[k])
-        for k, (source, target) in enumerate(
-            [(sh_hbm, sh_ref), (la_hbm, la_ref), (in_hbm_ref, in_ref)]
-        )
-    ]
-    for copy in cells:
-        copy.start()
+    sums = [jnp.zeros((8, 128), F32) for _ in range(2)]
+
+    def emit(x, total):
+        for c in range(3):
+            e_ref[c, x] = total[c]
+            w = w1_ref[c, x]
+            sums[0] = sums[0] + fold(w * w)
+            sums[1] = sums[1] + fold(w * total[c])
+
+    elastic(w1_ref, sh_ref, la_ref, in_ref, None, None, emit)
     acc_ref[...] = jnp.zeros_like(acc_ref)
 
     def device(d, carry):
@@ -644,34 +676,28 @@
         force = moved * acc[3:4] - acc
         force_ref[k] = force
         inner = inner + moved * force
-    inner = jnp.sum(inner[0:3], axis=0, keepdims=True)
-    blank = jnp.zeros_like(inner)
-    dots_ref[...] = jnp.concatenate([move_ref[blocks][0:2], blank, inner], axis=0)
-    for copy in cells:
-        copy.wait()
-
-
-def stencil_two_kernel(
-    w1_ref, sh_ref, la_ref, in_ref, xe, xo, ye, yo, cxe, cxo, cye, cyo, dots_ref, e_ref, red_ref
-):
-    sums = [jnp.zeros((8, 128), F32) for _ in range(2)]
-
-    def emit(x, total):
-        for c in range(3):
-            e_ref[c, x] = total[c]
-            w = w1_ref[c, x]
-            sums[0] = sums[0] + fold(w * w)
-            sums[1] = sums[1] + fold(w * total[c])
-
-    elastic(w1_ref, sh_ref, la_ref, in_ref, (xe, xo, ye, yo), (cxe, cxo, cye, cyo), emit, 0)
     lines = [jnp.sum(value, axis=0, keepdims=True) for value in sums]
-    blank = jnp.zeros_like(lines[0])
-    line = dots_ref[...] + jnp.concatenate([blank, blank] + lines, axis=0)
+    lines[1] = lines[1] + jnp.sum(inner[0:3], axis=0, keepdims=True)
+    dots_ref[...] = jnp.concatenate([move_ref[blocks][0:2]] + lines, axis=0)
+
+
+def faces_two_kernel(
+    w1_ref, sh_ref, la_ref, xe, xo, ye, yo, cxe, cxo, cye, cyo, dots_ref, face_ref, red_ref
+):
+    parts = elastic(
+        w1_ref, sh_ref, la_ref, None, (xe, xo, ye, yo), (cxe, cxo, cye, cyo), None, 0
+    )
+    product = store_faces(w1_ref, parts, face_ref)
+    line = dots_ref[...]
+    line = line + jnp.where(lax.broadcasted_iota(I32, line.shape, 0) == 3, product, 0.0)
     for d in range(red_ref.shape[0]):
         red_ref[d] = line
 
 
-def final_kernel(r_ref, w1_ref, w2_ref, red_ref, x_hbm, res_hbm, x_ref, res_ref, sem):
+def final_kernel(
+    r0_ref, r1_ref, r2_ref, w1_ref, w2_ref, red_ref, x_hbm, res_hbm, x_ref, res_ref, sem
+):
+    r_refs = (r0_ref, r1_ref, r2_ref)
     line = jnp.sum(red_ref[...], axis=0)
     moment = [
         jnp.broadcast_to(jnp.sum(line[k : k + 1], axis=1, keepdims=True), (8, 128)) for k in range(4)
@@ -685,13 +711,13 @@
     next_step = norm / curve
     alpha = step + next_step * grown
     gamma = next_step * step
-    cols, depth = r_ref.shape[2], r_ref.shape[3]
+    _, rows, cols, depth = w1_ref.shape
     alpha = jnp.broadcast_to(alpha[0:1, 0:1], (cols, depth))
     gamma = jnp.broadcast_to(gamma[0:1, 0:1], (cols, depth))
     copies = []
     for c in range(3):
-        for x in range(r_ref.shape[1]):
-            r, w1 = r_ref[c, x], w1_ref[c, x]
+        for x in range(rows):
+            r, w1 = r_refs[c][x], w1_ref[c, x]
             x_ref[c, x] = alpha * r - gamma * w1
             res_ref[c, x] = r - alpha * w1 + gamma * w2_ref[c, x]
         copies.append(pltpu.make_async_copy(x_ref.at[c], x_hbm.at[c], sem.at[0, c]))
@@ -759,7 +785,7 @@
     r, shear, lame, inertia, cell_maps, xe, xo, ye, yo, own, first_moves, message, table = call(
         open_kernel, "open", [HBM] * 8, [VMEM] * 12 + [SMEM],
         (vector,) + cells + (sds(cell_maps.shape, I32),) + faces(5)
-        + (sds((blocks, 32, width), BF16), moves)
+        + (moves, moves)
         + (sds((bodies, 3 * slots + (cap + 1) // 2, 2, width)), sds((2, pairs), I32)),
         scratch=(
             pltpu.VMEM(points.shape, F32), pltpu.SMEM(counts.shape, I32),
@@ -784,33 +810,35 @@
         forces_one_kernel, "forces_one", [VMEM] * 2 + [SMEM] + [VMEM] * 2,
         [VMEM] * 3 + [SMEM, HBM],
         (moves, grown, sds((bodies, 2 * cap, 4, width)), sds((pairs,), I32), pltpu.HBM(kept, BF16)),
-        scratch=(pltpu.VMEM(kept, BF16), total, dma((bodies,))), cost=6.0, mib=kept_mib,
+        scratch=(
+            pltpu.VMEM(kept, BF16), total, pltpu.VMEM((blocks, 32, width), BF16), dma((bodies,))
+        ), cost=6.0, mib=kept_mib,
     )(got, own, table, first_moves, next_moves)
     got = lax.all_to_all(message, "body", 0, 0, tiled=True)
-    w1, xe, xo, ye, yo = call(
-        scatter_one_kernel, "scatter_one", [VMEM] * 6, [VMEM] * 5, (vector,) + faces(3),
-        scratch=sides, cost=3.0, mib=16,
-    )(*elastic_one, face_one, force_one, cell_maps)
+    w1, xe, xo, ye, yo, shear, lame, inertia = call(
+        scatter_one_kernel, "scatter_one", [VMEM] * 6 + [HBM] * 3, [VMEM] * 8,
+        (vector,) + faces(3) + cells, scratch=sides + (dma((3,)),), cost=3.0, mib=16,
+    )(*elastic_one, face_one, force_one, cell_maps, *in_hbm(*given))
     halo_two = exchange(xe, xo, ye, yo)
-    force_two, dots, shear, lame, inertia = call(
-        forces_two_kernel, "forces_two", [VMEM] + [SMEM] * 2 + [VMEM] + [HBM] * 4, [VMEM] * 5,
-        (moves, sds((4, 128))) + cells,
-        scratch=(pltpu.VMEM(kept, BF16), total, dma((bodies,)), dma((3,))), cost=3.0, mib=kept_mib,
-    )(got, targets, table, second_moves, *in_hbm(weights, *given))
-    elastic_two, partial = call(
-        stencil_two_kernel, "stencil_two", [VMEM] * 13, [VMEM] * 2, (vector, sds((devices, 4, 128))),
-        cost=1.5,
-    )(w1, shear, lame, inertia, *halo_two, *stiff, dots)
+    elastic_two, force_two, dots = call(
+        apply_two_kernel, "apply_two", [VMEM] * 5 + [SMEM] * 2 + [VMEM, HBM], [VMEM] * 3,
+        (vector, moves, sds((4, 128))),
+        scratch=(pltpu.VMEM(kept, BF16), total, dma((bodies,))), cost=3.0, mib=kept_mib,
+    )(w1, shear, lame, inertia, got, targets, table, second_moves, *in_hbm(weights))
+    face_two, partial = call(
+        faces_two_kernel, "faces_two", [VMEM] * 12, [VMEM] * 2,
+        (sds((3, rim, depth)), sds((devices, 4, 128))), cost=1.0,
+    )(w1, shear, lame, *halo_two, *stiff, dots)
     sums = lax.all_to_all(partial, ("body", "across"), 0, 0, tiled=True)
-    w2, r = call(
-        scatter_two_kernel, "scatter_two", [VMEM] * 3 + [HBM], [VMEM] * 2, (vector, vector),
-        scratch=sides + (dma(()),), cost=3.0, mib=16,
-    )(elastic_two, force_two, cell_maps, *in_hbm(cotangent))
+    w2, *parts = call(
+        scatter_two_kernel, "scatter_two", [VMEM] * 4 + [HBM], [VMEM] * 4, (vector,) + cells,
+        scratch=sides + (dma((3,)),), cost=3.0, mib=16,
+    )(elastic_two, face_two, force_two, cell_maps, *in_hbm(cotangent))
     out = pltpu.VMEM((3, rows, cols, depth), F32)
     return call(
-        final_kernel, "final", [VMEM] * 4, [HBM] * 2, (vector, vector),
+        final_kernel, "final", [VMEM] * 6, [HBM] * 2, (vector, vector),
         scratch=(out, out, dma((2, 3))), cost=1.0,
-    )(r, w1, w2, sums)
+    )(*parts, w1, w2, sums)
 
 
 def solution(mesh):

time: 63.2 us -> 62.3 us (0.986)
  Pallas kernels: 24.3 us -> 23.5 us
    pallas_call x5, Pallas kernels: 10.2 us -> 9.39 us  [the longest x1 3.3 us: on_device(): call(apply_two_kernel, 'apply_two', [VMEM] * 5 + [SMEM] * 2 + [VMEM, HBM]...]
where the time goes in v7:
time: 62.3 us; the launch traced here: 61.9 us
  starting transfers between devices  28.5 us (46%)
  Pallas kernels  23.5 us (38%)
  waiting for transfers between devices  9.23 us (15%)
  between operations  0.76 us (1%)
    all_to_all x2, starting transfers between devices, on_device(): got = lax.all_to_all(message, 'body', 0, 0, tiled=True)  11 us
    ppermute x2, starting transfers between devices, exchange(): got_xo = lax.ppermute(xo, 'body', pairs('body', 1))  6.53 us
    pallas_call x1, Pallas kernels, on_device(): call(forces_one_kernel, 'forces_one', [VMEM] * 2 + [SMEM] + [VMEM] * 2, [...  5.6 us
    all_to_all x1, waiting for transfers between devices, on_device(): sums = lax.all_to_all(partial, ('body', 'across'), 0, 0, tiled=True)  5.5 us
    pallas_call x1, Pallas kernels, on_device(): call(open_kernel, 'open', [HBM] * 8, [VMEM] * 12 + [SMEM], (vector,) + ce...  4.47 us
    ppermute x2, starting transfers between devices, exchange(): got_xe = lax.ppermute(xe, 'body', pairs('body', 0))  4.1 us
    all_to_all x1, starting transfers between devices, on_device(): sums = lax.all_to_all(partial, ('body', 'across'), 0, 0, tiled=True)  3.64 us
    pallas_call x1, Pallas kernels, on_device(): call(apply_two_kernel, 'apply_two', [VMEM] * 5 + [SMEM] * 2 + [VMEM, HBM]...  3.3 us
  transfers between devices with their start and end apart: 11, of which 3 were waited for; matrix products, arithmetic and copies ran while one was open for 0% of the time, Pallas kernels for 18%

profile of v7, /device:TPU:0, one launch (start us, length us, event | category | flops | bytes accessed | tf_op | source)
XLA Modules:
  0.0 61.9 jit_solution(14376232350824537648)
XLA Ops:
  0.6 4.5 %open.1 = (f32[3,8,32,256]{3,2,1,0:T(8,128)S(1)}, f32[8,32,256]{2,1,0:T(8,128)S(1)}, f32[8,32,256]{2,1,0:T(8,128)S(1)}, f32[8,32,256]{2,1,0:T(8,128)S(1)}, s32[8...) custom-call(f32[3,8,32,256]{3,2,1,0:T(8,128)} %r_hbm.3, ...), custom_call_target="tpu_custom_call" | custom-call | flops 400000000 | bytes 12000000 | tf_op jit(solution)/shard_map/open/pallas_call | solution.py:785
  5.1 7.3 %all-to-all-start = ((f32[8,38,2,128]{3,2,1,0:T(2,128)}), f32[8,38,2,128]{3,2,1,0:T(2,128)S(1)}, u32[]{:S(2)}, u32[]{:S(2)}) async-start(f32[8,38,2,128]{3,2,1,0:T(2,128)} %get-tuple-element.61), calls=%async_computation | async-start | bytes 622592 | tf_op jit(solution)/shard_map/all_to_all | solution.py:796
  12.4 2.0 %collective-permute-start = (f32[5,32,256]{2,1,0:T(8,128)S(1)}, f32[5,32,256]{2,1,0:T(8,128)S(1)}, u32[]{:S(2)}, u32[]{:S(2)}) collective-permute-start(f32[5,32,256]{2,1,0:T(8,128)S(1)} %get-tuple-element.55), channel_id=1, source_target_pairs={{0,4},{4,0},{8,12},{12,8},{16,20},{20,16},{24,28},{28,24},{1,5},{5... | collective-permute-start | bytes 491528 | tf_op jit(solution)/shard_map/ppermute | solution.py:741
  14.4 3.3 %collective-permute-start.1 = (f32[5,32,256]{2,1,0:T(8,128)S(1)}, f32[5,32,256]{2,1,0:T(8,128)S(1)}, u32[]{:S(2)}, u32[]{:S(2)}) collective-permute-start(f32[5,32,256]{2,1,0:T(8,128)S(1)} %get-tuple-element.56), channel_id=1, source_target_pairs={{0,28},{4,8},{8,4},{12,16},{16,12},{20,24},{24,20},{28,0},{1,29},{... | collective-permute-start | bytes 491528 | tf_op jit(solution)/shard_map/ppermute | solution.py:740
  17.7 1.6 %collective-permute-start.3 = (f32[5,8,256]{2,1,0:T(8,128)S(1)}, f32[5,8,256]{2,1,0:T(8,128)S(1)}, u32[]{:S(2)}, u32[]{:S(2)}) collective-permute-start(f32[5,8,256]{2,1,0:T(8,128)S(1)} %get-tuple-element.58), channel_id=1, source_target_pairs={{0,3},{1,2},{2,1},{3,0},{4,7},{5,6},{6,5},{7,4},{8,11},{9,10},{10,... | collective-permute-start | bytes 122888 | tf_op jit(solution)/shard_map/ppermute | solution.py:742
  19.3 2.9 %stencil_one.1 = (f32[8,32,256]{2,1,0:T(8,128)S(1)}, f32[8,32,256]{2,1,0:T(8,128)S(1)}, f32[8,32,256]{2,1,0:T(8,128)S(1)}, f32[17,4,128]{2,1,0:T(4,128)S(1)}) custom-call(f32[3,8,32,256]{3,2,1,0:T(8,128)S(1)} %get-tuple-element.47.r_ref, f32[8,32,256]{2,1,0:T(8,128)S(1)} %get-tuple-element.48.sh_ref, f32[8,32,256]{2,1,0:T(8,128)S(1)} %get-tuple-element.49.la_ref, ...), custom_call_target="tpu_custom_call" | custom-call | flops 500000000 | bytes 15000000 | tf_op jit(solution)/shard_map/stencil_one/pallas_call | solution.py:799
  22.3 0.0 collective-permute-done.2.ye
  22.3 1.4 %collective-permute-done.xe = f32[5,32,256]{2,1,0:T(8,128)S(1)} collective-permute-done((f32[5,32,256]{2,1,0:T(8,128)S(1)}, f32[5,32,256]{2,1,0:T(8,128)S(1)}, u32[]{:S(2)}, u32[]{:S(2)}) %collective-permute-start) | collective-permute-done | bytes 163872 | tf_op jit(solution)/shard_map/ppermute | solution.py:741
  23.7 2.3 %collective-permute-done.1.xo = f32[5,32,256]{2,1,0:T(8,128)S(1)} collective-permute-done((f32[5,32,256]{2,1,0:T(8,128)S(1)}, f32[5,32,256]{2,1,0:T(8,128)S(1)}, u32[]{:S(2)}, u32[]{:S(2)}) %collective-permute-start.1) | collective-permute-done | bytes 163872 | tf_op jit(solution)/shard_map/ppermute | solution.py:740
  26.0 1.1 %faces_one.1 = (f32[3,80,256]{2,1,0:T(8,128)S(1)}, f32[17,4,128]{2,1,0:T(4,128)S(1)}, f32[2,32,256]{2,1,0:T(8,128)S(1)}, f32[2,32,256]{2,1,0:T(8,128)S(1)}, f32[...) custom-call(f32[3,8,32,256]{3,2,1,0:T(8,128)S(1)} %get-tuple-element.47.r_ref, ...), custom_call_target="tpu_custom_call" | custom-call | flops 100000000 | bytes 3000000 | tf_op jit(solution)/shard_map/faces_one/pallas_call | solution.py:804
  27.1 5.6 %forces_one.1 = (f32[16,4,128]{2,1,0:T(4,128)S(1)}, f32[17,4,128]{2,1,0:T(4,128)S(1)}, f32[8,8,4,128]{3,2,1,0:T(4,128)}, s32[32]{0:T(128)S(1)}, bf16[8,8,128,256]{3,2,1,0:T(8,128)(2,1)}) custom-call(f32[8,38,2,128]{3,2,1,0:T(2,128)S(1)} %all-to-all-done.got_ref, f32[16,4,128]{2,1,0:T(4,128)S(1)} %get-tuple-element.62.own_ref, ...), custom_call_target="tpu_custom_call" | custom-call | flops 600000000 | bytes 18000000 | tf_op jit(solution)/shard_map/forces_one/pallas_call | solution.py:809
  32.7 3.7 %all-to-all-start.1 = ((f32[8,8,4,128]{3,2,1,0:T(4,128)}), f32[8,8,4,128]{3,2,1,0:T(4,128)S(1)}, u32[]{:S(2)}, u32[]{:S(2)}) async-start(f32[8,8,4,128]{3,2,1,0:T(4,128)} %get-tuple-element.71), calls=%async_computation.1 | async-start | bytes 262144 | tf_op jit(solution)/shard_map/all_to_all | solution.py:817
  36.4 2.0 %scatter_one.1 = (f32[3,8,32,256]{3,2,1,0:T(8,128)S(1)}, f32[3,32,256]{2,1,0:T(8,128)S(1)}, f32[3,32,256]{2,1,0:T(8,128)S(1)}, f32[3,8,256]{2,1,0:T(8,128)S(1)},...) custom-call(f32[8,32,256]{2,1,0:T(8,128)S(1)} %get-tuple-element.52., ...), custom_call_target="tpu_custom_call" | custom-call | flops 300000000 | bytes 9000000 | tf_op jit(solution)/shard_map/scatter_one/pallas_call | solution.py:818
  38.4 2.1 %collective-permute-start.4 = (f32[3,32,256]{2,1,0:T(8,128)S(1)}, f32[3,32,256]{2,1,0:T(8,128)S(1)}, u32[]{:S(2)}, u32[]{:S(2)}) collective-permute-start(f32[3,32,256]{2,1,0:T(8,128)S(1)} %get-tuple-element.76), channel_id=1, source_target_pairs={{0,4},{4,0},{8,12},{12,8},{16,20},{20,16},{24,28},{28,24},{1,5},{5... | collective-permute-start | bytes 294920 | tf_op jit(solution)/shard_map/ppermute | solution.py:741
  40.4 3.3 %collective-permute-start.5 = (f32[3,32,256]{2,1,0:T(8,128)S(1)}, f32[3,32,256]{2,1,0:T(8,128)S(1)}, u32[]{:S(2)}, u32[]{:S(2)}) collective-permute-start(f32[3,32,256]{2,1,0:T(8,128)S(1)} %get-tuple-element.77), channel_id=1, source_target_pairs={{0,28},{4,8},{8,4},{12,16},{16,12},{20,24},{24,20},{28,0},{1,29},{... | collective-permute-start | bytes 294920 | tf_op jit(solution)/shard_map/ppermute | solution.py:740
  43.7 0.0 collective-permute-start.6
  43.7 1.6 %collective-permute-start.7 = (f32[3,8,256]{2,1,0:T(8,128)S(1)}, f32[3,8,256]{2,1,0:T(8,128)S(1)}, u32[]{:S(2)}, u32[]{:S(2)}) collective-permute-start(f32[3,8,256]{2,1,0:T(8,128)S(1)} %get-tuple-element.79), channel_id=1, source_target_pairs={{0,3},{1,2},{2,1},{3,0},{4,7},{5,6},{6,5},{7,4},{8,11},{9,10},{10,... | collective-permute-start | bytes 73736 | tf_op jit(solution)/shard_map/ppermute | solution.py:742
  45.3 3.3 %apply_two.1 = (f32[3,8,32,256]{3,2,1,0:T(8,128)S(1)}, f32[16,4,128]{2,1,0:T(4,128)S(1)}, f32[4,128]{1,0:T(4,128)S(1)}) custom-call(f32[3,8,32,256]{3,2,1,0:T(8,128)S(1)} %get-tuple-element.67.w1_ref, f32[8,32,256]{2,1,0:T(8,128)S(1)} %get-tuple-element.68.sh_ref, f32[8,32,256]{2,1,0:T(8,128)S(1)} %get-tuple-element.69.la_ref, ...), custom_call_target="tpu_custom_call" | custom-call | flops 300000000 | bytes 9000000 | tf_op jit(solution)/shard_map/apply_two/pallas_call | solution.py:823
  48.6 0.0 collective-permute-done.6.ye
  48.7 0.8 %faces_two.1 = (f32[3,80,256]{2,1,0:T(8,128)S(1)}, f32[32,4,128]{2,1,0:T(4,128)}) custom-call(f32[3,8,32,256]{3,2,1,0:T(8,128)S(1)} %get-tuple-element.67.w1_ref, f32[8,32,256]{2,1,0:T(8,128)S(1)} %get-tuple-element.68.sh_ref, f32[8,32,256]{2,1,0:T(8,128)S(1)} %get-tuple-element.69.la_ref, f32[3,32,256]{2,1,0:T(8,128)S(1)} %collective-permute-done.4.xe, ...), custom_call_target="tpu_custom_call" | custom-call | flops 100000000 | bytes 3000000 | tf_op jit(solution)/shard_map/faces_two/pallas_call | solution.py:828
  49.5 3.6 %all-to-all-start.2 = ((f32[32,4,128]{2,1,0:T(4,128)}), f32[32,4,128]{2,1,0:T(4,128)S(1)}, u32[]{:S(2)}, u32[]{:S(2)}) async-start(f32[32,4,128]{2,1,0:T(4,128)} %get-tuple-element.91), calls=%async_computation.2 | async-start | bytes 131072 | tf_op jit(solution)/shard_map/all_to_all | solution.py:832
  53.2 1.9 %scatter_two.1 = (f32[3,8,32,256]{3,2,1,0:T(8,128)S(1)}, f32[8,32,256]{2,1,0:T(8,128)S(1)}, f32[8,32,256]{2,1,0:T(8,128)S(1)}, f32[8,32,256]{2,1,0:T(8,128)S(1)}) custom-call(f32[3,8,32,256]{3,2,1,0:T(8,128)S(1)} %get-tuple-element.75.e_ref, f32[3,80,256]{2,1,0:T(8,128)S(1)} %get-tuple-element.85.face_ref, f32[16,4,128]{2,1,0:T(4,128)S(1)} %get-tuple-element.86.force_ref, ...), custom_call_target="tpu_custom_call" | custom-call | flops 300000000 | bytes 9000000 | tf_op jit(solution)/shard_map/scatter_two/pallas_call | solution.py:833
  55.1 5.5 %all-to-all-done.2.red_ref = f32[32,4,128]{2,1,0:T(4,128)S(1)} async-done(((f32[32,4,128]{2,1,0:T(4,128)}), f32[32,4,128]{2,1,0:T(4,128)S(1)}, u32[]{:S(2)}, u32[]{:S(2)}) %all-to-all-start.2) | async-done | bytes 65568 | tf_op jit(solution)/shard_map/all_to_all | solution.py:832
  60.6 1.4 %final.1 = (f32[3,8,32,256]{3,2,1,0:T(8,128)}, f32[3,8,32,256]{3,2,1,0:T(8,128)}) custom-call(f32[8,32,256]{2,1,0:T(8,128)S(1)} %get-tuple-element.87.r0_ref, f32[8,32,256]{2,1,0:T(8,128)S(1)} %get-tuple-element.88.r1_ref, f32[8,32,256]{2,1,0:T(8,128)S(1)} %get-tuple-element.89.r2_ref, f32[3,8,32,256]{3,2,1,0:T(8,128)S(1)} %get-tuple-element.67.w1_ref, ...), custom_call_target="tpu_custom_call" | custom-call | flops 100000000 | bytes 3000000 | tf_op jit(solution)/shard_map/final/pallas_call | solution.py:838
  (7 shorter events, 0.0 us)
Async XLA Ops:
  5.1 22.0 %all-to-all-start = ((f32[8,38,2,128]{3,2,1,0:T(2,128)}), f32[8,38,2,128]{3,2,1,0:T(2,128)S(1)}, u32[]{:S(2)}, u32[]{:S(2)}) async-start(f32[8,38,2,128]{3,2,1,0:T(2,128)} %get-tuple-element.61), calls=%async_computation | async-start | bytes 622592 | tf_op jit(solution)/shard_map/all_to_all | solution.py:796
  12.4 11.2 %collective-permute-start = (f32[5,32,256]{2,1,0:T(8,128)S(1)}, f32[5,32,256]{2,1,0:T(8,128)S(1)}, u32[]{:S(2)}, u32[]{:S(2)}) collective-permute-start(f32[5,32,256]{2,1,0:T(8,128)S(1)} %get-tuple-element.55), channel_id=1, source_target_pairs={{0,4},{4,0},{8,12},{12,8},{16,20},{20,16},{24,28},{28,24},{1,5},{5... | collective-permute-start | bytes 491528 | tf_op jit(solution)/shard_map/ppermute | solution.py:741
  14.4 11.6 %collective-permute-start.1 = (f32[5,32,256]{2,1,0:T(8,128)S(1)}, f32[5,32,256]{2,1,0:T(8,128)S(1)}, u32[]{:S(2)}, u32[]{:S(2)}) collective-permute-start(f32[5,32,256]{2,1,0:T(8,128)S(1)} %get-tuple-element.56), channel_id=1, source_target_pairs={{0,28},{4,8},{8,4},{12,16},{16,12},{20,24},{24,20},{28,0},{1,29},{... | collective-permute-start | bytes 491528 | tf_op jit(solution)/shard_map/ppermute | solution.py:740
  17.7 4.6 %collective-permute-start.2 = (f32[5,8,256]{2,1,0:T(8,128)S(1)}, f32[5,8,256]{2,1,0:T(8,128)S(1)}, u32[]{:S(2)}, u32[]{:S(2)}) collective-permute-start(f32[5,8,256]{2,1,0:T(8,128)S(1)} %get-tuple-element.57), channel_id=1, source_target_pairs={{0,1},{1,0},{2,3},{3,2},{4,5},{5,4},{6,7},{7,6},{8,9},{9,8},{10,11... | collective-permute-start | bytes 122888 | tf_op jit(solution)/shard_map/ppermute | solution.py:743
  17.7 4.6 %collective-permute-start.3 = (f32[5,8,256]{2,1,0:T(8,128)S(1)}, f32[5,8,256]{2,1,0:T(8,128)S(1)}, u32[]{:S(2)}, u32[]{:S(2)}) collective-permute-start(f32[5,8,256]{2,1,0:T(8,128)S(1)} %get-tuple-element.58), channel_id=1, source_target_pairs={{0,3},{1,2},{2,1},{3,0},{4,7},{5,6},{6,5},{7,4},{8,11},{9,10},{10,... | collective-permute-start | bytes 122888 | tf_op jit(solution)/shard_map/ppermute | solution.py:742
  32.7 12.6 %all-to-all-start.1 = ((f32[8,8,4,128]{3,2,1,0:T(4,128)}), f32[8,8,4,128]{3,2,1,0:T(4,128)S(1)}, u32[]{:S(2)}, u32[]{:S(2)}) async-start(f32[8,8,4,128]{3,2,1,0:T(4,128)} %get-tuple-element.71), calls=%async_computation.1 | async-start | bytes 262144 | tf_op jit(solution)/shard_map/all_to_all | solution.py:817
  38.4 10.3 %collective-permute-start.4 = (f32[3,32,256]{2,1,0:T(8,128)S(1)}, f32[3,32,256]{2,1,0:T(8,128)S(1)}, u32[]{:S(2)}, u32[]{:S(2)}) collective-permute-start(f32[3,32,256]{2,1,0:T(8,128)S(1)} %get-tuple-element.76), channel_id=1, source_target_pairs={{0,4},{4,0},{8,12},{12,8},{16,20},{20,16},{24,28},{28,24},{1,5},{5... | collective-permute-start | bytes 294920 | tf_op jit(solution)/shard_map/ppermute | solution.py:741
  40.4 8.2 %collective-permute-start.5 = (f32[3,32,256]{2,1,0:T(8,128)S(1)}, f32[3,32,256]{2,1,0:T(8,128)S(1)}, u32[]{:S(2)}, u32[]{:S(2)}) collective-permute-start(f32[3,32,256]{2,1,0:T(8,128)S(1)} %get-tuple-element.77), channel_id=1, source_target_pairs={{0,28},{4,8},{8,4},{12,16},{16,12},{20,24},{24,20},{28,0},{1,29},{... | collective-permute-start | bytes 294920 | tf_op jit(solution)/shard_map/ppermute | solution.py:740
  43.7 4.9 %collective-permute-start.6 = (f32[3,8,256]{2,1,0:T(8,128)S(1)}, f32[3,8,256]{2,1,0:T(8,128)S(1)}, u32[]{:S(2)}, u32[]{:S(2)}) collective-permute-start(f32[3,8,256]{2,1,0:T(8,128)S(1)} %get-tuple-element.78), channel_id=1, source_target_pairs={{0,1},{1,0},{2,3},{3,2},{4,5},{5,4},{6,7},{7,6},{8,9},{9,8},{10,11... | collective-permute-start | bytes 73736 | tf_op jit(solution)/shard_map/ppermute | solution.py:743
  43.7 4.9 %collective-permute-start.7 = (f32[3,8,256]{2,1,0:T(8,128)S(1)}, f32[3,8,256]{2,1,0:T(8,128)S(1)}, u32[]{:S(2)}, u32[]{:S(2)}) collective-permute-start(f32[3,8,256]{2,1,0:T(8,128)S(1)} %get-tuple-element.79), channel_id=1, source_target_pairs={{0,3},{1,2},{2,1},{3,0},{4,7},{5,6},{6,5},{7,4},{8,11},{9,10},{10,... | collective-permute-start | bytes 73736 | tf_op jit(solution)/shard_map/ppermute | solution.py:742
  49.5 11.1 %all-to-all-start.2 = ((f32[32,4,128]{2,1,0:T(4,128)}), f32[32,4,128]{2,1,0:T(4,128)S(1)}, u32[]{:S(2)}, u32[]{:S(2)}) async-start(f32[32,4,128]{2,1,0:T(4,128)} %get-tuple-element.91), calls=%async_computation.2 | async-start | bytes 131072 | tf_op jit(solution)/shard_map/all_to_all | solution.py:832

commit v8 on v7

--- a/solution.py
+++ b/solution.py
@@ -668,7 +668,7 @@
             acc_ref[at] = acc_ref[at] + part
         return carry
 
-    lax.fori_loop(0, bodies, device, 0)
+    lax.fori_loop(0, bodies, device, 0, unroll=4)
     inner = jnp.zeros((4, points), F32)
     for k in range(blocks):
         acc = acc_ref[k]

time: 62.3 us -> 62.3 us (level)
  no operation moved by 1% of the time
where the time goes in v8:
time: 62.3 us; the launch traced here: 61.9 us
  starting transfers between devices  28.5 us (46%)
  Pallas kernels  23.5 us (38%)
  waiting for transfers between devices  9.23 us (15%)
  between operations  0.76 us (1%)
    all_to_all x2, starting transfers between devices, on_device(): got = lax.all_to_all(message, 'body', 0, 0, tiled=True)  11 us
    ppermute x2, starting transfers between devices, exchange(): got_xo = lax.ppermute(xo, 'body', pairs('body', 1))  6.53 us
    pallas_call x1, Pallas kernels, on_device(): call(forces_one_kernel, 'forces_one', [VMEM] * 2 + [SMEM] + [VMEM] * 2, [...  5.6 us
    all_to_all x1, waiting for transfers between devices, on_device(): sums = lax.all_to_all(partial, ('body', 'across'), 0, 0, tiled=True)  5.5 us
    pallas_call x1, Pallas kernels, on_device(): call(open_kernel, 'open', [HBM] * 8, [VMEM] * 12 + [SMEM], (vector,) + ce...  4.47 us
    ppermute x2, starting transfers between devices, exchange(): got_xe = lax.ppermute(xe, 'body', pairs('body', 0))  4.1 us
    all_to_all x1, starting transfers between devices, on_device(): sums = lax.all_to_all(partial, ('body', 'across'), 0, 0, tiled=True)  3.64 us
    pallas_call x1, Pallas kernels, on_device(): call(apply_two_kernel, 'apply_two', [VMEM] * 5 + [SMEM] * 2 + [VMEM, HBM]...  3.3 us
  transfers between devices with their start and end apart: 11, of which 3 were waited for; matrix products, arithmetic and copies ran while one was open for 0% of the time, Pallas kernels for 18%

profile of v8, /device:TPU:0, one launch (start us, length us, event | category | flops | bytes accessed | tf_op | source)
XLA Modules:
  0.0 61.9 jit_solution(14094172279487709836)
XLA Ops:
  0.6 4.5 %open.1 = (f32[3,8,32,256]{3,2,1,0:T(8,128)S(1)}, f32[8,32,256]{2,1,0:T(8,128)S(1)}, f32[8,32,256]{2,1,0:T(8,128)S(1)}, f32[8,32,256]{2,1,0:T(8,128)S(1)}, s32[8...) custom-call(f32[3,8,32,256]{3,2,1,0:T(8,128)} %r_hbm.3, ...), custom_call_target="tpu_custom_call" | custom-call | flops 400000000 | bytes 12000000 | tf_op jit(solution)/shard_map/open/pallas_call | solution.py:785
  5.1 7.3 %all-to-all-start = ((f32[8,38,2,128]{3,2,1,0:T(2,128)}), f32[8,38,2,128]{3,2,1,0:T(2,128)S(1)}, u32[]{:S(2)}, u32[]{:S(2)}) async-start(f32[8,38,2,128]{3,2,1,0:T(2,128)} %get-tuple-element.61), calls=%async_computation | async-start | bytes 622592 | tf_op jit(solution)/shard_map/all_to_all | solution.py:796
  12.4 2.0 %collective-permute-start = (f32[5,32,256]{2,1,0:T(8,128)S(1)}, f32[5,32,256]{2,1,0:T(8,128)S(1)}, u32[]{:S(2)}, u32[]{:S(2)}) collective-permute-start(f32[5,32,256]{2,1,0:T(8,128)S(1)} %get-tuple-element.55), channel_id=1, source_target_pairs={{0,4},{4,0},{8,12},{12,8},{16,20},{20,16},{24,28},{28,24},{1,5},{5... | collective-permute-start | bytes 491528 | tf_op jit(solution)/shard_map/ppermute | solution.py:741
  14.4 3.3 %collective-permute-start.1 = (f32[5,32,256]{2,1,0:T(8,128)S(1)}, f32[5,32,256]{2,1,0:T(8,128)S(1)}, u32[]{:S(2)}, u32[]{:S(2)}) collective-permute-start(f32[5,32,256]{2,1,0:T(8,128)S(1)} %get-tuple-element.56), channel_id=1, source_target_pairs={{0,28},{4,8},{8,4},{12,16},{16,12},{20,24},{24,20},{28,0},{1,29},{... | collective-permute-start | bytes 491528 | tf_op jit(solution)/shard_map/ppermute | solution.py:740
  17.7 1.6 %collective-permute-start.3 = (f32[5,8,256]{2,1,0:T(8,128)S(1)}, f32[5,8,256]{2,1,0:T(8,128)S(1)}, u32[]{:S(2)}, u32[]{:S(2)}) collective-permute-start(f32[5,8,256]{2,1,0:T(8,128)S(1)} %get-tuple-element.58), channel_id=1, source_target_pairs={{0,3},{1,2},{2,1},{3,0},{4,7},{5,6},{6,5},{7,4},{8,11},{9,10},{10,... | collective-permute-start | bytes 122888 | tf_op jit(solution)/shard_map/ppermute | solution.py:742
  19.3 2.9 %stencil_one.1 = (f32[8,32,256]{2,1,0:T(8,128)S(1)}, f32[8,32,256]{2,1,0:T(8,128)S(1)}, f32[8,32,256]{2,1,0:T(8,128)S(1)}, f32[17,4,128]{2,1,0:T(4,128)S(1)}) custom-call(f32[3,8,32,256]{3,2,1,0:T(8,128)S(1)} %get-tuple-element.47.r_ref, f32[8,32,256]{2,1,0:T(8,128)S(1)} %get-tuple-element.48.sh_ref, f32[8,32,256]{2,1,0:T(8,128)S(1)} %get-tuple-element.49.la_ref, ...), custom_call_target="tpu_custom_call" | custom-call | flops 500000000 | bytes 15000000 | tf_op jit(solution)/shard_map/stencil_one/pallas_call | solution.py:799
  22.3 0.0 collective-permute-done.2.ye
  22.3 1.4 %collective-permute-done.xe = f32[5,32,256]{2,1,0:T(8,128)S(1)} collective-permute-done((f32[5,32,256]{2,1,0:T(8,128)S(1)}, f32[5,32,256]{2,1,0:T(8,128)S(1)}, u32[]{:S(2)}, u32[]{:S(2)}) %collective-permute-start) | collective-permute-done | bytes 163872 | tf_op jit(solution)/shard_map/ppermute | solution.py:741
  23.7 2.3 %collective-permute-done.1.xo = f32[5,32,256]{2,1,0:T(8,128)S(1)} collective-permute-done((f32[5,32,256]{2,1,0:T(8,128)S(1)}, f32[5,32,256]{2,1,0:T(8,128)S(1)}, u32[]{:S(2)}, u32[]{:S(2)}) %collective-permute-start.1) | collective-permute-done | bytes 163872 | tf_op jit(solution)/shard_map/ppermute | solution.py:740
  26.0 1.1 %faces_one.1 = (f32[3,80,256]{2,1,0:T(8,128)S(1)}, f32[17,4,128]{2,1,0:T(4,128)S(1)}, f32[2,32,256]{2,1,0:T(8,128)S(1)}, f32[2,32,256]{2,1,0:T(8,128)S(1)}, f32[...) custom-call(f32[3,8,32,256]{3,2,1,0:T(8,128)S(1)} %get-tuple-element.47.r_ref, ...), custom_call_target="tpu_custom_call" | custom-call | flops 100000000 | bytes 3000000 | tf_op jit(solution)/shard_map/faces_one/pallas_call | solution.py:804
  27.1 5.6 %forces_one.1 = (f32[16,4,128]{2,1,0:T(4,128)S(1)}, f32[17,4,128]{2,1,0:T(4,128)S(1)}, f32[8,8,4,128]{3,2,1,0:T(4,128)}, s32[32]{0:T(128)S(1)}, bf16[8,8,128,256]{3,2,1,0:T(8,128)(2,1)}) custom-call(f32[8,38,2,128]{3,2,1,0:T(2,128)S(1)} %all-to-all-done.got_ref, f32[16,4,128]{2,1,0:T(4,128)S(1)} %get-tuple-element.62.own_ref, ...), custom_call_target="tpu_custom_call" | custom-call | flops 600000000 | bytes 18000000 | tf_op jit(solution)/shard_map/forces_one/pallas_call | solution.py:809
  32.7 3.7 %all-to-all-start.1 = ((f32[8,8,4,128]{3,2,1,0:T(4,128)}), f32[8,8,4,128]{3,2,1,0:T(4,128)S(1)}, u32[]{:S(2)}, u32[]{:S(2)}) async-start(f32[8,8,4,128]{3,2,1,0:T(4,128)} %get-tuple-element.71), calls=%async_computation.1 | async-start | bytes 262144 | tf_op jit(solution)/shard_map/all_to_all | solution.py:817
  36.4 2.0 %scatter_one.1 = (f32[3,8,32,256]{3,2,1,0:T(8,128)S(1)}, f32[3,32,256]{2,1,0:T(8,128)S(1)}, f32[3,32,256]{2,1,0:T(8,128)S(1)}, f32[3,8,256]{2,1,0:T(8,128)S(1)},...) custom-call(f32[8,32,256]{2,1,0:T(8,128)S(1)} %get-tuple-element.52., ...), custom_call_target="tpu_custom_call" | custom-call | flops 300000000 | bytes 9000000 | tf_op jit(solution)/shard_map/scatter_one/pallas_call | solution.py:818
  38.4 2.1 %collective-permute-start.4 = (f32[3,32,256]{2,1,0:T(8,128)S(1)}, f32[3,32,256]{2,1,0:T(8,128)S(1)}, u32[]{:S(2)}, u32[]{:S(2)}) collective-permute-start(f32[3,32,256]{2,1,0:T(8,128)S(1)} %get-tuple-element.76), channel_id=1, source_target_pairs={{0,4},{4,0},{8,12},{12,8},{16,20},{20,16},{24,28},{28,24},{1,5},{5... | collective-permute-start | bytes 294920 | tf_op jit(solution)/shard_map/ppermute | solution.py:741
  40.4 3.3 %collective-permute-start.5 = (f32[3,32,256]{2,1,0:T(8,128)S(1)}, f32[3,32,256]{2,1,0:T(8,128)S(1)}, u32[]{:S(2)}, u32[]{:S(2)}) collective-permute-start(f32[3,32,256]{2,1,0:T(8,128)S(1)} %get-tuple-element.77), channel_id=1, source_target_pairs={{0,28},{4,8},{8,4},{12,16},{16,12},{20,24},{24,20},{28,0},{1,29},{... | collective-permute-start | bytes 294920 | tf_op jit(solution)/shard_map/ppermute | solution.py:740
  43.7 0.0 collective-permute-start.6
  43.7 1.6 %collective-permute-start.7 = (f32[3,8,256]{2,1,0:T(8,128)S(1)}, f32[3,8,256]{2,1,0:T(8,128)S(1)}, u32[]{:S(2)}, u32[]{:S(2)}) collective-permute-start(f32[3,8,256]{2,1,0:T(8,128)S(1)} %get-tuple-element.79), channel_id=1, source_target_pairs={{0,3},{1,2},{2,1},{3,0},{4,7},{5,6},{6,5},{7,4},{8,11},{9,10},{10,... | collective-permute-start | bytes 73736 | tf_op jit(solution)/shard_map/ppermute | solution.py:742
  45.3 3.3 %apply_two.1 = (f32[3,8,32,256]{3,2,1,0:T(8,128)S(1)}, f32[16,4,128]{2,1,0:T(4,128)S(1)}, f32[4,128]{1,0:T(4,128)S(1)}) custom-call(f32[3,8,32,256]{3,2,1,0:T(8,128)S(1)} %get-tuple-element.67.w1_ref, f32[8,32,256]{2,1,0:T(8,128)S(1)} %get-tuple-element.68.sh_ref, f32[8,32,256]{2,1,0:T(8,128)S(1)} %get-tuple-element.69.la_ref, ...), custom_call_target="tpu_custom_call" | custom-call | flops 300000000 | bytes 9000000 | tf_op jit(solution)/shard_map/apply_two/pallas_call | solution.py:823
  48.6 0.0 collective-permute-done.6.ye
  48.7 0.8 %faces_two.1 = (f32[3,80,256]{2,1,0:T(8,128)S(1)}, f32[32,4,128]{2,1,0:T(4,128)}) custom-call(f32[3,8,32,256]{3,2,1,0:T(8,128)S(1)} %get-tuple-element.67.w1_ref, f32[8,32,256]{2,1,0:T(8,128)S(1)} %get-tuple-element.68.sh_ref, f32[8,32,256]{2,1,0:T(8,128)S(1)} %get-tuple-element.69.la_ref, f32[3,32,256]{2,1,0:T(8,128)S(1)} %collective-permute-done.4.xe, ...), custom_call_target="tpu_custom_call" | custom-call | flops 100000000 | bytes 3000000 | tf_op jit(solution)/shard_map/faces_two/pallas_call | solution.py:828
  49.5 3.6 %all-to-all-start.2 = ((f32[32,4,128]{2,1,0:T(4,128)}), f32[32,4,128]{2,1,0:T(4,128)S(1)}, u32[]{:S(2)}, u32[]{:S(2)}) async-start(f32[32,4,128]{2,1,0:T(4,128)} %get-tuple-element.91), calls=%async_computation.2 | async-start | bytes 131072 | tf_op jit(solution)/shard_map/all_to_all | solution.py:832
  53.2 1.9 %scatter_two.1 = (f32[3,8,32,256]{3,2,1,0:T(8,128)S(1)}, f32[8,32,256]{2,1,0:T(8,128)S(1)}, f32[8,32,256]{2,1,0:T(8,128)S(1)}, f32[8,32,256]{2,1,0:T(8,128)S(1)}) custom-call(f32[3,8,32,256]{3,2,1,0:T(8,128)S(1)} %get-tuple-element.75.e_ref, f32[3,80,256]{2,1,0:T(8,128)S(1)} %get-tuple-element.85.face_ref, f32[16,4,128]{2,1,0:T(4,128)S(1)} %get-tuple-element.86.force_ref, ...), custom_call_target="tpu_custom_call" | custom-call | flops 300000000 | bytes 9000000 | tf_op jit(solution)/shard_map/scatter_two/pallas_call | solution.py:833
  55.1 5.5 %all-to-all-done.2.red_ref = f32[32,4,128]{2,1,0:T(4,128)S(1)} async-done(((f32[32,4,128]{2,1,0:T(4,128)}), f32[32,4,128]{2,1,0:T(4,128)S(1)}, u32[]{:S(2)}, u32[]{:S(2)}) %all-to-all-start.2) | async-done | bytes 65568 | tf_op jit(solution)/shard_map/all_to_all | solution.py:832
  60.6 1.4 %final.1 = (f32[3,8,32,256]{3,2,1,0:T(8,128)}, f32[3,8,32,256]{3,2,1,0:T(8,128)}) custom-call(f32[8,32,256]{2,1,0:T(8,128)S(1)} %get-tuple-element.87.r0_ref, f32[8,32,256]{2,1,0:T(8,128)S(1)} %get-tuple-element.88.r1_ref, f32[8,32,256]{2,1,0:T(8,128)S(1)} %get-tuple-element.89.r2_ref, f32[3,8,32,256]{3,2,1,0:T(8,128)S(1)} %get-tuple-element.67.w1_ref, ...), custom_call_target="tpu_custom_call" | custom-call | flops 100000000 | bytes 3000000 | tf_op jit(solution)/shard_map/final/pallas_call | solution.py:838
  (7 shorter events, 0.0 us)
Async XLA Ops:
  5.1 22.0 %all-to-all-start = ((f32[8,38,2,128]{3,2,1,0:T(2,128)}), f32[8,38,2,128]{3,2,1,0:T(2,128)S(1)}, u32[]{:S(2)}, u32[]{:S(2)}) async-start(f32[8,38,2,128]{3,2,1,0:T(2,128)} %get-tuple-element.61), calls=%async_computation | async-start | bytes 622592 | tf_op jit(solution)/shard_map/all_to_all | solution.py:796
  12.4 11.2 %collective-permute-start = (f32[5,32,256]{2,1,0:T(8,128)S(1)}, f32[5,32,256]{2,1,0:T(8,128)S(1)}, u32[]{:S(2)}, u32[]{:S(2)}) collective-permute-start(f32[5,32,256]{2,1,0:T(8,128)S(1)} %get-tuple-element.55), channel_id=1, source_target_pairs={{0,4},{4,0},{8,12},{12,8},{16,20},{20,16},{24,28},{28,24},{1,5},{5... | collective-permute-start | bytes 491528 | tf_op jit(solution)/shard_map/ppermute | solution.py:741
  14.4 11.6 %collective-permute-start.1 = (f32[5,32,256]{2,1,0:T(8,128)S(1)}, f32[5,32,256]{2,1,0:T(8,128)S(1)}, u32[]{:S(2)}, u32[]{:S(2)}) collective-permute-start(f32[5,32,256]{2,1,0:T(8,128)S(1)} %get-tuple-element.56), channel_id=1, source_target_pairs={{0,28},{4,8},{8,4},{12,16},{16,12},{20,24},{24,20},{28,0},{1,29},{... | collective-permute-start | bytes 491528 | tf_op jit(solution)/shard_map/ppermute | solution.py:740
  17.7 4.6 %collective-permute-start.2 = (f32[5,8,256]{2,1,0:T(8,128)S(1)}, f32[5,8,256]{2,1,0:T(8,128)S(1)}, u32[]{:S(2)}, u32[]{:S(2)}) collective-permute-start(f32[5,8,256]{2,1,0:T(8,128)S(1)} %get-tuple-element.57), channel_id=1, source_target_pairs={{0,1},{1,0},{2,3},{3,2},{4,5},{5,4},{6,7},{7,6},{8,9},{9,8},{10,11... | collective-permute-start | bytes 122888 | tf_op jit(solution)/shard_map/ppermute | solution.py:743
  17.7 4.6 %collective-permute-start.3 = (f32[5,8,256]{2,1,0:T(8,128)S(1)}, f32[5,8,256]{2,1,0:T(8,128)S(1)}, u32[]{:S(2)}, u32[]{:S(2)}) collective-permute-start(f32[5,8,256]{2,1,0:T(8,128)S(1)} %get-tuple-element.58), channel_id=1, source_target_pairs={{0,3},{1,2},{2,1},{3,0},{4,7},{5,6},{6,5},{7,4},{8,11},{9,10},{10,... | collective-permute-start | bytes 122888 | tf_op jit(solution)/shard_map/ppermute | solution.py:742
  32.7 12.6 %all-to-all-start.1 = ((f32[8,8,4,128]{3,2,1,0:T(4,128)}), f32[8,8,4,128]{3,2,1,0:T(4,128)S(1)}, u32[]{:S(2)}, u32[]{:S(2)}) async-start(f32[8,8,4,128]{3,2,1,0:T(4,128)} %get-tuple-element.71), calls=%async_computation.1 | async-start | bytes 262144 | tf_op jit(solution)/shard_map/all_to_all | solution.py:817
  38.4 10.3 %collective-permute-start.4 = (f32[3,32,256]{2,1,0:T(8,128)S(1)}, f32[3,32,256]{2,1,0:T(8,128)S(1)}, u32[]{:S(2)}, u32[]{:S(2)}) collective-permute-start(f32[3,32,256]{2,1,0:T(8,128)S(1)} %get-tuple-element.76), channel_id=1, source_target_pairs={{0,4},{4,0},{8,12},{12,8},{16,20},{20,16},{24,28},{28,24},{1,5},{5... | collective-permute-start | bytes 294920 | tf_op jit(solution)/shard_map/ppermute | solution.py:741
  40.4 8.2 %collective-permute-start.5 = (f32[3,32,256]{2,1,0:T(8,128)S(1)}, f32[3,32,256]{2,1,0:T(8,128)S(1)}, u32[]{:S(2)}, u32[]{:S(2)}) collective-permute-start(f32[3,32,256]{2,1,0:T(8,128)S(1)} %get-tuple-element.77), channel_id=1, source_target_pairs={{0,28},{4,8},{8,4},{12,16},{16,12},{20,24},{24,20},{28,0},{1,29},{... | collective-permute-start | bytes 294920 | tf_op jit(solution)/shard_map/ppermute | solution.py:740
  43.7 4.9 %collective-permute-start.6 = (f32[3,8,256]{2,1,0:T(8,128)S(1)}, f32[3,8,256]{2,1,0:T(8,128)S(1)}, u32[]{:S(2)}, u32[]{:S(2)}) collective-permute-start(f32[3,8,256]{2,1,0:T(8,128)S(1)} %get-tuple-element.78), channel_id=1, source_target_pairs={{0,1},{1,0},{2,3},{3,2},{4,5},{5,4},{6,7},{7,6},{8,9},{9,8},{10,11... | collective-permute-start | bytes 73736 | tf_op jit(solution)/shard_map/ppermute | solution.py:743
  43.7 4.9 %collective-permute-start.7 = (f32[3,8,256]{2,1,0:T(8,128)S(1)}, f32[3,8,256]{2,1,0:T(8,128)S(1)}, u32[]{:S(2)}, u32[]{:S(2)}) collective-permute-start(f32[3,8,256]{2,1,0:T(8,128)S(1)} %get-tuple-element.79), channel_id=1, source_target_pairs={{0,3},{1,2},{2,1},{3,0},{4,7},{5,6},{6,5},{7,4},{8,11},{9,10},{10,... | collective-permute-start | bytes 73736 | tf_op jit(solution)/shard_map/ppermute | solution.py:742
  49.5 11.1 %all-to-all-start.2 = ((f32[32,4,128]{2,1,0:T(4,128)}), f32[32,4,128]{2,1,0:T(4,128)S(1)}, u32[]{:S(2)}, u32[]{:S(2)}) async-start(f32[32,4,128]{2,1,0:T(4,128)} %get-tuple-element.91), calls=%async_computation.2 | async-start | bytes 131072 | tf_op jit(solution)/shard_map/all_to_all | solution.py:832
